TPU v7x, 32 devices: a whole 2x2x4 slice. The times are simulated.
32 devices in a mesh: frames: 8 (over z, y), rows: 4 (over x, core).
Axes of the slice: x: 2, y: 2, z: 4, core: 2. Of those that a mesh axis runs over, the one named last changes fastest.
Arguments:
- features: bfloat16 [8, 64, 128, 128], P('frames', 'rows'), may hold values from -6 to 6
- pair_weight: bfloat16 [8, 64, 4, 128, 128], P('frames', 'rows'), may hold values from -0.5 to 0.5
- target_tile: int32 [8, 64, 4], P('frames', 'rows'), may hold values from 0 to 31, all different within a row; in each aligned block of 16 rows (0 to 15, 16 to 31, ..., all dimensions but the last counted through in order) at most 4 rows name the same one
- target_block: int32 [8, 64, 4], P('frames', 'rows'), may hold values from 0 to 15
- conv1_weight: bfloat16 [3, 3, 3, 128, 128], replicated, may hold values from -0.109375 to 0.109375
- conv1_bias: float32 [128], replicated, may hold values from -3 to 3
- conv2_weight: bfloat16 [3, 3, 3, 128, 128], replicated, may hold values from -0.109375 to 0.109375
- conv2_bias: float32 [128], replicated, may hold values from -3 to 3
Outputs:
- occupancy: bfloat16 [64, 256, 4, 128], P('frames', 'rows')
Inputs may be any that keep to these rules, and one draw needn't show every extreme that they name: `target_tile`: each image block names 4 different tiles; among the pairs of one device no tile is named more than 4 times, a bound that some block reaches.
All inputs are finite; a program needn't handle non-finite values.
Results may differ from a plain program's by a relative error of at most 0.0055.
Values may be sent and summed in bfloat16 or wider, within the bound.
No kernel may reach another device: no remote copies, remote signals or barrier semaphores. Data moves between devices by JAX's collectives and lax.ppermute only.
A program may use at most 128 MiB of HBM per device.

v0:
```python
import functools

import jax
import jax.numpy as jnp
from jax import lax
from jax.experimental import pallas as pl
from jax.experimental.pallas import tpu as pltpu
from jax.sharding import PartitionSpec as P


DEPTH = 4
TX = 8
TY = 64
CORES = 2
ORDER = (0, 3, 1, 2)
LABEL_ROWS = 16
VMEM = pltpu.VMEM
LIMIT = 12 * 1024 * 1024


def vmem():
    return pl.BlockSpec(memory_space=pltpu.VMEM)


def smem():
    return pl.BlockSpec(memory_space=pltpu.SMEM)


def anywhere():
    return pl.BlockSpec(memory_space=pl.ANY)


def params():
    return pltpu.CompilerParams(vmem_limit_bytes=LIMIT)


def arrays(count, rows, channels, dtype=jnp.bfloat16):
    return [jax.ShapeDtypeStruct((rows, channels), dtype)] * count


def split_low(value, count):
    if count & (count - 1) == 0:
        return value >> (count.bit_length() - 1), value & (count - 1)
    return value // count, value % count


def apart(target, source, count):
    if count & (count - 1) == 0:
        return target ^ source
    return (target - source + count) % count


def step_to(source, step, count):
    if count & (count - 1) == 0:
        return source ^ step
    return (source + step) % count


def index_kernel(shape, slots, blocks, *refs):
    n_z, n_y, n_x, n_c = shape
    codes = refs[:n_c]
    weight_ref, feature_ref, index_ref, label_ref, weight_out, feature_out, counts, labels, sems = refs[n_c:]
    copies = [
        pltpu.make_async_copy(feature_ref, feature_out, sems.at[0]),
        pltpu.make_async_copy(weight_ref, weight_out, sems.at[1]),
    ]
    for copy in copies:
        copy.start()
    tiles = n_z * n_y * n_x * n_c
    groups = n_y * n_x
    spare = groups * n_z * slots

    def clear(t, carry):
        counts[t] = 0
        return carry

    lax.fori_loop(0, tiles, clear, 0, unroll=8)

    def blank(s, carry):
        labels[s] = -1
        return carry

    lax.fori_loop(0, spare, blank, 0, unroll=8)
    z, y = split_low(lax.axis_index("frames"), n_y)
    x, c = split_low(lax.axis_index("rows"), n_c)
    pairs = codes[0].shape[0]
    for source in range(n_c):
        ref = codes[source]

        def place(p, carry):
            tile, block = split_low(ref[p], blocks)
            rank = counts[tile]
            counts[tile] = rank + 1
            rest, c_to = split_low(tile, n_c)
            rest, x_to = split_low(rest, n_x)
            z_to, y_to = split_low(rest, n_y)
            group = apart(y_to, y, n_y) * n_x + apart(x_to, x, n_x)
            slot = (group * n_z + apart(z_to, z, n_z)) * slots + rank
            slot = jnp.where(c_to == c, slot, spare)
            index_ref[source * pairs + p] = slot
            labels[slot] = block
            return carry

        lax.fori_loop(0, pairs, place, 0, unroll=4)
    lane = lax.broadcasted_iota(jnp.int32, (LABEL_ROWS, label_ref.shape[1]), 1)
    for g in range(groups):
        row = jnp.full(lane.shape, -1, jnp.int32)
        for k in range(n_z * slots):
            row = jnp.where(lane == k, labels[g * n_z * slots + k], row)
        label_ref[g * LABEL_ROWS : (g + 1) * LABEL_ROWS, :] = row.astype(jnp.float32).astype(jnp.bfloat16)
    for copy in copies:
        copy.wait()


def contribute_kernel(n_c, groups, per_group, top, spans, first, *refs):
    index_ref = refs[0]
    sources = refs[1 : 1 + n_c]
    features = refs[1 + n_c : 1 + 2 * n_c]
    refs = refs[1 + 2 * n_c :]
    label_ref = refs[0]
    outs = refs[1 : 1 + groups * len(spans)]
    refs = refs[1 + groups * len(spans) :]
    buffers = refs[: len(spans)]
    held, load_sems, store_sems = refs[len(spans) :]
    images = features[0].shape[0]
    begin, rows = min(span[0] for span in spans), sum(span[1] for span in spans)
    loads = [
        pltpu.make_async_copy(
            sources[s].at[:, pl.ds(begin, rows), :], held.at[pl.ds(s * images * top, images * top)], load_sems.at[s]
        )
        for s in range(n_c)
    ]
    for load in loads:
        load.start()
    for s in range(n_c):
        loads[s].wait()

        def image(b, carry):
            p0 = s * images * top + b * top
            weights = held[pl.ds(p0, top)].reshape(top * rows, held.shape[2])
            product = jnp.dot(weights, features[s][b], preferred_element_type=jnp.float32)
            product = product.astype(jnp.bfloat16)
            for t in range(top):
                slot = index_ref[p0 + t]
                for (start, chunk), buffer in zip(spans, buffers):
                    at = t * rows + start - begin
                    buffer[pl.ds(pl.multiple_of(slot * chunk, chunk), chunk), :] = product[at : at + chunk]
            return carry

        lax.fori_loop(0, images, image, 0, unroll=4)
    copies = []
    for i, ((_, chunk), buffer) in enumerate(zip(spans, buffers)):
        length = per_group * chunk
        for g in range(groups):
            n = i * groups + g
            data = outs[n].at[pl.ds(0, length)] if first else outs[n]
            copies.append(pltpu.make_async_copy(buffer.at[pl.ds(g * length, length)], data, store_sems.at[n]))
            if first:
                copies.append(
                    pltpu.make_async_copy(
                        label_ref.at[pl.ds(g * LABEL_ROWS, LABEL_ROWS)],
                        outs[n].at[pl.ds(length, LABEL_ROWS)],
                        store_sems.at[groups * len(spans) + g],
                    )
                )
    for copy in copies:
        copy.start()
    for copy in copies:
        copy.wait()


def merge_kernel(n_z, groups, slots, chunk, blocks, first, *refs):
    messages = refs[:groups]
    refs = refs[groups:]
    per_group = n_z * slots
    stride = per_group + 1
    if first:
        outs = refs[:n_z]
        plan_ref, total, marks, marks_smem, sem = refs[n_z:]
        for g in range(groups):
            row = messages[g][per_group * chunk :, :].astype(jnp.float32)
            marks[g : g + 1, :] = row[0:1, :].astype(jnp.int32)
        copy = pltpu.make_async_copy(marks, marks_smem, sem)
        copy.start()
    else:
        plan_ref = refs[0]
        outs = refs[1 : 1 + n_z]
        (total,) = refs[1 + n_z :]
    total[...] = jnp.zeros_like(total)
    if first:
        copy.wait()
        for g in range(groups):

            def note(s, count):
                label = marks_smem[g, s]
                plan_ref[g * stride + 1 + count] = s * blocks + jnp.maximum(label, 0)
                return count + (label >= 0).astype(jnp.int32)

            plan_ref[g * stride] = lax.fori_loop(0, per_group, note, 0, unroll=8)
    for g in range(groups):

        def add(n, carry):
            slot, label = split_low(plan_ref[g * stride + 1 + n], blocks)
            step = split_low(slot, slots)[0]
            source = pl.ds(pl.multiple_of(slot * chunk, chunk), chunk)
            target = pl.ds(pl.multiple_of((step * blocks + label) * chunk, chunk), chunk)
            total[target, :] += messages[g][source, :].astype(jnp.float32)
            return carry

        lax.fori_loop(0, plan_ref[g * stride], add, 0)
    rows = blocks * chunk
    for step, out in enumerate(outs):
        out[...] = total[step * rows : (step + 1) * rows, :].astype(jnp.bfloat16)


def sum_parts(parts, block, chunk):
    value = None
    for ref in parts:
        part = ref[block * chunk : (block + 1) * chunk, :].astype(jnp.float32)
        value = part if value is None else value + part
    return value


def tail_kernel(n_z, blocks, halves, *refs):
    parts = refs[: 2 * n_z]
    left_ref, right_ref, columns = refs[2 * n_z + 1 :]
    chunk = parts[0].shape[0] // blocks
    width = 2 * DEPTH
    channels = columns.shape[2]
    for x in range(blocks // halves):
        value = sum_parts(parts[:n_z], x * halves, chunk)
        columns[0, x * width : (x + 1) * width, :] = value[:width]
        value = sum_parts(parts[n_z:], x * halves + halves - 1, chunk)
        columns[1, x * width : (x + 1) * width, :] = value[chunk - width :]
    cells = columns.shape[1] // DEPTH
    for side, ref in enumerate((left_ref, right_ref)):
        for z in range(DEPTH):
            part = columns[side, pl.ds(z, cells, stride=DEPTH), :].astype(jnp.bfloat16)
            ref[:, z * channels : (z + 1) * channels] = part


def finish_kernel(n_z, spans, blocks, size, *refs):
    count = n_z * len(spans)
    parts = refs[:count]
    left_ref, right_ref, _, out_ref, first_ref, last_ref, total = refs[count:]
    for k, (start, chunk) in enumerate(spans):
        for block in range(blocks):
            at = block * size + start
            total[at : at + chunk, :] = sum_parts(parts[k * n_z : (k + 1) * n_z], block, chunk)
    cells = total.shape[0] // DEPTH
    channels = total.shape[1]
    for z in range(DEPTH):
        part = total[pl.ds(z, cells, stride=DEPTH), :].astype(jnp.bfloat16)
        lanes = slice(z * channels, (z + 1) * channels)
        out_ref[:, lanes] = part
        for x in range(2):
            first_ref[x, 0:TY, lanes] = part[x * TY : (x + 1) * TY]
            last_ref[x, 0:TY, lanes] = part[cells - (2 - x) * TY : cells - (1 - x) * TY]
    rows = cells // TY
    for x in range(2):
        for ref, at in ((first_ref, x), (last_ref, rows - 2 + x)):
            ref[x, TY : TY + 2, :] = left_ref[2 * at : 2 * at + 2, :]
            ref[x, TY + 2 : TY + 4, :] = right_ref[2 * at : 2 * at + 2, :]


def band_kernel(first_ref, second_ref, after_ref, out1_ref, out2_ref):
    channels = first_ref.shape[-1]
    zero = jnp.zeros((channels, channels), jnp.bfloat16)
    for source, target in ((first_ref, out1_ref), (second_ref, out2_ref)):
        for dx in range(3):
            for half in range(2):
                for dy in range(3):
                    for k in range(3):
                        z_in = k + half
                        for j in range(2):
                            dz = z_in - (2 * half + j) + 1
                            value = source[dx, dy, dz] if 0 <= dz < 3 else zero
                            row = (dy * 3 + k) * channels
                            target[dx, half, row : row + channels, j * channels : (j + 1) * channels] = value


def silu(v):
    return v / (1.0 + jnp.exp(-v))


def convolve_half(copies, bands, half, slabs, out_rows, channels):
    total = None
    for dx in range(3):
        pieces = []
        for dy in range(3):
            lanes = slice(half * channels, (half + 3) * channels)
            height = copies[dy].shape[0] // slabs
            parts = [copies[dy][s * height + dx : s * height + dx + out_rows, :, lanes] for s in range(slabs)]
            piece = parts[0] if slabs == 1 else jnp.concatenate(parts, axis=0)
            pieces.append(piece.reshape(-1, 3 * channels))
        product = jnp.dot(
            jnp.concatenate(pieces, axis=1), bands[dx, half], preferred_element_type=jnp.float32
        )
        total = product if total is None else total + product
    return total


def volume_ends():
    ends = []
    for axis in ("frames", "rows"):
        at = lax.axis_index(axis)
        ends += [(at == 0).astype(jnp.int32), (at == lax.axis_size(axis) - 1).astype(jnp.int32)]
    return ends


def first_layer(copies, band_ref, bias_ref, slabs, out_rows, cols, put):
    ends = volume_ends()
    channels = bias_ref.shape[1]
    bias = jnp.concatenate([bias_ref[...], bias_ref[...]], axis=1)
    for half in range(2):
        total = convolve_half(copies, band_ref, half, slabs, out_rows, channels)
        value = silu(total + bias).reshape(slabs * out_rows, -1, 2 * channels)
        y_at = lax.broadcasted_iota(jnp.int32, value.shape, 1)
        keep = (y_at >= ends[2]) & (y_at < cols + 2 - ends[3])
        if slabs > 1:
            x_at = lax.broadcasted_iota(jnp.int32, value.shape, 0)
            keep = keep & (x_at >= ends[0]) & (x_at < slabs * out_rows - ends[1])
        value = jnp.where(keep, value, 0.0).astype(jnp.bfloat16)
        put(half, value)


def second_layer(copies, band_ref, bias_ref, slabs, out_rows, stage):
    channels = bias_ref.shape[1]
    cells = stage.shape[0] // DEPTH
    for half in range(2):
        total = convolve_half(copies, band_ref, half, slabs, out_rows, channels)
        for j in range(2):
            value = silu(total[:, j * channels : (j + 1) * channels] + bias_ref[...])
            stage[pl.ds(2 * half + j, cells, stride=DEPTH), :] = value


def fill(copies, x0, value, left, right):
    cols = value.shape[1]
    part = slice(x0, x0 + value.shape[0])
    copies[0][part, 2 : 2 + cols, :] = value
    copies[1][part, 1 : 1 + cols, :] = value
    copies[2][part, 0:cols, :] = value
    for i in range(value.shape[0]):
        x, j = x0 + i, 2 * i
        copies[0][x, 0:2, :] = left[j : j + 2]
        copies[1][x, 0:1, :] = left[j + 1 : j + 2]
        copies[1][x, 1 + cols : 2 + cols, :] = right[j : j + 1]
        copies[2][x, cols : 2 + cols, :] = right[j : j + 2]


def interior_kernel(
    main_ref, left_ref, right_ref, band1_ref, band2_ref, bias1_ref, bias2_ref, out_ref, kept_ref,
    copies0, copies1, copies2, hidden, shift1, shift2, stage,
):
    rows, cols = main_ref.shape[0], main_ref.shape[1]
    channels = bias1_ref.shape[1]
    copies = (copies0, copies1, copies2)
    fill(copies, 0, main_ref[...], left_ref[...], right_ref[...])
    inner = rows - 2

    def put(half, value):
        lanes = slice(half * 2 * channels, (half + 1) * 2 * channels)
        hidden[:, :, lanes] = value
        kept_ref[0:2, :, lanes] = value[0:2]
        kept_ref[2:4, :, lanes] = value[inner - 2 :]

    first_layer(copies, band1_ref, bias1_ref, 1, inner, cols, put)
    shift1[...] = hidden[:, 1 : 1 + cols, :]
    shift2[...] = hidden[:, 2 : 2 + cols, :]
    second_layer((hidden.at[:, 0:cols, :], shift1, shift2), band2_ref, bias2_ref, 1, rows - 4, stage)
    out_ref[...] = stage[...].astype(jnp.bfloat16)


def border_kernel(
    main_ref, low_ref, high_ref, left_ref, right_ref,
    band1_ref, band2_ref, bias1_ref, bias2_ref, inner_ref, kept_ref, out_ref,
    copies0, copies1, copies2, hidden, shift1, shift2, stage,
):
    channels = bias1_ref.shape[1]
    rows, cols = main_ref.shape[0], main_ref.shape[1]
    copies = (copies0, copies1, copies2)
    left, right = left_ref[...], right_ref[...]
    for x0, ref in ((0, low_ref), (6, high_ref)):
        for x in range(2):
            corner = ref[x, cols : cols + 4, :]
            fill(copies, x0 + x, ref[x : x + 1, 0:cols, :], corner[0:2], corner[2:4])
    fill(copies, 2, main_ref[0:2], left[0:4], right[0:4])
    fill(copies, 4, main_ref[rows - 2 :], left[2 * rows - 4 :], right[2 * rows - 4 :])

    def put(half, value):
        lanes = slice(half * 2 * channels, (half + 1) * 2 * channels)
        hidden[0:2, :, lanes] = value[0:2]
        hidden[6:8, :, lanes] = value[2:4]

    first_layer(copies, band1_ref, bias1_ref, 2, 2, cols, put)
    hidden[2:6, :, :] = kept_ref[...]
    shift1[...] = hidden[:, 1 : 1 + cols, :]
    shift2[...] = hidden[:, 2 : 2 + cols, :]
    second_layer((hidden.at[:, 0:cols, :], shift1, shift2), band2_ref, bias2_ref, 2, 2, stage)
    value = stage[...].astype(jnp.bfloat16)
    border = value.shape[0] // 2
    out_ref[:border, :] = value[:border]
    out_ref[border : border + inner_ref.shape[0], :] = inner_ref[...]
    out_ref[border + inner_ref.shape[0] :, :] = value[border:]


def shards(features, pair_weight, target_tile, target_block, conv1_weight, conv1_bias, conv2_weight, conv2_bias):
    images, size, channels = features.shape[1:]
    top = target_tile.shape[2]
    n_frames = lax.axis_size("frames")
    n_rows = lax.axis_size("rows")
    devices = n_frames * n_rows
    capacity = max(2, 2 * images * top // devices)
    blocks = TX * TY * DEPTH // size
    n_c = CORES if n_rows % CORES == 0 else 1
    n_x = n_rows // n_c
    n_y = n_x if n_frames % n_x == 0 else 1
    n_z = n_frames // n_y
    shape = (n_z, n_y, n_x, n_c)
    groups = n_y * n_x
    slots = n_c * capacity
    per_group = n_z * slots
    stride = per_group + 1
    quarter = size // 4
    spans = [(part * quarter, quarter) for part in ORDER]

    def moved_by(value, dz=0, dy=0, dx=0, dc=0):
        pairs = []
        for source in range(devices):
            f, r = divmod(source, n_rows)
            z, y = divmod(f, n_y)
            x, c = divmod(r, n_c)
            z, y, x = step_to(z, dz, n_z), step_to(y, dy, n_y), step_to(x, dx, n_x)
            c = step_to(c, dc, n_c)
            pairs.append((source, ((z * n_y + y) * n_x + x) * n_c + c))
        return lax.ppermute(value, ("frames", "rows"), pairs)

    code = (target_tile * blocks + target_block).reshape(-1)
    weights = pair_weight[0].reshape(images * top, size, size)
    shared = [(weights, features[0], code)]
    for dc in range(1, n_c):
        shared.append(tuple(moved_by(v, dc=dc) for v in shared[0]))
    index, labels, own_weights, own_features = pl.pallas_call(
        functools.partial(index_kernel, shape, slots, blocks),
        out_shape=(
            jax.ShapeDtypeStruct((n_c * images * top,), jnp.int32),
            jax.ShapeDtypeStruct((groups * LABEL_ROWS, channels), jnp.bfloat16),
            jax.ShapeDtypeStruct(weights.shape, weights.dtype),
            jax.ShapeDtypeStruct(features.shape[1:], features.dtype),
        ),
        in_specs=[smem()] * n_c + [anywhere()] * 2,
        out_specs=(smem(), vmem(), anywhere(), anywhere()),
        scratch_shapes=[
            pltpu.SMEM((devices,), jnp.int32),
            pltpu.SMEM((groups * per_group + 1,), jnp.int32),
            pltpu.SemaphoreType.DMA((2,)),
        ],
        compiler_params=params(),
        name="index",
    )(*[v[2] for v in shared], weights, features[0])
    shared[0] = (own_weights, own_features, code)

    def contribute(ks):
        own = [spans[k] for k in ks]
        first = ks[0] == 0
        outs, scratch = [], []
        for _, chunk in own:
            outs += arrays(groups, per_group * chunk + (LABEL_ROWS if first else 0), channels)
            scratch.append(VMEM(((groups * per_group + 1) * chunk, channels), jnp.bfloat16))
        rows = sum(chunk for _, chunk in own)
        scratch += [
            VMEM((n_c * images * top, rows, size), jnp.bfloat16),
            pltpu.SemaphoreType.DMA((n_c,)),
            pltpu.SemaphoreType.DMA((len(outs) + groups,)),
        ]
        made = pl.pallas_call(
            functools.partial(contribute_kernel, n_c, groups, per_group, top, own, first),
            out_shape=tuple(outs),
            in_specs=[smem()] + [anywhere()] * n_c + [vmem()] * (n_c + 1),
            out_specs=(anywhere(),) * len(outs),
            scratch_shapes=scratch,
            compiler_params=params(),
        )(index, *[v[0] for v in shared], *[v[1] for v in shared], labels)
        for i, k in enumerate(ks):
            messages[k] = made[i * groups : (i + 1) * groups]

    def exchange(k):
        return [
            moved_by(value, dy=g // n_x, dx=g % n_x) if g else value
            for g, value in enumerate(messages[k])
        ]

    def merge(k, received, plan):
        first = k == 0
        chunk = spans[k][1]
        outs = arrays(n_z, blocks * chunk, channels)
        out_specs = [vmem()] * n_z
        scratch = [VMEM((n_z * blocks * chunk, channels), jnp.float32)]
        in_specs = [vmem()] * groups
        args = tuple(received)
        if first:
            outs.append(jax.ShapeDtypeStruct((stride * groups,), jnp.int32))
            out_specs.append(smem())
            scratch += [
                VMEM((groups, channels), jnp.int32),
                pltpu.SMEM((groups, channels), jnp.int32),
                pltpu.SemaphoreType.DMA,
            ]
        else:
            in_specs.append(smem())
            args += (plan,)
        return pl.pallas_call(
            functools.partial(merge_kernel, n_z, groups, slots, chunk, blocks, first),
            out_shape=tuple(outs),
            in_specs=in_specs,
            out_specs=tuple(out_specs),
            scratch_shapes=scratch,
            compiler_params=params(),
        )(*args)

    messages = {}
    contribute([0])
    contribute(list(range(1, len(spans))))
    plan, final = None, []
    for k in range(len(spans)):
        merged = merge(k, exchange(k), plan)
        if k == 0:
            plan = merged[-1]
        final += [moved_by(part, dz=dz) if dz else part for dz, part in enumerate(merged[:n_z])]
    bands = jax.ShapeDtypeStruct((3, 2, 9 * channels, 2 * channels), jnp.bfloat16)
    band1, band2 = pl.pallas_call(
        band_kernel,
        out_shape=(bands, bands),
        in_specs=[vmem(), vmem(), anywhere()],
        out_specs=(vmem(), vmem()),
        compiler_params=params(),
        name="bands",
    )(conv1_weight, conv2_weight, merged[0])
    cells = TX * TY
    lanes = DEPTH * channels
    halves = blocks // TX
    side = jax.ShapeDtypeStruct((2 * TX, lanes), jnp.bfloat16)
    left_cols, right_cols = pl.pallas_call(
        functools.partial(tail_kernel, n_z, blocks, halves),
        out_shape=(side, side),
        in_specs=[vmem()] * (2 * n_z) + [anywhere()],
        out_specs=(vmem(),) * 2,
        scratch_shapes=[VMEM((2, 2 * TX * DEPTH, channels), jnp.float32)],
        compiler_params=params(),
        name="tail",
    )(*final[: 2 * n_z], final[(len(spans) - 1) * n_z])

    def moved(value, axis, count, step):
        pairs = [(i, i + step) for i in range(count) if 0 <= i + step < count]
        return lax.ppermute(value, axis, pairs)

    left = moved(right_cols, "rows", n_rows, 1)
    right = moved(left_cols, "rows", n_rows, -1)
    wide = 80
    packed = jax.ShapeDtypeStruct((2, wide, lanes), jnp.bfloat16)
    main, first_rows, last_rows = pl.pallas_call(
        functools.partial(finish_kernel, n_z, spans, blocks, size),
        out_shape=(jax.ShapeDtypeStruct((cells, lanes), jnp.bfloat16), packed, packed),
        in_specs=[vmem()] * (len(final) + 2) + [anywhere()],
        out_specs=(vmem(),) * 3,
        scratch_shapes=[VMEM((cells * DEPTH, channels), jnp.float32)],
        compiler_params=params(),
        name="finish",
    )(*final, left, right, band1)
    low = moved(last_rows, "frames", n_frames, 1)
    high = moved(first_rows, "frames", n_frames, -1)
    main = main.reshape(TX, TY, lanes)
    bias = (conv1_bias[None], conv2_bias[None])

    def conv_scratch(height, hidden, out):
        return (
            [VMEM((height, wide, lanes), jnp.bfloat16)] * 3
            + [VMEM((hidden, wide, lanes), jnp.bfloat16)]
            + [VMEM((hidden, TY, lanes), jnp.bfloat16)] * 2
            + [VMEM((out * TY * DEPTH, channels), jnp.float32)]
        )

    inner, kept = pl.pallas_call(
        interior_kernel,
        out_shape=(
            jax.ShapeDtypeStruct(((TX - 4) * TY * DEPTH, channels), jnp.bfloat16),
            jax.ShapeDtypeStruct((4, wide, lanes), jnp.bfloat16),
        ),
        in_specs=[vmem()] * 7,
        out_specs=(vmem(),) * 2,
        scratch_shapes=conv_scratch(TX, TX - 2, TX - 4),
        compiler_params=params(),
        name="interior",
    )(main, left, right, band1, band2, *bias)
    out = pl.pallas_call(
        border_kernel,
        out_shape=jax.ShapeDtypeStruct((cells * DEPTH, channels), jnp.bfloat16),
        in_specs=[vmem()] * 11,
        out_specs=vmem(),
        scratch_shapes=conv_scratch(8, 8, 4),
        compiler_params=params(),
        name="border",
    )(main, low, high, left, right, band1, band2, *bias, inner, kept)
    return out.reshape(TX, TY, DEPTH, channels)


def solution(mesh):
    placed = (
        P("frames", "rows", None, None),
        P("frames", "rows", None, None, None),
        P("frames", "rows", None),
        P("frames", "rows", None),
        P(),
        P(),
        P(),
        P(),
    )
    return jax.shard_map(
        shards,
        mesh=mesh,
        in_specs=placed,
        out_specs=P("frames", "rows", None, None),
        check_vma=False,
    )
```

profile of v0, /device:TPU:1, one launch (start us, length us, event | category | flops | bytes accessed | tf_op | source)
XLA Modules:
  0.0 117.8 jit_solution(12592111049088673183)
XLA Ops:
  0.0 0.0 collective-permute-start.1
  0.0 0.5 collective-permute-start.2
  0.5 0.7 multiply_add_fusion
  1.2 0.1 copy.10
  1.3 0.1 reshape.9.refs_0_
  1.4 0.1 collective-permute-start
  1.5 3.7 %collective-permute-done.refs_1_ = s32[64]{0:T(128)S(1)} collective-permute-done((s32[64]{0:T(128)S(1)}, s32[64]{0:T(128)S(1)}, u32[]{:S(2)}, u32[]{:S(2)}) %collective-permute-start) | collective-permute-done | bytes 288 | tf_op jit(solution)/shard_map/ppermute | solution.py:436
  5.1 1.6 %copy-done = bf16[1,16,4,128,128]{4,3,2,1,0:T(8,128)(2,1)S(1)} copy-done((bf16[1,16,4,128,128]{4,3,2,1,0:T(8,128)(2,1)S(1)}, bf16[1,16,4,128,128]{4,3,2,1,0:T(8,128)(2,1)}, u32[]{:S(2)}) %copy-start) | copy-done | bytes 2097176
  6.7 1.0 copy-done.3
  7.8 2.7 %index.1 = (s32[128]{0:T(128)S(1)}, bf16[64,128]{1,0:T(8,128)(2,1)S(1)}, bf16[64,128,128]{2,1,0:T(8,128)(2,1)S(1)}, bf16[16,128,128]{2,1,0:T(8,128)(2,1)S(1)}) custom-call(s32[64]{0:T(128)S(1)} %reshape.9.refs_0_, s32[64]{0:T(128)S(1)} %collective-permute-done.refs_1_, bf16[64,128,128]{2,1,0:T(8,128)(2,1)S(1)} %bitcast.9, bf16[16,128,128]{2,1,0:T(8,128)(2,1)S(1)} %bitcast.11), custom_call_target="tpu_custom_call" | custom-call | tf_op jit(solution)/shard_map/index/pallas_call | solution.py:443
  10.5 3.5 %shard_map.84 = (bf16[1024,128]{1,0:T(8,128)(2,1)S(1)}, bf16[1024,128]{1,0:T(8,128)(2,1)S(1)}, bf16[1024,128]{1,0:T(8,128)(2,1)S(1)}, bf16[1024,128]{1,0:T(8,128...) custom-call(s32[128]{0:T(128)S(1)} %get-tuple-element.51.refs_0_, ...), custom_call_target="tpu_custom_call" | custom-call | tf_op jit(solution)/shard_map/pallas_call | solution.py:476
  13.9 2.4 %collective-permute-start.9 = (bf16[1024,128]{1,0:T(8,128)(2,1)S(1)}, bf16[1024,128]{1,0:T(8,128)(2,1)S(1)}, u32[]{:S(2)}, u32[]{:S(2)}) collective-permute-start(bf16[1024,128]{1,0:T(8,128)(2,1)S(1)} %get-tuple-element.64), channel_id=1, source_target_pairs={{0,2},{1,3},{2,0},{3,1},{4,6},{5,7},{6,4},{7,5},{8,10},{9,11},{10,... | collective-permute-start | bytes 786440 | tf_op jit(solution)/shard_map/ppermute | solution.py:436
  16.3 1.2 %collective-permute-start.10 = (bf16[1024,128]{1,0:T(8,128)(2,1)S(1)}, bf16[1024,128]{1,0:T(8,128)(2,1)S(1)}, u32[]{:S(2)}, u32[]{:S(2)}) collective-permute-start(bf16[1024,128]{1,0:T(8,128)(2,1)S(1)} %get-tuple-element.65), channel_id=1, source_target_pairs={{0,4},{1,5},{2,6},{3,7},{4,0},{5,1},{6,2},{7,3},{8,12},{9,13},{10,... | collective-permute-start | bytes 786440 | tf_op jit(solution)/shard_map/ppermute | solution.py:436
  17.6 0.0 collective-permute-start.11
  17.6 1.4 %collective-permute-start.21 = (bf16[1024,128]{1,0:T(8,128)(2,1)S(1)}, bf16[1024,128]{1,0:T(8,128)(2,1)S(1)}, u32[]{:S(2)}, u32[]{:S(2)}) collective-permute-start(bf16[1024,128]{1,0:T(8,128)(2,1)S(1)} %get-tuple-element.81), channel_id=1, source_target_pairs={{0,2},{1,3},{2,0},{3,1},{4,6},{5,7},{6,4},{7,5},{8,10},{9,11},{10,... | collective-permute-start | bytes 786440 | tf_op jit(solution)/shard_map/ppermute | solution.py:436
  19.0 2.4 %shard_map.82 = (bf16[1040,128]{1,0:T(8,128)(2,1)S(1)}, bf16[1040,128]{1,0:T(8,128)(2,1)S(1)}, bf16[1040,128]{1,0:T(8,128)(2,1)S(1)}, bf16[1040,128]{1,0:T(8,128)(2,1)S(1)}) custom-call(s32[128]{0:T(128)S(1)} %get-tuple-element.51.refs_0_, bf16[64,128,128]{2,1,0:T(8,128)(2,1)S(1)} %get-tuple-element.52.refs_1_, ...), custom_call_target="tpu_custom_call" | custom-call | tf_op jit(solution)/shard_map/pallas_call | solution.py:476
  21.4 0.1 collective-permute-start.3
  21.5 1.1 collective-permute-done.9.refs_1_
  22.7 1.2 %collective-permute-start.4 = (bf16[1040,128]{1,0:T(8,128)(2,1)S(1)}, bf16[1040,128]{1,0:T(8,128)(2,1)S(1)}, u32[]{:S(2)}, u32[]{:S(2)}) collective-permute-start(bf16[1040,128]{1,0:T(8,128)(2,1)S(1)} %get-tuple-element.57), channel_id=1, source_target_pairs={{0,4},{1,5},{2,6},{3,7},{4,0},{5,1},{6,2},{7,3},{8,12},{9,13},{10,... | collective-permute-start | bytes 798728 | tf_op jit(solution)/shard_map/ppermute | solution.py:436
  23.9 0.0 collective-permute-done.10.refs_2_
  23.9 1.2 collective-permute-start.5
  25.0 4.2 %collective-permute-done.11.refs_3_ = bf16[1024,128]{1,0:T(8,128)(2,1)S(1)} collective-permute-done((bf16[1024,128]{1,0:T(8,128)(2,1)S(1)}, bf16[1024,128]{1,0:T(8,128)(2,1)S(1)}, u32[]{:S(2)}, u32[]{:S(2)}) %collective-permute-start.11) | collective-permute-done | bytes 262176 | tf_op jit(solution)/shard_map/ppermute | solution.py:436
  29.2 1.0 collective-permute-start.22
  30.2 3.7 %collective-permute-done.21.refs_1_ = bf16[1024,128]{1,0:T(8,128)(2,1)S(1)} collective-permute-done((bf16[1024,128]{1,0:T(8,128)(2,1)S(1)}, bf16[1024,128]{1,0:T(8,128)(2,1)S(1)}, u32[]{:S(2)}, u32[]{:S(2)}) %collective-permute-start.21) | collective-permute-done | bytes 262176 | tf_op jit(solution)/shard_map/ppermute | solution.py:436
  33.9 2.1 %collective-permute-start.23 = (bf16[1024,128]{1,0:T(8,128)(2,1)S(1)}, bf16[1024,128]{1,0:T(8,128)(2,1)S(1)}, u32[]{:S(2)}, u32[]{:S(2)}) collective-permute-start(bf16[1024,128]{1,0:T(8,128)(2,1)S(1)} %get-tuple-element.83), channel_id=1, source_target_pairs={{0,6},{1,7},{2,4},{3,5},{4,2},{5,3},{6,0},{7,1},{8,14},{9,15},{10,... | collective-permute-start | bytes 786440 | tf_op jit(solution)/shard_map/ppermute | solution.py:436
  36.1 3.6 %collective-permute-done.3.refs_1_ = bf16[1040,128]{1,0:T(8,128)(2,1)S(1)} collective-permute-done((bf16[1040,128]{1,0:T(8,128)(2,1)S(1)}, bf16[1040,128]{1,0:T(8,128)(2,1)S(1)}, u32[]{:S(2)}, u32[]{:S(2)}) %collective-permute-start.3) | collective-permute-done | bytes 266272 | tf_op jit(solution)/shard_map/ppermute | solution.py:436
  39.6 1.2 %collective-permute-start.15 = (bf16[1024,128]{1,0:T(8,128)(2,1)S(1)}, bf16[1024,128]{1,0:T(8,128)(2,1)S(1)}, u32[]{:S(2)}, u32[]{:S(2)}) collective-permute-start(bf16[1024,128]{1,0:T(8,128)(2,1)S(1)} %get-tuple-element.73), channel_id=1, source_target_pairs={{0,2},{1,3},{2,0},{3,1},{4,6},{5,7},{6,4},{7,5},{8,10},{9,11},{10,... | collective-permute-start | bytes 786440 | tf_op jit(solution)/shard_map/ppermute | solution.py:436
  40.8 0.0 collective-permute-done.4.refs_2_
  40.8 1.2 %collective-permute-start.16 = (bf16[1024,128]{1,0:T(8,128)(2,1)S(1)}, bf16[1024,128]{1,0:T(8,128)(2,1)S(1)}, u32[]{:S(2)}, u32[]{:S(2)}) collective-permute-start(bf16[1024,128]{1,0:T(8,128)(2,1)S(1)} %get-tuple-element.74), channel_id=1, source_target_pairs={{0,4},{1,5},{2,6},{3,7},{4,0},{5,1},{6,2},{7,3},{8,12},{9,13},{10,... | collective-permute-start | bytes 786440 | tf_op jit(solution)/shard_map/ppermute | solution.py:436
  42.1 4.3 %collective-permute-done.5.refs_3_ = bf16[1040,128]{1,0:T(8,128)(2,1)S(1)} collective-permute-done((bf16[1040,128]{1,0:T(8,128)(2,1)S(1)}, bf16[1040,128]{1,0:T(8,128)(2,1)S(1)}, u32[]{:S(2)}, u32[]{:S(2)}) %collective-permute-start.5) | collective-permute-done | bytes 266272 | tf_op jit(solution)/shard_map/ppermute | solution.py:436
  46.3 1.2 collective-permute-start.17
  47.5 2.6 %shard_map.83 = (bf16[512,128]{1,0:T(8,128)(2,1)S(1)}, bf16[512,128]{1,0:T(8,128)(2,1)S(1)}, bf16[512,128]{1,0:T(8,128)(2,1)S(1)}, bf16[512,128]{1,0:T(8,128)(2,1)S(1)}, s32[132]{0:T(256)S(1)}) custom-call(bf16[1040,128]{1,0:T(8,128)(2,1)S(1)} %get-tuple-element.55.refs_0_, bf16[1040,128]{1,0:T(8,128)(2,1)S(1)} %collective-permute-done.3.refs_1_, ...), custom_call_target="tpu_custom_call" | custom-call | tf_op jit(solution)/shard_map/pallas_call | solution.py:512
  50.1 0.0 collective-permute-done.22.refs_2_
  50.1 1.4 %collective-permute-start.6 = (bf16[512,128]{1,0:T(8,128)(2,1)S(1)}, bf16[512,128]{1,0:T(8,128)(2,1)S(1)}, u32[]{:S(2)}, u32[]{:S(2)}) collective-permute-start(bf16[512,128]{1,0:T(8,128)(2,1)S(1)} %get-tuple-element.60), channel_id=1, source_target_pairs={{0,8},{1,9},{2,10},{3,11},{4,12},{5,13},{6,14},{7,15},{8,0},{9,1},... | collective-permute-start | bytes 393224 | tf_op jit(solution)/shard_map/ppermute | solution.py:436
  51.5 0.5 collective-permute-done.23.refs_3_
  51.9 2.3 %collective-permute-start.7 = (bf16[512,128]{1,0:T(8,128)(2,1)S(1)}, bf16[512,128]{1,0:T(8,128)(2,1)S(1)}, u32[]{:S(2)}, u32[]{:S(2)}) collective-permute-start(bf16[512,128]{1,0:T(8,128)(2,1)S(1)} %get-tuple-element.61), channel_id=1, source_target_pairs={{0,16},{1,17},{2,18},{3,19},{4,20},{5,21},{6,22},{7,23},{8,24},{9,... | collective-permute-start | bytes 393224 | tf_op jit(solution)/shard_map/ppermute | solution.py:436
  54.2 1.4 %shard_map.87 = (bf16[512,128]{1,0:T(8,128)(2,1)S(1)}, bf16[512,128]{1,0:T(8,128)(2,1)S(1)}, bf16[512,128]{1,0:T(8,128)(2,1)S(1)}, bf16[512,128]{1,0:T(8,128)(2,1)S(1)}) custom-call(bf16[1024,128]{1,0:T(8,128)(2,1)S(1)} %get-tuple-element.80.refs_0_, bf16[1024,128]{1,0:T(8,128)(2,1)S(1)} %collective-permute-done.21.refs_1_, ...), custom_call_target="tpu_custom_call" | custom-call | tf_op jit(solution)/shard_map/pallas_call | solution.py:512
  55.7 1.0 collective-permute-done.15.refs_1_
  56.6 3.3 %collective-permute-start.8 = (bf16[512,128]{1,0:T(8,128)(2,1)S(1)}, bf16[512,128]{1,0:T(8,128)(2,1)S(1)}, u32[]{:S(2)}, u32[]{:S(2)}) collective-permute-start(bf16[512,128]{1,0:T(8,128)(2,1)S(1)} %get-tuple-element.62), channel_id=1, source_target_pairs={{0,24},{1,25},{2,26},{3,27},{4,28},{5,29},{6,30},{7,31},{8,16},{9,... | collective-permute-start | bytes 393224 | tf_op jit(solution)/shard_map/ppermute | solution.py:436
  59.9 0.0 collective-permute-done.16.refs_2_
  59.9 0.7 collective-permute-start.24
  60.6 1.4 %shard_map.85 = (bf16[512,128]{1,0:T(8,128)(2,1)S(1)}, bf16[512,128]{1,0:T(8,128)(2,1)S(1)}, bf16[512,128]{1,0:T(8,128)(2,1)S(1)}, bf16[512,128]{1,0:T(8,128)(2,1)S(1)}) custom-call(bf16[1024,128]{1,0:T(8,128)(2,1)S(1)} %get-tuple-element.63.refs_0_, bf16[1024,128]{1,0:T(8,128)(2,1)S(1)} %collective-permute-done.9.refs_1_, ...), custom_call_target="tpu_custom_call" | custom-call | tf_op jit(solution)/shard_map/pallas_call | solution.py:512
  62.0 1.2 %collective-permute-done.17.refs_3_ = bf16[1024,128]{1,0:T(8,128)(2,1)S(1)} collective-permute-done((bf16[1024,128]{1,0:T(8,128)(2,1)S(1)}, bf16[1024,128]{1,0:T(8,128)(2,1)S(1)}, u32[]{:S(2)}, u32[]{:S(2)}) %collective-permute-start.17) | collective-permute-done | bytes 262176 | tf_op jit(solution)/shard_map/ppermute | solution.py:436
  63.2 1.3 %collective-permute-start.12 = (bf16[512,128]{1,0:T(8,128)(2,1)S(1)}, bf16[512,128]{1,0:T(8,128)(2,1)S(1)}, u32[]{:S(2)}, u32[]{:S(2)}) collective-permute-start(bf16[512,128]{1,0:T(8,128)(2,1)S(1)} %get-tuple-element.69), channel_id=1, source_target_pairs={{0,8},{1,9},{2,10},{3,11},{4,12},{5,13},{6,14},{7,15},{8,0},{9,1},... | collective-permute-start | bytes 393224 | tf_op jit(solution)/shard_map/ppermute | solution.py:436
  64.5 0.0 collective-permute-done.6.refs_1_
  64.5 2.3 %collective-permute-start.13 = (bf16[512,128]{1,0:T(8,128)(2,1)S(1)}, bf16[512,128]{1,0:T(8,128)(2,1)S(1)}, u32[]{:S(2)}, u32[]{:S(2)}) collective-permute-start(bf16[512,128]{1,0:T(8,128)(2,1)S(1)} %get-tuple-element.70), channel_id=1, source_target_pairs={{0,16},{1,17},{2,18},{3,19},{4,20},{5,21},{6,22},{7,23},{8,24},{9,... | collective-permute-start | bytes 393224 | tf_op jit(solution)/shard_map/ppermute | solution.py:436
  66.8 1.7 %collective-permute-start.25 = (bf16[512,128]{1,0:T(8,128)(2,1)S(1)}, bf16[512,128]{1,0:T(8,128)(2,1)S(1)}, u32[]{:S(2)}, u32[]{:S(2)}) collective-permute-start(bf16[512,128]{1,0:T(8,128)(2,1)S(1)} %get-tuple-element.86), channel_id=1, source_target_pairs={{0,16},{1,17},{2,18},{3,19},{4,20},{5,21},{6,22},{7,23},{8,24},{9,... | collective-permute-start | bytes 393224 | tf_op jit(solution)/shard_map/ppermute | solution.py:436
  68.6 1.6 %collective-permute-start.26 = (bf16[512,128]{1,0:T(8,128)(2,1)S(1)}, bf16[512,128]{1,0:T(8,128)(2,1)S(1)}, u32[]{:S(2)}, u32[]{:S(2)}) collective-permute-start(bf16[512,128]{1,0:T(8,128)(2,1)S(1)} %get-tuple-element.87), channel_id=1, source_target_pairs={{0,24},{1,25},{2,26},{3,27},{4,28},{5,29},{6,30},{7,31},{8,16},{9,... | collective-permute-start | bytes 393224 | tf_op jit(solution)/shard_map/ppermute | solution.py:436
  70.2 1.4 %shard_map.86 = (bf16[512,128]{1,0:T(8,128)(2,1)S(1)}, bf16[512,128]{1,0:T(8,128)(2,1)S(1)}, bf16[512,128]{1,0:T(8,128)(2,1)S(1)}, bf16[512,128]{1,0:T(8,128)(2,1)S(1)}) custom-call(bf16[1024,128]{1,0:T(8,128)(2,1)S(1)} %get-tuple-element.72.refs_0_, bf16[1024,128]{1,0:T(8,128)(2,1)S(1)} %collective-permute-done.15.refs_1_, ...), custom_call_target="tpu_custom_call" | custom-call | tf_op jit(solution)/shard_map/pallas_call | solution.py:512
  71.6 0.3 collective-permute-start.18
  71.9 1.7 %collective-permute-start.19 = (bf16[512,128]{1,0:T(8,128)(2,1)S(1)}, bf16[512,128]{1,0:T(8,128)(2,1)S(1)}, u32[]{:S(2)}, u32[]{:S(2)}) collective-permute-start(bf16[512,128]{1,0:T(8,128)(2,1)S(1)} %get-tuple-element.78), channel_id=1, source_target_pairs={{0,16},{1,17},{2,18},{3,19},{4,20},{5,21},{6,22},{7,23},{8,24},{9,... | collective-permute-start | bytes 393224 | tf_op jit(solution)/shard_map/ppermute | solution.py:436
  73.6 0.5 collective-permute-done.14.refs_7_
  74.1 2.7 %collective-permute-start.20 = (bf16[512,128]{1,0:T(8,128)(2,1)S(1)}, bf16[512,128]{1,0:T(8,128)(2,1)S(1)}, u32[]{:S(2)}, u32[]{:S(2)}) collective-permute-start(bf16[512,128]{1,0:T(8,128)(2,1)S(1)} %get-tuple-element.79), channel_id=1, source_target_pairs={{0,24},{1,25},{2,26},{3,27},{4,28},{5,29},{6,30},{7,31},{8,16},{9,... | collective-permute-start | bytes 393224 | tf_op jit(solution)/shard_map/ppermute | solution.py:436
  76.8 11.1 %collective-permute-done.25.refs_14_ = bf16[512,128]{1,0:T(8,128)(2,1)S(1)} collective-permute-done((bf16[512,128]{1,0:T(8,128)(2,1)S(1)}, bf16[512,128]{1,0:T(8,128)(2,1)S(1)}, u32[]{:S(2)}, u32[]{:S(2)}) %collective-permute-start.25) | collective-permute-done | bytes 131104 | tf_op jit(solution)/shard_map/ppermute | solution.py:436
  88.0 10.2 %collective-permute-start.27 = (bf16[16,512]{1,0:T(8,128)(2,1)S(1)}, bf16[16,512]{1,0:T(8,128)(2,1)S(1)}, u32[]{:S(2)}, u32[]{:S(2)}) collective-permute-start(bf16[16,512]{1,0:T(8,128)(2,1)S(1)} %get-tuple-element.88), channel_id=1, source_target_pairs={{0,1},{1,2},{2,3},{4,5},{5,6},{6,7},{8,9},{9,10},{10,11},{12,13},{... | collective-permute-start | bytes 49160 | tf_op jit(solution)/shard_map/ppermute | solution.py:555
  98.2 1.9 %collective-permute-start.28 = (bf16[16,512]{1,0:T(8,128)(2,1)S(1)}, bf16[16,512]{1,0:T(8,128)(2,1)S(1)}, u32[]{:S(2)}, u32[]{:S(2)}) collective-permute-start(bf16[16,512]{1,0:T(8,128)(2,1)S(1)} %get-tuple-element.89), channel_id=1, source_target_pairs={{1,0},{2,1},{3,2},{5,4},{6,5},{7,6},{9,8},{10,9},{11,10},{13,12},{... | collective-permute-start | bytes 49160 | tf_op jit(solution)/shard_map/ppermute | solution.py:555
  100.2 0.9 bands.1
  101.1 2.1 %collective-permute-done.28.refs_17_.right_ref = bf16[16,512]{1,0:T(8,128)(2,1)S(1)} collective-permute-done((bf16[16,512]{1,0:T(8,128)(2,1)S(1)}, bf16[16,512]{1,0:T(8,128)(2,1)S(1)}, u32[]{:S(2)}, u32[]{:S(2)}) %collective-permute-start.28) | collective-permute-done | bytes 16416 | tf_op jit(solution)/shard_map/ppermute | solution.py:555
  103.3 0.4 finish.1
  103.6 3.2 %collective-permute-start.29 = (bf16[2,80,512]{2,1,0:T(8,128)(2,1)S(1)}, bf16[2,80,512]{2,1,0:T(8,128)(2,1)S(1)}, u32[]{:S(2)}, u32[]{:S(2)}) collective-permute-start(bf16[2,80,512]{2,1,0:T(8,128)(2,1)S(1)} %get-tuple-element.92), channel_id=1, source_target_pairs={{0,4},{4,8},{8,12},{12,16},{16,20},{20,24},{24,28},{1,5},{5,9},{9,... | collective-permute-start | bytes 491528 | tf_op jit(solution)/shard_map/ppermute | solution.py:555
  106.8 1.3 %collective-permute-start.30 = (bf16[2,80,512]{2,1,0:T(8,128)(2,1)S(1)}, bf16[2,80,512]{2,1,0:T(8,128)(2,1)S(1)}, u32[]{:S(2)}, u32[]{:S(2)}) collective-permute-start(bf16[2,80,512]{2,1,0:T(8,128)(2,1)S(1)} %get-tuple-element.93), channel_id=1, source_target_pairs={{4,0},{8,4},{12,8},{16,12},{20,16},{24,20},{28,24},{5,1},{9,5},{13... | collective-permute-start | bytes 491528 | tf_op jit(solution)/shard_map/ppermute | solution.py:555
  108.2 3.6 %interior.1 = (bf16[1024,128]{1,0:T(8,128)(2,1)S(1)}, bf16[4,80,512]{2,1,0:T(8,128)(2,1)S(1)}) custom-call(bf16[8,64,512]{2,1,0:T(8,128)(2,1)S(1)} %bitcast.6, bf16[16,512]{1,0:T(8,128)(2,1)S(1)} %collective-permute-done.27.refs_16_.left_ref, bf16[16,512]{1,0:T(8,128)(2,1)S(1)} %collective-permute-done.28.refs_17_.right_ref, ...), custom_call_target="tpu_custom_call" | custom-call | tf_op jit(solution)/shard_map/interior/pallas_call | solution.py:583
  111.8 2.3 %collective-permute-done.30.high_ref = bf16[2,80,512]{2,1,0:T(8,128)(2,1)S(1)} collective-permute-done((bf16[2,80,512]{2,1,0:T(8,128)(2,1)S(1)}, bf16[2,80,512]{2,1,0:T(8,128)(2,1)S(1)}, u32[]{:S(2)}, u32[]{:S(2)}) %collective-permute-start.30) | collective-permute-done | bytes 163872 | tf_op jit(solution)/shard_map/ppermute | solution.py:555
  114.1 3.7 %border.1 = bf16[2048,128]{1,0:T(8,128)(2,1)} custom-call(bf16[8,64,512]{2,1,0:T(8,128)(2,1)S(1)} %bitcast.7, bf16[2,80,512]{2,1,0:T(8,128)(2,1)S(1)} %collective-permute-done.29.low_ref, bf16[2,80,512]{2,1,0:T(8,128)(2,1)S(1)} %collective-permute-done.30.high_ref, bf16[16,512]{1,0:T(8,128)(2,1)S(1)} %collective-permute-done.27.refs_16_.left_ref, ...), custom_call_target="tpu_custom_call" | custom-call | tf_op jit(solution)/shard_map/border/pallas_call | solution.py:595
  (25 shorter events, 0.1 us)
Async XLA Ops:
  0.0 10.4 %collective-permute-start.1 = (bf16[64,128,128]{2,1,0:T(8,128)(2,1)}, bf16[64,128,128]{2,1,0:T(8,128)(2,1)S(1)}, u32[]{:S(2)}, u32[]{:S(2)}) collective-permute-start(bf16[64,128,128]{2,1,0:T(8,128)(2,1)} %bitcast.8), channel_id=1, source_target_pairs={{0,1},{1,0},{2,3},{3,2},{4,5},{5,4},{6,7},{7,6},{8,9},{9,8},{10,11... | collective-permute-start | bytes 6291464 | tf_op jit(solution)/shard_map/ppermute | solution.py:436
  0.0 10.4 %collective-permute-start.2 = (bf16[16,128,128]{2,1,0:T(8,128)(2,1)}, bf16[16,128,128]{2,1,0:T(8,128)(2,1)S(1)}, u32[]{:S(2)}, u32[]{:S(2)}) collective-permute-start(bf16[16,128,128]{2,1,0:T(8,128)(2,1)} %bitcast.10), channel_id=1, source_target_pairs={{0,1},{1,0},{2,3},{3,2},{4,5},{5,4},{6,7},{7,6},{8,9},{9,8},{10,11... | collective-permute-start | bytes 1572872 | tf_op jit(solution)/shard_map/ppermute | solution.py:436
  1.4 3.7 %collective-permute-start = (s32[64]{0:T(128)S(1)}, s32[64]{0:T(128)S(1)}, u32[]{:S(2)}, u32[]{:S(2)}) collective-permute-start(s32[64]{0:T(128)S(1)} %reshape.9.refs_0_), channel_id=1, source_target_pairs={{0,1},{1,0},{2,3},{3,2},{4,5},{5,4},{6,7},{7,6},{8,9},{9,8},{10,11... | collective-permute-start | bytes 776 | tf_op jit(solution)/shard_map/ppermute | solution.py:436
  5.1 1.6 %copy-start = (bf16[1,16,4,128,128]{4,3,2,1,0:T(8,128)(2,1)S(1)}, bf16[1,16,4,128,128]{4,3,2,1,0:T(8,128)(2,1)}, u32[]{:S(2)}) copy-start(bf16[1,16,4,128,128]{4,3,2,1,0:T(8,128)(2,1)} %param.9) | copy-start | bytes 6291460
  6.7 1.0 copy-start.3
  13.9 8.7 %collective-permute-start.9 = (bf16[1024,128]{1,0:T(8,128)(2,1)S(1)}, bf16[1024,128]{1,0:T(8,128)(2,1)S(1)}, u32[]{:S(2)}, u32[]{:S(2)}) collective-permute-start(bf16[1024,128]{1,0:T(8,128)(2,1)S(1)} %get-tuple-element.64), channel_id=1, source_target_pairs={{0,2},{1,3},{2,0},{3,1},{4,6},{5,7},{6,4},{7,5},{8,10},{9,11},{10,... | collective-permute-start | bytes 786440 | tf_op jit(solution)/shard_map/ppermute | solution.py:436
  16.3 7.5 %collective-permute-start.10 = (bf16[1024,128]{1,0:T(8,128)(2,1)S(1)}, bf16[1024,128]{1,0:T(8,128)(2,1)S(1)}, u32[]{:S(2)}, u32[]{:S(2)}) collective-permute-start(bf16[1024,128]{1,0:T(8,128)(2,1)S(1)} %get-tuple-element.65), channel_id=1, source_target_pairs={{0,4},{1,5},{2,6},{3,7},{4,0},{5,1},{6,2},{7,3},{8,12},{9,13},{10,... | collective-permute-start | bytes 786440 | tf_op jit(solution)/shard_map/ppermute | solution.py:436
  17.6 11.7 %collective-permute-start.11 = (bf16[1024,128]{1,0:T(8,128)(2,1)S(1)}, bf16[1024,128]{1,0:T(8,128)(2,1)S(1)}, u32[]{:S(2)}, u32[]{:S(2)}) collective-permute-start(bf16[1024,128]{1,0:T(8,128)(2,1)S(1)} %get-tuple-element.66), channel_id=1, source_target_pairs={{0,6},{1,7},{2,4},{3,5},{4,2},{5,3},{6,0},{7,1},{8,14},{9,15},{10,... | collective-permute-start | bytes 786440 | tf_op jit(solution)/shard_map/ppermute | solution.py:436
  17.6 16.3 %collective-permute-start.21 = (bf16[1024,128]{1,0:T(8,128)(2,1)S(1)}, bf16[1024,128]{1,0:T(8,128)(2,1)S(1)}, u32[]{:S(2)}, u32[]{:S(2)}) collective-permute-start(bf16[1024,128]{1,0:T(8,128)(2,1)S(1)} %get-tuple-element.81), channel_id=1, source_target_pairs={{0,2},{1,3},{2,0},{3,1},{4,6},{5,7},{6,4},{7,5},{8,10},{9,11},{10,... | collective-permute-start | bytes 786440 | tf_op jit(solution)/shard_map/ppermute | solution.py:436
  21.4 18.3 %collective-permute-start.3 = (bf16[1040,128]{1,0:T(8,128)(2,1)S(1)}, bf16[1040,128]{1,0:T(8,128)(2,1)S(1)}, u32[]{:S(2)}, u32[]{:S(2)}) collective-permute-start(bf16[1040,128]{1,0:T(8,128)(2,1)S(1)} %get-tuple-element.56), channel_id=1, source_target_pairs={{0,2},{1,3},{2,0},{3,1},{4,6},{5,7},{6,4},{7,5},{8,10},{9,11},{10,... | collective-permute-start | bytes 798728 | tf_op jit(solution)/shard_map/ppermute | solution.py:436
  22.7 18.2 %collective-permute-start.4 = (bf16[1040,128]{1,0:T(8,128)(2,1)S(1)}, bf16[1040,128]{1,0:T(8,128)(2,1)S(1)}, u32[]{:S(2)}, u32[]{:S(2)}) collective-permute-start(bf16[1040,128]{1,0:T(8,128)(2,1)S(1)} %get-tuple-element.57), channel_id=1, source_target_pairs={{0,4},{1,5},{2,6},{3,7},{4,0},{5,1},{6,2},{7,3},{8,12},{9,13},{10,... | collective-permute-start | bytes 798728 | tf_op jit(solution)/shard_map/ppermute | solution.py:436
  23.9 22.4 %collective-permute-start.5 = (bf16[1040,128]{1,0:T(8,128)(2,1)S(1)}, bf16[1040,128]{1,0:T(8,128)(2,1)S(1)}, u32[]{:S(2)}, u32[]{:S(2)}) collective-permute-start(bf16[1040,128]{1,0:T(8,128)(2,1)S(1)} %get-tuple-element.58), channel_id=1, source_target_pairs={{0,6},{1,7},{2,4},{3,5},{4,2},{5,3},{6,0},{7,1},{8,14},{9,15},{10,... | collective-permute-start | bytes 798728 | tf_op jit(solution)/shard_map/ppermute | solution.py:436
  29.2 20.8 %collective-permute-start.22 = (bf16[1024,128]{1,0:T(8,128)(2,1)S(1)}, bf16[1024,128]{1,0:T(8,128)(2,1)S(1)}, u32[]{:S(2)}, u32[]{:S(2)}) collective-permute-start(bf16[1024,128]{1,0:T(8,128)(2,1)S(1)} %get-tuple-element.82), channel_id=1, source_target_pairs={{0,4},{1,5},{2,6},{3,7},{4,0},{5,1},{6,2},{7,3},{8,12},{9,13},{10,... | collective-permute-start | bytes 786440 | tf_op jit(solution)/shard_map/ppermute | solution.py:436
  33.9 18.0 %collective-permute-start.23 = (bf16[1024,128]{1,0:T(8,128)(2,1)S(1)}, bf16[1024,128]{1,0:T(8,128)(2,1)S(1)}, u32[]{:S(2)}, u32[]{:S(2)}) collective-permute-start(bf16[1024,128]{1,0:T(8,128)(2,1)S(1)} %get-tuple-element.83), channel_id=1, source_target_pairs={{0,6},{1,7},{2,4},{3,5},{4,2},{5,3},{6,0},{7,1},{8,14},{9,15},{10,... | collective-permute-start | bytes 786440 | tf_op jit(solution)/shard_map/ppermute | solution.py:436
  39.6 17.0 %collective-permute-start.15 = (bf16[1024,128]{1,0:T(8,128)(2,1)S(1)}, bf16[1024,128]{1,0:T(8,128)(2,1)S(1)}, u32[]{:S(2)}, u32[]{:S(2)}) collective-permute-start(bf16[1024,128]{1,0:T(8,128)(2,1)S(1)} %get-tuple-element.73), channel_id=1, source_target_pairs={{0,2},{1,3},{2,0},{3,1},{4,6},{5,7},{6,4},{7,5},{8,10},{9,11},{10,... | collective-permute-start | bytes 786440 | tf_op jit(solution)/shard_map/ppermute | solution.py:436
  40.8 19.1 %collective-permute-start.16 = (bf16[1024,128]{1,0:T(8,128)(2,1)S(1)}, bf16[1024,128]{1,0:T(8,128)(2,1)S(1)}, u32[]{:S(2)}, u32[]{:S(2)}) collective-permute-start(bf16[1024,128]{1,0:T(8,128)(2,1)S(1)} %get-tuple-element.74), channel_id=1, source_target_pairs={{0,4},{1,5},{2,6},{3,7},{4,0},{5,1},{6,2},{7,3},{8,12},{9,13},{10,... | collective-permute-start | bytes 786440 | tf_op jit(solution)/shard_map/ppermute | solution.py:436
  46.3 16.9 %collective-permute-start.17 = (bf16[1024,128]{1,0:T(8,128)(2,1)S(1)}, bf16[1024,128]{1,0:T(8,128)(2,1)S(1)}, u32[]{:S(2)}, u32[]{:S(2)}) collective-permute-start(bf16[1024,128]{1,0:T(8,128)(2,1)S(1)} %get-tuple-element.75), channel_id=1, source_target_pairs={{0,6},{1,7},{2,4},{3,5},{4,2},{5,3},{6,0},{7,1},{8,14},{9,15},{10,... | collective-permute-start | bytes 786440 | tf_op jit(solution)/shard_map/ppermute | solution.py:436
  50.1 14.4 %collective-permute-start.6 = (bf16[512,128]{1,0:T(8,128)(2,1)S(1)}, bf16[512,128]{1,0:T(8,128)(2,1)S(1)}, u32[]{:S(2)}, u32[]{:S(2)}) collective-permute-start(bf16[512,128]{1,0:T(8,128)(2,1)S(1)} %get-tuple-element.60), channel_id=1, source_target_pairs={{0,8},{1,9},{2,10},{3,11},{4,12},{5,13},{6,14},{7,15},{8,0},{9,1},... | collective-permute-start | bytes 393224 | tf_op jit(solution)/shard_map/ppermute | solution.py:436
  51.9 14.9 %collective-permute-start.7 = (bf16[512,128]{1,0:T(8,128)(2,1)S(1)}, bf16[512,128]{1,0:T(8,128)(2,1)S(1)}, u32[]{:S(2)}, u32[]{:S(2)}) collective-permute-start(bf16[512,128]{1,0:T(8,128)(2,1)S(1)} %get-tuple-element.61), channel_id=1, source_target_pairs={{0,16},{1,17},{2,18},{3,19},{4,20},{5,21},{6,22},{7,23},{8,24},{9,... | collective-permute-start | bytes 393224 | tf_op jit(solution)/shard_map/ppermute | solution.py:436
  54.2 45.9 %copy-start.1 = (bf16[3,3,3,128,128]{4,3,2,1,0:T(8,128)(2,1)S(1)}, bf16[3,3,3,128,128]{4,3,2,1,0:T(8,128)(2,1)}, u32[]{:S(2)}) copy-start(bf16[3,3,3,128,128]{4,3,2,1,0:T(8,128)(2,1)} %first_ref.1) | copy-start | bytes 2654212
  54.2 45.9 %copy-start.2 = (bf16[3,3,3,128,128]{4,3,2,1,0:T(8,128)(2,1)S(1)}, bf16[3,3,3,128,128]{4,3,2,1,0:T(8,128)(2,1)}, u32[]{:S(2)}) copy-start(bf16[3,3,3,128,128]{4,3,2,1,0:T(8,128)(2,1)} %second_ref.1) | copy-start | bytes 2654212
  56.6 10.2 %collective-permute-start.8 = (bf16[512,128]{1,0:T(8,128)(2,1)S(1)}, bf16[512,128]{1,0:T(8,128)(2,1)S(1)}, u32[]{:S(2)}, u32[]{:S(2)}) collective-permute-start(bf16[512,128]{1,0:T(8,128)(2,1)S(1)} %get-tuple-element.62), channel_id=1, source_target_pairs={{0,24},{1,25},{2,26},{3,27},{4,28},{5,29},{6,30},{7,31},{8,16},{9,... | collective-permute-start | bytes 393224 | tf_op jit(solution)/shard_map/ppermute | solution.py:436
  59.9 8.6 %collective-permute-start.24 = (bf16[512,128]{1,0:T(8,128)(2,1)S(1)}, bf16[512,128]{1,0:T(8,128)(2,1)S(1)}, u32[]{:S(2)}, u32[]{:S(2)}) collective-permute-start(bf16[512,128]{1,0:T(8,128)(2,1)S(1)} %get-tuple-element.85), channel_id=1, source_target_pairs={{0,8},{1,9},{2,10},{3,11},{4,12},{5,13},{6,14},{7,15},{8,0},{9,1},... | collective-permute-start | bytes 393224 | tf_op jit(solution)/shard_map/ppermute | solution.py:436
  63.2 8.4 %collective-permute-start.12 = (bf16[512,128]{1,0:T(8,128)(2,1)S(1)}, bf16[512,128]{1,0:T(8,128)(2,1)S(1)}, u32[]{:S(2)}, u32[]{:S(2)}) collective-permute-start(bf16[512,128]{1,0:T(8,128)(2,1)S(1)} %get-tuple-element.69), channel_id=1, source_target_pairs={{0,8},{1,9},{2,10},{3,11},{4,12},{5,13},{6,14},{7,15},{8,0},{9,1},... | collective-permute-start | bytes 393224 | tf_op jit(solution)/shard_map/ppermute | solution.py:436
  64.5 7.4 %collective-permute-start.13 = (bf16[512,128]{1,0:T(8,128)(2,1)S(1)}, bf16[512,128]{1,0:T(8,128)(2,1)S(1)}, u32[]{:S(2)}, u32[]{:S(2)}) collective-permute-start(bf16[512,128]{1,0:T(8,128)(2,1)S(1)} %get-tuple-element.70), channel_id=1, source_target_pairs={{0,16},{1,17},{2,18},{3,19},{4,20},{5,21},{6,22},{7,23},{8,24},{9,... | collective-permute-start | bytes 393224 | tf_op jit(solution)/shard_map/ppermute | solution.py:436
  66.8 7.3 %collective-permute-start.14 = (bf16[512,128]{1,0:T(8,128)(2,1)S(1)}, bf16[512,128]{1,0:T(8,128)(2,1)S(1)}, u32[]{:S(2)}, u32[]{:S(2)}) collective-permute-start(bf16[512,128]{1,0:T(8,128)(2,1)S(1)} %get-tuple-element.71), channel_id=1, source_target_pairs={{0,24},{1,25},{2,26},{3,27},{4,28},{5,29},{6,30},{7,31},{8,16},{9,... | collective-permute-start | bytes 393224 | tf_op jit(solution)/shard_map/ppermute | solution.py:436
  66.8 21.1 %collective-permute-start.25 = (bf16[512,128]{1,0:T(8,128)(2,1)S(1)}, bf16[512,128]{1,0:T(8,128)(2,1)S(1)}, u32[]{:S(2)}, u32[]{:S(2)}) collective-permute-start(bf16[512,128]{1,0:T(8,128)(2,1)S(1)} %get-tuple-element.86), channel_id=1, source_target_pairs={{0,16},{1,17},{2,18},{3,19},{4,20},{5,21},{6,22},{7,23},{8,24},{9,... | collective-permute-start | bytes 393224 | tf_op jit(solution)/shard_map/ppermute | solution.py:436
  68.6 29.7 %collective-permute-start.26 = (bf16[512,128]{1,0:T(8,128)(2,1)S(1)}, bf16[512,128]{1,0:T(8,128)(2,1)S(1)}, u32[]{:S(2)}, u32[]{:S(2)}) collective-permute-start(bf16[512,128]{1,0:T(8,128)(2,1)S(1)} %get-tuple-element.87), channel_id=1, source_target_pairs={{0,24},{1,25},{2,26},{3,27},{4,28},{5,29},{6,30},{7,31},{8,16},{9,... | collective-permute-start | bytes 393224 | tf_op jit(solution)/shard_map/ppermute | solution.py:436
  71.6 29.5 %collective-permute-start.18 = (bf16[512,128]{1,0:T(8,128)(2,1)S(1)}, bf16[512,128]{1,0:T(8,128)(2,1)S(1)}, u32[]{:S(2)}, u32[]{:S(2)}) collective-permute-start(bf16[512,128]{1,0:T(8,128)(2,1)S(1)} %get-tuple-element.77), channel_id=1, source_target_pairs={{0,8},{1,9},{2,10},{3,11},{4,12},{5,13},{6,14},{7,15},{8,0},{9,1},... | collective-permute-start | bytes 393224 | tf_op jit(solution)/shard_map/ppermute | solution.py:436
  71.9 29.2 %collective-permute-start.19 = (bf16[512,128]{1,0:T(8,128)(2,1)S(1)}, bf16[512,128]{1,0:T(8,128)(2,1)S(1)}, u32[]{:S(2)}, u32[]{:S(2)}) collective-permute-start(bf16[512,128]{1,0:T(8,128)(2,1)S(1)} %get-tuple-element.78), channel_id=1, source_target_pairs={{0,16},{1,17},{2,18},{3,19},{4,20},{5,21},{6,22},{7,23},{8,24},{9,... | collective-permute-start | bytes 393224 | tf_op jit(solution)/shard_map/ppermute | solution.py:436
  74.1 27.0 %collective-permute-start.20 = (bf16[512,128]{1,0:T(8,128)(2,1)S(1)}, bf16[512,128]{1,0:T(8,128)(2,1)S(1)}, u32[]{:S(2)}, u32[]{:S(2)}) collective-permute-start(bf16[512,128]{1,0:T(8,128)(2,1)S(1)} %get-tuple-element.79), channel_id=1, source_target_pairs={{0,24},{1,25},{2,26},{3,27},{4,28},{5,29},{6,30},{7,31},{8,16},{9,... | collective-permute-start | bytes 393224 | tf_op jit(solution)/shard_map/ppermute | solution.py:436
  88.0 13.2 %collective-permute-start.27 = (bf16[16,512]{1,0:T(8,128)(2,1)S(1)}, bf16[16,512]{1,0:T(8,128)(2,1)S(1)}, u32[]{:S(2)}, u32[]{:S(2)}) collective-permute-start(bf16[16,512]{1,0:T(8,128)(2,1)S(1)} %get-tuple-element.88), channel_id=1, source_target_pairs={{0,1},{1,2},{2,3},{4,5},{5,6},{6,7},{8,9},{9,10},{10,11},{12,13},{... | collective-permute-start | bytes 49160 | tf_op jit(solution)/shard_map/ppermute | solution.py:555
  98.2 5.1 %collective-permute-start.28 = (bf16[16,512]{1,0:T(8,128)(2,1)S(1)}, bf16[16,512]{1,0:T(8,128)(2,1)S(1)}, u32[]{:S(2)}, u32[]{:S(2)}) collective-permute-start(bf16[16,512]{1,0:T(8,128)(2,1)S(1)} %get-tuple-element.89), channel_id=1, source_target_pairs={{1,0},{2,1},{3,2},{5,4},{6,5},{7,6},{9,8},{10,9},{11,10},{13,12},{... | collective-permute-start | bytes 49160 | tf_op jit(solution)/shard_map/ppermute | solution.py:555
  103.3 4.9 %copy-start.4 = (f32[128]{0:T(128)S(1)}, f32[128]{0:T(128)}, u32[]{:S(2)}) copy-start(f32[128]{0:T(128)} %param.13) | copy-start | bytes 1540
  103.3 4.9 %copy-start.5 = (f32[128]{0:T(128)S(1)}, f32[128]{0:T(128)}, u32[]{:S(2)}) copy-start(f32[128]{0:T(128)} %param.15) | copy-start | bytes 1540
  103.6 8.1 %collective-permute-start.29 = (bf16[2,80,512]{2,1,0:T(8,128)(2,1)S(1)}, bf16[2,80,512]{2,1,0:T(8,128)(2,1)S(1)}, u32[]{:S(2)}, u32[]{:S(2)}) collective-permute-start(bf16[2,80,512]{2,1,0:T(8,128)(2,1)S(1)} %get-tuple-element.92), channel_id=1, source_target_pairs={{0,4},{4,8},{8,12},{12,16},{16,20},{20,24},{24,28},{1,5},{5,9},{9,... | collective-permute-start | bytes 491528 | tf_op jit(solution)/shard_map/ppermute | solution.py:555
  106.8 7.2 %collective-permute-start.30 = (bf16[2,80,512]{2,1,0:T(8,128)(2,1)S(1)}, bf16[2,80,512]{2,1,0:T(8,128)(2,1)S(1)}, u32[]{:S(2)}, u32[]{:S(2)}) collective-permute-start(bf16[2,80,512]{2,1,0:T(8,128)(2,1)S(1)} %get-tuple-element.93), channel_id=1, source_target_pairs={{4,0},{8,4},{12,8},{16,12},{20,16},{24,20},{28,24},{5,1},{9,5},{13... | collective-permute-start | bytes 491528 | tf_op jit(solution)/shard_map/ppermute | solution.py:555
where the time goes:
time: 118 us
  starting transfers between devices  50.7 us (43%)
  waiting for transfers between devices  39.4 us (33%)
  Pallas kernels  23.9 us (20%)
  local copies, waits for them, and re-layouts  2.82 us (2%)
    ppermute x27, waiting for transfers between devices, moved_by(): return lax.ppermute(value, ('frames', 'rows'), pairs)  34.9 us
    ppermute x27, starting transfers between devices, moved_by(): return lax.ppermute(value, ('frames', 'rows'), pairs)  34.1 us
    ppermute x4, starting transfers between devices, moved(): return lax.ppermute(value, axis, pairs)  16.6 us
    pallas_call x4, Pallas kernels, merge(): pl.pallas_call(functools.partial(merge_kernel, n_z, groups, slots, chunk,...  6.83 us
    pallas_call x2, Pallas kernels, contribute(): pl.pallas_call(functools.partial(contribute_kernel, n_c, groups, per_grou...  5.85 us
    ppermute x4, waiting for transfers between devices, moved(): return lax.ppermute(value, axis, pairs)  4.46 us
    pallas_call x1, Pallas kernels, shards(): pl.pallas_call(border_kernel, out_shape=jax.ShapeDtypeStruct((cells * DEP...  3.68 us
    pallas_call x1, Pallas kernels, shards(): pl.pallas_call(interior_kernel, out_shape=(jax.ShapeDtypeStruct(((TX - 4)...  3.61 us
  transfers between devices with their start and end apart: 31, of which 13 were waited for; matrix products, arithmetic and copies ran while one was open for 1% of the time, Pallas kernels for 14%

commit v1 on v0

--- a/solution.py
+++ b/solution.py
@@ -59,13 +59,7 @@
 def index_kernel(shape, slots, blocks, *refs):
     n_z, n_y, n_x, n_c = shape
     codes = refs[:n_c]
-    weight_ref, feature_ref, index_ref, label_ref, weight_out, feature_out, counts, labels, sems = refs[n_c:]
-    copies = [
-        pltpu.make_async_copy(feature_ref, feature_out, sems.at[0]),
-        pltpu.make_async_copy(weight_ref, weight_out, sems.at[1]),
-    ]
-    for copy in copies:
-        copy.start()
+    index_ref, label_ref, counts, labels = refs[n_c:]
     tiles = n_z * n_y * n_x * n_c
     groups = n_y * n_x
     spare = groups * n_z * slots
@@ -108,37 +102,46 @@
         for k in range(n_z * slots):
             row = jnp.where(lane == k, labels[g * n_z * slots + k], row)
         label_ref[g * LABEL_ROWS : (g + 1) * LABEL_ROWS, :] = row.astype(jnp.float32).astype(jnp.bfloat16)
-    for copy in copies:
-        copy.wait()
-
-
-def contribute_kernel(n_c, groups, per_group, top, spans, first, *refs):
+
+
+def contribute_kernel(n_c, groups, per_group, images, top, spans, first, *refs):
     index_ref = refs[0]
-    sources = refs[1 : 1 + n_c]
-    features = refs[1 + n_c : 1 + 2 * n_c]
-    refs = refs[1 + 2 * n_c :]
-    label_ref = refs[0]
-    outs = refs[1 : 1 + groups * len(spans)]
-    refs = refs[1 + groups * len(spans) :]
-    buffers = refs[: len(spans)]
-    held, load_sems, store_sems = refs[len(spans) :]
-    images = features[0].shape[0]
+    heads = refs[1 : 1 + n_c]
+    refs = refs[1 + n_c :]
     begin, rows = min(span[0] for span in spans), sum(span[1] for span in spans)
-    loads = [
-        pltpu.make_async_copy(
-            sources[s].at[:, pl.ds(begin, rows), :], held.at[pl.ds(s * images * top, images * top)], load_sems.at[s]
-        )
-        for s in range(n_c)
-    ]
-    for load in loads:
-        load.start()
+    pairs = images * top
+    size = heads[0].shape[1]
+    if first:
+        label_ref, refs = refs[0], refs[1:]
+    else:
+        sources, refs = refs[:n_c], refs[n_c:]
+    outs = refs[: groups * len(spans)]
+    refs = refs[groups * len(spans) :]
+    buffers, refs = refs[: len(spans)], refs[len(spans) :]
+    store_sems = refs[0]
+    if not first:
+        held, load_sems = refs[1:]
+        loads = [
+            pltpu.make_async_copy(
+                sources[s].at[:, pl.ds(begin, rows), :], held.at[pl.ds(s * pairs, pairs)], load_sems.at[s]
+            )
+            for s in range(n_c)
+        ]
+        for load in loads:
+            load.start()
     for s in range(n_c):
-        loads[s].wait()
+        if not first:
+            loads[s].wait()
+        base = heads[s].shape[0] - images * size
 
         def image(b, carry):
-            p0 = s * images * top + b * top
-            weights = held[pl.ds(p0, top)].reshape(top * rows, held.shape[2])
-            product = jnp.dot(weights, features[s][b], preferred_element_type=jnp.float32)
+            p0 = s * pairs + b * top
+            if first:
+                weights = heads[s][pl.ds(pl.multiple_of(b * top * rows, top * rows), top * rows), :]
+            else:
+                weights = held[pl.ds(p0, top)].reshape(top * rows, size)
+            pixels = heads[s][pl.ds(pl.multiple_of(base + b * size, size), size), :]
+            product = jnp.dot(weights, pixels, preferred_element_type=jnp.float32)
             product = product.astype(jnp.bfloat16)
             for t in range(top):
                 slot = index_ref[p0 + t]
@@ -437,28 +440,25 @@
 
     code = (target_tile * blocks + target_block).reshape(-1)
     weights = pair_weight[0].reshape(images * top, size, size)
-    shared = [(weights, features[0], code)]
+    begin, rows = spans[0]
+    head = jnp.concatenate(
+        [weights[:, begin : begin + rows].reshape(-1, size), features[0].reshape(-1, channels)], axis=0
+    )
+    shared = [(code, head, weights)]
     for dc in range(1, n_c):
         shared.append(tuple(moved_by(v, dc=dc) for v in shared[0]))
-    index, labels, own_weights, own_features = pl.pallas_call(
+    index, labels = pl.pallas_call(
         functools.partial(index_kernel, shape, slots, blocks),
         out_shape=(
             jax.ShapeDtypeStruct((n_c * images * top,), jnp.int32),
             jax.ShapeDtypeStruct((groups * LABEL_ROWS, channels), jnp.bfloat16),
-            jax.ShapeDtypeStruct(weights.shape, weights.dtype),
-            jax.ShapeDtypeStruct(features.shape[1:], features.dtype),
         ),
-        in_specs=[smem()] * n_c + [anywhere()] * 2,
-        out_specs=(smem(), vmem(), anywhere(), anywhere()),
-        scratch_shapes=[
-            pltpu.SMEM((devices,), jnp.int32),
-            pltpu.SMEM((groups * per_group + 1,), jnp.int32),
-            pltpu.SemaphoreType.DMA((2,)),
-        ],
+        in_specs=[smem()] * n_c,
+        out_specs=(smem(), vmem()),
+        scratch_shapes=[pltpu.SMEM((devices,), jnp.int32), pltpu.SMEM((groups * per_group + 1,), jnp.int32)],
         compiler_params=params(),
         name="index",
-    )(*[v[2] for v in shared], weights, features[0])
-    shared[0] = (own_weights, own_features, code)
+    )(*[v[0] for v in shared])
 
     def contribute(ks):
         own = [spans[k] for k in ks]
@@ -468,19 +468,27 @@
             outs += arrays(groups, per_group * chunk + (LABEL_ROWS if first else 0), channels)
             scratch.append(VMEM(((groups * per_group + 1) * chunk, channels), jnp.bfloat16))
         rows = sum(chunk for _, chunk in own)
-        scratch += [
-            VMEM((n_c * images * top, rows, size), jnp.bfloat16),
-            pltpu.SemaphoreType.DMA((n_c,)),
-            pltpu.SemaphoreType.DMA((len(outs) + groups,)),
-        ]
+        scratch.append(pltpu.SemaphoreType.DMA((len(outs) + groups,)))
+        in_specs = [smem()] + [vmem()] * n_c
+        args = [index] + [v[1] for v in shared]
+        if first:
+            in_specs.append(vmem())
+            args.append(labels)
+        else:
+            in_specs += [anywhere()] * n_c
+            args += [v[2] for v in shared]
+            scratch += [
+                VMEM((n_c * images * top, rows, size), jnp.bfloat16),
+                pltpu.SemaphoreType.DMA((n_c,)),
+            ]
         made = pl.pallas_call(
-            functools.partial(contribute_kernel, n_c, groups, per_group, top, own, first),
+            functools.partial(contribute_kernel, n_c, groups, per_group, images, top, own, first),
             out_shape=tuple(outs),
-            in_specs=[smem()] + [anywhere()] * n_c + [vmem()] * (n_c + 1),
+            in_specs=in_specs,
             out_specs=(anywhere(),) * len(outs),
             scratch_shapes=scratch,
             compiler_params=params(),
-        )(index, *[v[0] for v in shared], *[v[1] for v in shared], labels)
+        )(*args)
         for i, k in enumerate(ks):
             messages[k] = made[i * groups : (i + 1) * groups]
 

time: 118 us -> 119 us (level)
  waiting for transfers between devices: 39.4 us -> 44.9 us
  starting transfers between devices: 50.7 us -> 47 us
  local copies, waits for them, and re-layouts: 2.82 us -> 1.29 us
    ppermute x27, starting transfers between devices: 34.1 us -> 23.9 us  [moved_by(): return lax.ppermute(value, ('frames', 'rows'), pairs)]
    ppermute x4, starting transfers between devices: 16.6 us -> 23.1 us  [moved(): return lax.ppermute(value, axis, pairs)]
    ppermute x27, waiting for transfers between devices: 34.9 us -> 40.4 us  [moved_by(): return lax.ppermute(value, ('frames', 'rows'), pairs)]
    unnamed x12 -> x14, local copies, waits for them, and re-layouts: 2.65 us -> 0.03 us
  transfers between devices with their start and end apart: 31 -> 31, of which waited for: 13 -> 13; matrix products, arithmetic and copies ran while one was open for 1% -> 2% of each run, Pallas kernels for 14% -> 17%
where the time goes in v1:
time: 119 us; the launch traced here: 118 us
  starting transfers between devices  47 us (39%)
  waiting for transfers between devices  44.9 us (38%)
  Pallas kernels  23.6 us (20%)
  local copies, waits for them, and re-layouts  1.29 us (1%)
    ppermute x27, waiting for transfers between devices, moved_by(): return lax.ppermute(value, ('frames', 'rows'), pairs)  40.4 us
    ppermute x27, starting transfers between devices, moved_by(): return lax.ppermute(value, ('frames', 'rows'), pairs)  23.9 us
    ppermute x4, starting transfers between devices, moved(): return lax.ppermute(value, axis, pairs)  23.1 us
    pallas_call x4, Pallas kernels, merge(): pl.pallas_call(functools.partial(merge_kernel, n_z, groups, slots, chunk,...  6.83 us
    pallas_call x2, Pallas kernels, contribute(): pl.pallas_call(functools.partial(contribute_kernel, n_c, groups, per_grou...  5.72 us
    ppermute x4, waiting for transfers between devices, moved(): return lax.ppermute(value, axis, pairs)  4.47 us
    pallas_call x1, Pallas kernels, shards(): pl.pallas_call(border_kernel, out_shape=jax.ShapeDtypeStruct((cells * DEP...  3.68 us
    pallas_call x1, Pallas kernels, shards(): pl.pallas_call(interior_kernel, out_shape=(jax.ShapeDtypeStruct(((TX - 4)...  3.61 us
  transfers between devices with their start and end apart: 31, of which 13 were waited for; matrix products, arithmetic and copies ran while one was open for 2% of the time, Pallas kernels for 17%

profile of v1, /device:TPU:1, one launch (start us, length us, event | category | flops | bytes accessed | tf_op | source)
XLA Modules:
  0.0 118.1 jit_solution(5287483689684159513)
XLA Ops:
  0.0 0.0 collective-permute-start.8
  0.0 1.1 slice.4
  1.1 1.1 pad_maximum_fusion.refs_1_
  2.2 0.5 collective-permute-start.1
  2.8 0.1 copy.10
  2.9 0.1 reshape.12.refs_0_
  3.0 0.0 copy-start
  3.0 0.1 collective-permute-start
  3.1 2.8 %collective-permute-done.refs_1_ = s32[64]{0:T(128)S(1)} collective-permute-done((s32[64]{0:T(128)S(1)}, s32[64]{0:T(128)S(1)}, u32[]{:S(2)}, u32[]{:S(2)}) %collective-permute-start) | collective-permute-done | bytes 288 | tf_op jit(solution)/shard_map/ppermute | solution.py:439
  5.9 2.5 %index.1 = (s32[128]{0:T(128)S(1)}, bf16[64,128]{1,0:T(8,128)(2,1)S(1)}) custom-call(s32[64]{0:T(128)S(1)} %reshape.12.refs_0_, s32[64]{0:T(128)S(1)} %collective-permute-done.refs_1_), custom_call_target="tpu_custom_call" | custom-call | tf_op jit(solution)/shard_map/index/pallas_call | solution.py:450
  8.3 2.1 %shard_map.82 = (bf16[1040,128]{1,0:T(8,128)(2,1)S(1)}, bf16[1040,128]{1,0:T(8,128)(2,1)S(1)}, bf16[1040,128]{1,0:T(8,128)(2,1)S(1)}, bf16[1040,128]{1,0:T(8,128)(2,1)S(1)}) custom-call(s32[128]{0:T(128)S(1)} %get-tuple-element.49.refs_0_, bf16[4096,128]{1,0:T(8,128)(2,1)S(1)} %pad_maximum_fusion.refs_1_, ...), custom_call_target="tpu_custom_call" | custom-call | tf_op jit(solution)/shard_map/pallas_call | solution.py:484
  10.5 2.4 %collective-permute-start.2 = (bf16[1040,128]{1,0:T(8,128)(2,1)S(1)}, bf16[1040,128]{1,0:T(8,128)(2,1)S(1)}, u32[]{:S(2)}, u32[]{:S(2)}) collective-permute-start(bf16[1040,128]{1,0:T(8,128)(2,1)S(1)} %get-tuple-element.52), channel_id=1, source_target_pairs={{0,2},{1,3},{2,0},{3,1},{4,6},{5,7},{6,4},{7,5},{8,10},{9,11},{10,... | collective-permute-start | bytes 798728 | tf_op jit(solution)/shard_map/ppermute | solution.py:439
  12.9 1.2 %collective-permute-start.3 = (bf16[1040,128]{1,0:T(8,128)(2,1)S(1)}, bf16[1040,128]{1,0:T(8,128)(2,1)S(1)}, u32[]{:S(2)}, u32[]{:S(2)}) collective-permute-start(bf16[1040,128]{1,0:T(8,128)(2,1)S(1)} %get-tuple-element.53), channel_id=1, source_target_pairs={{0,4},{1,5},{2,6},{3,7},{4,0},{5,1},{6,2},{7,3},{8,12},{9,13},{10,... | collective-permute-start | bytes 798728 | tf_op jit(solution)/shard_map/ppermute | solution.py:439
  14.1 0.0 collective-permute-start.4
  14.2 5.1 %collective-permute-done.2.refs_1_ = bf16[1040,128]{1,0:T(8,128)(2,1)S(1)} collective-permute-done((bf16[1040,128]{1,0:T(8,128)(2,1)S(1)}, bf16[1040,128]{1,0:T(8,128)(2,1)S(1)}, u32[]{:S(2)}, u32[]{:S(2)}) %collective-permute-start.2) | collective-permute-done | bytes 266272 | tf_op jit(solution)/shard_map/ppermute | solution.py:439
  19.3 0.9 collective-permute-done.3.refs_2_
  20.2 5.8 %collective-permute-done.4.refs_3_ = bf16[1040,128]{1,0:T(8,128)(2,1)S(1)} collective-permute-done((bf16[1040,128]{1,0:T(8,128)(2,1)S(1)}, bf16[1040,128]{1,0:T(8,128)(2,1)S(1)}, u32[]{:S(2)}, u32[]{:S(2)}) %collective-permute-start.4) | collective-permute-done | bytes 266272 | tf_op jit(solution)/shard_map/ppermute | solution.py:439
  26.0 2.6 %shard_map.83 = (bf16[512,128]{1,0:T(8,128)(2,1)S(1)}, bf16[512,128]{1,0:T(8,128)(2,1)S(1)}, bf16[512,128]{1,0:T(8,128)(2,1)S(1)}, bf16[512,128]{1,0:T(8,128)(2,1)S(1)}, s32[132]{0:T(256)S(1)}) custom-call(bf16[1040,128]{1,0:T(8,128)(2,1)S(1)} %get-tuple-element.51.refs_0_, bf16[1040,128]{1,0:T(8,128)(2,1)S(1)} %collective-permute-done.2.refs_1_, ...), custom_call_target="tpu_custom_call" | custom-call | tf_op jit(solution)/shard_map/pallas_call | solution.py:520
  28.6 1.4 %collective-permute-start.5 = (bf16[512,128]{1,0:T(8,128)(2,1)S(1)}, bf16[512,128]{1,0:T(8,128)(2,1)S(1)}, u32[]{:S(2)}, u32[]{:S(2)}) collective-permute-start(bf16[512,128]{1,0:T(8,128)(2,1)S(1)} %get-tuple-element.56), channel_id=1, source_target_pairs={{0,8},{1,9},{2,10},{3,11},{4,12},{5,13},{6,14},{7,15},{8,0},{9,1},... | collective-permute-start | bytes 393224 | tf_op jit(solution)/shard_map/ppermute | solution.py:439
  29.9 0.0 collective-permute-done.8.refs_4_
  30.0 3.6 %shard_map.84 = (bf16[1024,128]{1,0:T(8,128)(2,1)S(1)}, bf16[1024,128]{1,0:T(8,128)(2,1)S(1)}, bf16[1024,128]{1,0:T(8,128)(2,1)S(1)}, bf16[1024,128]{1,0:T(8,128...) custom-call(s32[128]{0:T(128)S(1)} %get-tuple-element.49.refs_0_, ...), custom_call_target="tpu_custom_call" | custom-call | tf_op jit(solution)/shard_map/pallas_call | solution.py:484
  33.5 1.1 collective-permute-start.9
  34.6 2.3 %collective-permute-start.6 = (bf16[512,128]{1,0:T(8,128)(2,1)S(1)}, bf16[512,128]{1,0:T(8,128)(2,1)S(1)}, u32[]{:S(2)}, u32[]{:S(2)}) collective-permute-start(bf16[512,128]{1,0:T(8,128)(2,1)S(1)} %get-tuple-element.57), channel_id=1, source_target_pairs={{0,16},{1,17},{2,18},{3,19},{4,20},{5,21},{6,22},{7,23},{8,24},{9,... | collective-permute-start | bytes 393224 | tf_op jit(solution)/shard_map/ppermute | solution.py:439
  36.9 0.3 collective-permute-start.10
  37.2 1.4 %collective-permute-start.11 = (bf16[1024,128]{1,0:T(8,128)(2,1)S(1)}, bf16[1024,128]{1,0:T(8,128)(2,1)S(1)}, u32[]{:S(2)}, u32[]{:S(2)}) collective-permute-start(bf16[1024,128]{1,0:T(8,128)(2,1)S(1)} %get-tuple-element.62), channel_id=1, source_target_pairs={{0,6},{1,7},{2,4},{3,5},{4,2},{5,3},{6,0},{7,1},{8,14},{9,15},{10,... | collective-permute-start | bytes 786440 | tf_op jit(solution)/shard_map/ppermute | solution.py:439
  38.6 1.0 collective-permute-start.15
  39.6 3.2 %collective-permute-done.6.refs_2_ = bf16[512,128]{1,0:T(8,128)(2,1)S(1)} collective-permute-done((bf16[512,128]{1,0:T(8,128)(2,1)S(1)}, bf16[512,128]{1,0:T(8,128)(2,1)S(1)}, u32[]{:S(2)}, u32[]{:S(2)}) %collective-permute-start.6) | collective-permute-done | bytes 131104 | tf_op jit(solution)/shard_map/ppermute | solution.py:439
  42.8 0.0 collective-permute-start.16
  42.8 0.0 collective-permute-done.9.refs_1_
  42.8 1.5 %collective-permute-start.17 = (bf16[1024,128]{1,0:T(8,128)(2,1)S(1)}, bf16[1024,128]{1,0:T(8,128)(2,1)S(1)}, u32[]{:S(2)}, u32[]{:S(2)}) collective-permute-start(bf16[1024,128]{1,0:T(8,128)(2,1)S(1)} %get-tuple-element.71), channel_id=1, source_target_pairs={{0,6},{1,7},{2,4},{3,5},{4,2},{5,3},{6,0},{7,1},{8,14},{9,15},{10,... | collective-permute-start | bytes 786440 | tf_op jit(solution)/shard_map/ppermute | solution.py:439
  44.3 3.2 %collective-permute-done.10.refs_2_ = bf16[1024,128]{1,0:T(8,128)(2,1)S(1)} collective-permute-done((bf16[1024,128]{1,0:T(8,128)(2,1)S(1)}, bf16[1024,128]{1,0:T(8,128)(2,1)S(1)}, u32[]{:S(2)}, u32[]{:S(2)}) %collective-permute-start.10) | collective-permute-done | bytes 262176 | tf_op jit(solution)/shard_map/ppermute | solution.py:439
  47.6 0.0 collective-permute-start.21
  47.6 0.0 collective-permute-done.11.refs_3_
  47.6 1.9 %collective-permute-start.22 = (bf16[1024,128]{1,0:T(8,128)(2,1)S(1)}, bf16[1024,128]{1,0:T(8,128)(2,1)S(1)}, u32[]{:S(2)}, u32[]{:S(2)}) collective-permute-start(bf16[1024,128]{1,0:T(8,128)(2,1)S(1)} %get-tuple-element.78), channel_id=1, source_target_pairs={{0,4},{1,5},{2,6},{3,7},{4,0},{5,1},{6,2},{7,3},{8,12},{9,13},{10,... | collective-permute-start | bytes 786440 | tf_op jit(solution)/shard_map/ppermute | solution.py:439
  49.5 2.1 %collective-permute-done.15.refs_1_ = bf16[1024,128]{1,0:T(8,128)(2,1)S(1)} collective-permute-done((bf16[1024,128]{1,0:T(8,128)(2,1)S(1)}, bf16[1024,128]{1,0:T(8,128)(2,1)S(1)}, u32[]{:S(2)}, u32[]{:S(2)}) %collective-permute-start.15) | collective-permute-done | bytes 262176 | tf_op jit(solution)/shard_map/ppermute | solution.py:439
  51.5 0.5 collective-permute-start.23
  52.0 6.7 %collective-permute-done.16.refs_2_ = bf16[1024,128]{1,0:T(8,128)(2,1)S(1)} collective-permute-done((bf16[1024,128]{1,0:T(8,128)(2,1)S(1)}, bf16[1024,128]{1,0:T(8,128)(2,1)S(1)}, u32[]{:S(2)}, u32[]{:S(2)}) %collective-permute-start.16) | collective-permute-done | bytes 262176 | tf_op jit(solution)/shard_map/ppermute | solution.py:439
  58.8 0.0 collective-permute-start.7
  58.8 1.4 %shard_map.85 = (bf16[512,128]{1,0:T(8,128)(2,1)S(1)}, bf16[512,128]{1,0:T(8,128)(2,1)S(1)}, bf16[512,128]{1,0:T(8,128)(2,1)S(1)}, bf16[512,128]{1,0:T(8,128)(2,1)S(1)}) custom-call(bf16[1024,128]{1,0:T(8,128)(2,1)S(1)} %get-tuple-element.59.refs_0_, bf16[1024,128]{1,0:T(8,128)(2,1)S(1)} %collective-permute-done.9.refs_1_, ...), custom_call_target="tpu_custom_call" | custom-call | tf_op jit(solution)/shard_map/pallas_call | solution.py:520
  60.2 0.3 collective-permute-start.12
  60.5 1.4 %shard_map.86 = (bf16[512,128]{1,0:T(8,128)(2,1)S(1)}, bf16[512,128]{1,0:T(8,128)(2,1)S(1)}, bf16[512,128]{1,0:T(8,128)(2,1)S(1)}, bf16[512,128]{1,0:T(8,128)(2,1)S(1)}) custom-call(bf16[1024,128]{1,0:T(8,128)(2,1)S(1)} %get-tuple-element.68.refs_0_, bf16[1024,128]{1,0:T(8,128)(2,1)S(1)} %collective-permute-done.15.refs_1_, ...), custom_call_target="tpu_custom_call" | custom-call | tf_op jit(solution)/shard_map/pallas_call | solution.py:520
  61.9 2.6 %collective-permute-done.7.refs_3_ = bf16[512,128]{1,0:T(8,128)(2,1)S(1)} collective-permute-done((bf16[512,128]{1,0:T(8,128)(2,1)S(1)}, bf16[512,128]{1,0:T(8,128)(2,1)S(1)}, u32[]{:S(2)}, u32[]{:S(2)}) %collective-permute-start.7) | collective-permute-done | bytes 131104 | tf_op jit(solution)/shard_map/ppermute | solution.py:439
  64.5 0.8 collective-permute-start.13
  65.3 0.0 collective-permute-start.14
  65.3 6.2 %collective-permute-done.22.refs_2_ = bf16[1024,128]{1,0:T(8,128)(2,1)S(1)} collective-permute-done((bf16[1024,128]{1,0:T(8,128)(2,1)S(1)}, bf16[1024,128]{1,0:T(8,128)(2,1)S(1)}, u32[]{:S(2)}, u32[]{:S(2)}) %collective-permute-start.22) | collective-permute-done | bytes 262176 | tf_op jit(solution)/shard_map/ppermute | solution.py:439
  71.5 0.2 collective-permute-start.18
  71.7 0.0 collective-permute-done.23.refs_3_
  71.7 0.0 collective-permute-start.19
  71.7 3.4 %collective-permute-start.20 = (bf16[512,128]{1,0:T(8,128)(2,1)S(1)}, bf16[512,128]{1,0:T(8,128)(2,1)S(1)}, u32[]{:S(2)}, u32[]{:S(2)}) collective-permute-start(bf16[512,128]{1,0:T(8,128)(2,1)S(1)} %get-tuple-element.75), channel_id=1, source_target_pairs={{0,24},{1,25},{2,26},{3,27},{4,28},{5,29},{6,30},{7,31},{8,16},{9,... | collective-permute-start | bytes 393224 | tf_op jit(solution)/shard_map/ppermute | solution.py:439
  75.1 1.4 %shard_map.87 = (bf16[512,128]{1,0:T(8,128)(2,1)S(1)}, bf16[512,128]{1,0:T(8,128)(2,1)S(1)}, bf16[512,128]{1,0:T(8,128)(2,1)S(1)}, bf16[512,128]{1,0:T(8,128)(2,1)S(1)}) custom-call(bf16[1024,128]{1,0:T(8,128)(2,1)S(1)} %get-tuple-element.76.refs_0_, bf16[1024,128]{1,0:T(8,128)(2,1)S(1)} %collective-permute-done.21.refs_1_, ...), custom_call_target="tpu_custom_call" | custom-call | tf_op jit(solution)/shard_map/pallas_call | solution.py:520
  76.5 0.1 collective-permute-start.24
  76.6 0.3 collective-permute-start.25
  76.8 3.3 %collective-permute-start.26 = (bf16[512,128]{1,0:T(8,128)(2,1)S(1)}, bf16[512,128]{1,0:T(8,128)(2,1)S(1)}, u32[]{:S(2)}, u32[]{:S(2)}) collective-permute-start(bf16[512,128]{1,0:T(8,128)(2,1)S(1)} %get-tuple-element.83), channel_id=1, source_target_pairs={{0,24},{1,25},{2,26},{3,27},{4,28},{5,29},{6,30},{7,31},{8,16},{9,... | collective-permute-start | bytes 393224 | tf_op jit(solution)/shard_map/ppermute | solution.py:439
  80.1 1.8 %collective-permute-done.19.refs_10_ = bf16[512,128]{1,0:T(8,128)(2,1)S(1)} collective-permute-done((bf16[512,128]{1,0:T(8,128)(2,1)S(1)}, bf16[512,128]{1,0:T(8,128)(2,1)S(1)}, u32[]{:S(2)}, u32[]{:S(2)}) %collective-permute-start.19) | collective-permute-done | bytes 131104 | tf_op jit(solution)/shard_map/ppermute | solution.py:439
  81.9 16.5 %collective-permute-start.27 = (bf16[16,512]{1,0:T(8,128)(2,1)S(1)}, bf16[16,512]{1,0:T(8,128)(2,1)S(1)}, u32[]{:S(2)}, u32[]{:S(2)}) collective-permute-start(bf16[16,512]{1,0:T(8,128)(2,1)S(1)} %get-tuple-element.84), channel_id=1, source_target_pairs={{0,1},{1,2},{2,3},{4,5},{5,6},{6,7},{8,9},{9,10},{10,11},{12,13},{... | collective-permute-start | bytes 49160 | tf_op jit(solution)/shard_map/ppermute | solution.py:563
  98.4 1.9 %collective-permute-start.28 = (bf16[16,512]{1,0:T(8,128)(2,1)S(1)}, bf16[16,512]{1,0:T(8,128)(2,1)S(1)}, u32[]{:S(2)}, u32[]{:S(2)}) collective-permute-start(bf16[16,512]{1,0:T(8,128)(2,1)S(1)} %get-tuple-element.85), channel_id=1, source_target_pairs={{1,0},{2,1},{3,2},{5,4},{6,5},{7,6},{9,8},{10,9},{11,10},{13,12},{... | collective-permute-start | bytes 49160 | tf_op jit(solution)/shard_map/ppermute | solution.py:563
  100.3 0.9 bands.1
  101.3 2.1 %collective-permute-done.28.refs_17_.right_ref = bf16[16,512]{1,0:T(8,128)(2,1)S(1)} collective-permute-done((bf16[16,512]{1,0:T(8,128)(2,1)S(1)}, bf16[16,512]{1,0:T(8,128)(2,1)S(1)}, u32[]{:S(2)}, u32[]{:S(2)}) %collective-permute-start.28) | collective-permute-done | bytes 16416 | tf_op jit(solution)/shard_map/ppermute | solution.py:563
  103.4 0.4 finish.1
  103.8 3.4 %collective-permute-start.29 = (bf16[2,80,512]{2,1,0:T(8,128)(2,1)S(1)}, bf16[2,80,512]{2,1,0:T(8,128)(2,1)S(1)}, u32[]{:S(2)}, u32[]{:S(2)}) collective-permute-start(bf16[2,80,512]{2,1,0:T(8,128)(2,1)S(1)} %get-tuple-element.88), channel_id=1, source_target_pairs={{0,4},{4,8},{8,12},{12,16},{16,20},{20,24},{24,28},{1,5},{5,9},{9,... | collective-permute-start | bytes 491528 | tf_op jit(solution)/shard_map/ppermute | solution.py:563
  107.2 1.3 %collective-permute-start.30 = (bf16[2,80,512]{2,1,0:T(8,128)(2,1)S(1)}, bf16[2,80,512]{2,1,0:T(8,128)(2,1)S(1)}, u32[]{:S(2)}, u32[]{:S(2)}) collective-permute-start(bf16[2,80,512]{2,1,0:T(8,128)(2,1)S(1)} %get-tuple-element.89), channel_id=1, source_target_pairs={{4,0},{8,4},{12,8},{16,12},{20,16},{24,20},{28,24},{5,1},{9,5},{13... | collective-permute-start | bytes 491528 | tf_op jit(solution)/shard_map/ppermute | solution.py:563
  108.5 3.6 %interior.1 = (bf16[1024,128]{1,0:T(8,128)(2,1)S(1)}, bf16[4,80,512]{2,1,0:T(8,128)(2,1)S(1)}) custom-call(bf16[8,64,512]{2,1,0:T(8,128)(2,1)S(1)} %bitcast.10, bf16[16,512]{1,0:T(8,128)(2,1)S(1)} %collective-permute-done.27.refs_16_.left_ref, bf16[16,512]{1,0:T(8,128)(2,1)S(1)} %collective-permute-done.28.refs_17_.right_ref, ...), custom_call_target="tpu_custom_call" | custom-call | tf_op jit(solution)/shard_map/interior/pallas_call | solution.py:591
  112.1 2.3 %collective-permute-done.30.high_ref = bf16[2,80,512]{2,1,0:T(8,128)(2,1)S(1)} collective-permute-done((bf16[2,80,512]{2,1,0:T(8,128)(2,1)S(1)}, bf16[2,80,512]{2,1,0:T(8,128)(2,1)S(1)}, u32[]{:S(2)}, u32[]{:S(2)}) %collective-permute-start.30) | collective-permute-done | bytes 163872 | tf_op jit(solution)/shard_map/ppermute | solution.py:563
  114.5 3.7 %border.1 = bf16[2048,128]{1,0:T(8,128)(2,1)} custom-call(bf16[8,64,512]{2,1,0:T(8,128)(2,1)S(1)} %bitcast.11, bf16[2,80,512]{2,1,0:T(8,128)(2,1)S(1)} %collective-permute-done.29.low_ref, bf16[2,80,512]{2,1,0:T(8,128)(2,1)S(1)} %collective-permute-done.30.high_ref, bf16[16,512]{1,0:T(8,128)(2,1)S(1)} %collective-permute-done.27.refs_16_.left_ref, ...), custom_call_target="tpu_custom_call" | custom-call | tf_op jit(solution)/shard_map/border/pallas_call | solution.py:603
  (29 shorter events, 0.1 us)
Async XLA Ops:
  0.0 2.8 %copy-start.5 = (s32[1,16,4]{1,2,0:T(4,128)S(1)}, s32[1,16,4]{1,2,0:T(4,128)}, u32[]{:S(2)}) copy-start(s32[1,16,4]{1,2,0:T(4,128)} %param.11) | copy-start | bytes 772
  0.0 2.8 %copy-start.6 = (s32[1,16,4]{1,2,0:T(4,128)S(1)}, s32[1,16,4]{1,2,0:T(4,128)}, u32[]{:S(2)}) copy-start(s32[1,16,4]{1,2,0:T(4,128)} %param.10) | copy-start | bytes 772
  0.0 29.9 %collective-permute-start.8 = (bf16[64,128,128]{2,1,0:T(8,128)(2,1)}, bf16[64,128,128]{2,1,0:T(8,128)(2,1)}, u32[]{:S(2)}, u32[]{:S(2)}) collective-permute-start(bf16[64,128,128]{2,1,0:T(8,128)(2,1)} %bitcast.7), channel_id=1, source_target_pairs={{0,1},{1,0},{2,3},{3,2},{4,5},{5,4},{6,7},{7,6},{8,9},{9,8},{10,11... | collective-permute-start | bytes 6291464 | tf_op jit(solution)/shard_map/ppermute | solution.py:439
  2.2 6.1 %collective-permute-start.1 = (bf16[4096,128]{1,0:T(8,128)(2,1)S(1)}, bf16[4096,128]{1,0:T(8,128)(2,1)S(1)}, u32[]{:S(2)}, u32[]{:S(2)}) collective-permute-start(bf16[4096,128]{1,0:T(8,128)(2,1)S(1)} %pad_maximum_fusion.refs_1_), channel_id=1, source_target_pairs={{0,1},{1,0},{2,3},{3,2},{4,5},{5,4},{6,7},{7,6},{8,9},{9,8},{10,11... | collective-permute-start | bytes 3145736 | tf_op jit(solution)/shard_map/ppermute | solution.py:439
  3.0 27.0 %copy-start = (bf16[1,16,4,128,128]{4,3,2,1,0:T(8,128)(2,1)S(1)}, bf16[1,16,4,128,128]{4,3,2,1,0:T(8,128)(2,1)}, u32[]{:S(2)}) copy-start(bf16[1,16,4,128,128]{4,3,2,1,0:T(8,128)(2,1)} %param.9) | copy-start | bytes 6291460
  3.0 2.9 %collective-permute-start = (s32[64]{0:T(128)S(1)}, s32[64]{0:T(128)S(1)}, u32[]{:S(2)}, u32[]{:S(2)}) collective-permute-start(s32[64]{0:T(128)S(1)} %reshape.12.refs_0_), channel_id=1, source_target_pairs={{0,1},{1,0},{2,3},{3,2},{4,5},{5,4},{6,7},{7,6},{8,9},{9,8},{10,11... | collective-permute-start | bytes 776 | tf_op jit(solution)/shard_map/ppermute | solution.py:439
  10.5 8.8 %collective-permute-start.2 = (bf16[1040,128]{1,0:T(8,128)(2,1)S(1)}, bf16[1040,128]{1,0:T(8,128)(2,1)S(1)}, u32[]{:S(2)}, u32[]{:S(2)}) collective-permute-start(bf16[1040,128]{1,0:T(8,128)(2,1)S(1)} %get-tuple-element.52), channel_id=1, source_target_pairs={{0,2},{1,3},{2,0},{3,1},{4,6},{5,7},{6,4},{7,5},{8,10},{9,11},{10,... | collective-permute-start | bytes 798728 | tf_op jit(solution)/shard_map/ppermute | solution.py:439
  12.9 7.3 %collective-permute-start.3 = (bf16[1040,128]{1,0:T(8,128)(2,1)S(1)}, bf16[1040,128]{1,0:T(8,128)(2,1)S(1)}, u32[]{:S(2)}, u32[]{:S(2)}) collective-permute-start(bf16[1040,128]{1,0:T(8,128)(2,1)S(1)} %get-tuple-element.53), channel_id=1, source_target_pairs={{0,4},{1,5},{2,6},{3,7},{4,0},{5,1},{6,2},{7,3},{8,12},{9,13},{10,... | collective-permute-start | bytes 798728 | tf_op jit(solution)/shard_map/ppermute | solution.py:439
  14.1 11.8 %collective-permute-start.4 = (bf16[1040,128]{1,0:T(8,128)(2,1)S(1)}, bf16[1040,128]{1,0:T(8,128)(2,1)S(1)}, u32[]{:S(2)}, u32[]{:S(2)}) collective-permute-start(bf16[1040,128]{1,0:T(8,128)(2,1)S(1)} %get-tuple-element.54), channel_id=1, source_target_pairs={{0,6},{1,7},{2,4},{3,5},{4,2},{5,3},{6,0},{7,1},{8,14},{9,15},{10,... | collective-permute-start | bytes 798728 | tf_op jit(solution)/shard_map/ppermute | solution.py:439
  28.6 10.0 %collective-permute-start.5 = (bf16[512,128]{1,0:T(8,128)(2,1)S(1)}, bf16[512,128]{1,0:T(8,128)(2,1)S(1)}, u32[]{:S(2)}, u32[]{:S(2)}) collective-permute-start(bf16[512,128]{1,0:T(8,128)(2,1)S(1)} %get-tuple-element.56), channel_id=1, source_target_pairs={{0,8},{1,9},{2,10},{3,11},{4,12},{5,13},{6,14},{7,15},{8,0},{9,1},... | collective-permute-start | bytes 393224 | tf_op jit(solution)/shard_map/ppermute | solution.py:439
  33.5 9.2 %collective-permute-start.9 = (bf16[1024,128]{1,0:T(8,128)(2,1)S(1)}, bf16[1024,128]{1,0:T(8,128)(2,1)S(1)}, u32[]{:S(2)}, u32[]{:S(2)}) collective-permute-start(bf16[1024,128]{1,0:T(8,128)(2,1)S(1)} %get-tuple-element.60), channel_id=1, source_target_pairs={{0,2},{1,3},{2,0},{3,1},{4,6},{5,7},{6,4},{7,5},{8,10},{9,11},{10,... | collective-permute-start | bytes 786440 | tf_op jit(solution)/shard_map/ppermute | solution.py:439
  34.6 8.1 %collective-permute-start.6 = (bf16[512,128]{1,0:T(8,128)(2,1)S(1)}, bf16[512,128]{1,0:T(8,128)(2,1)S(1)}, u32[]{:S(2)}, u32[]{:S(2)}) collective-permute-start(bf16[512,128]{1,0:T(8,128)(2,1)S(1)} %get-tuple-element.57), channel_id=1, source_target_pairs={{0,16},{1,17},{2,18},{3,19},{4,20},{5,21},{6,22},{7,23},{8,24},{9,... | collective-permute-start | bytes 393224 | tf_op jit(solution)/shard_map/ppermute | solution.py:439
  36.9 10.6 %collective-permute-start.10 = (bf16[1024,128]{1,0:T(8,128)(2,1)S(1)}, bf16[1024,128]{1,0:T(8,128)(2,1)S(1)}, u32[]{:S(2)}, u32[]{:S(2)}) collective-permute-start(bf16[1024,128]{1,0:T(8,128)(2,1)S(1)} %get-tuple-element.61), channel_id=1, source_target_pairs={{0,4},{1,5},{2,6},{3,7},{4,0},{5,1},{6,2},{7,3},{8,12},{9,13},{10,... | collective-permute-start | bytes 786440 | tf_op jit(solution)/shard_map/ppermute | solution.py:439
  37.2 10.4 %collective-permute-start.11 = (bf16[1024,128]{1,0:T(8,128)(2,1)S(1)}, bf16[1024,128]{1,0:T(8,128)(2,1)S(1)}, u32[]{:S(2)}, u32[]{:S(2)}) collective-permute-start(bf16[1024,128]{1,0:T(8,128)(2,1)S(1)} %get-tuple-element.62), channel_id=1, source_target_pairs={{0,6},{1,7},{2,4},{3,5},{4,2},{5,3},{6,0},{7,1},{8,14},{9,15},{10,... | collective-permute-start | bytes 786440 | tf_op jit(solution)/shard_map/ppermute | solution.py:439
  38.6 12.9 %collective-permute-start.15 = (bf16[1024,128]{1,0:T(8,128)(2,1)S(1)}, bf16[1024,128]{1,0:T(8,128)(2,1)S(1)}, u32[]{:S(2)}, u32[]{:S(2)}) collective-permute-start(bf16[1024,128]{1,0:T(8,128)(2,1)S(1)} %get-tuple-element.69), channel_id=1, source_target_pairs={{0,2},{1,3},{2,0},{3,1},{4,6},{5,7},{6,4},{7,5},{8,10},{9,11},{10,... | collective-permute-start | bytes 786440 | tf_op jit(solution)/shard_map/ppermute | solution.py:439
  42.8 16.0 %collective-permute-start.16 = (bf16[1024,128]{1,0:T(8,128)(2,1)S(1)}, bf16[1024,128]{1,0:T(8,128)(2,1)S(1)}, u32[]{:S(2)}, u32[]{:S(2)}) collective-permute-start(bf16[1024,128]{1,0:T(8,128)(2,1)S(1)} %get-tuple-element.70), channel_id=1, source_target_pairs={{0,4},{1,5},{2,6},{3,7},{4,0},{5,1},{6,2},{7,3},{8,12},{9,13},{10,... | collective-permute-start | bytes 786440 | tf_op jit(solution)/shard_map/ppermute | solution.py:439
  42.8 17.4 %collective-permute-start.17 = (bf16[1024,128]{1,0:T(8,128)(2,1)S(1)}, bf16[1024,128]{1,0:T(8,128)(2,1)S(1)}, u32[]{:S(2)}, u32[]{:S(2)}) collective-permute-start(bf16[1024,128]{1,0:T(8,128)(2,1)S(1)} %get-tuple-element.71), channel_id=1, source_target_pairs={{0,6},{1,7},{2,4},{3,5},{4,2},{5,3},{6,0},{7,1},{8,14},{9,15},{10,... | collective-permute-start | bytes 786440 | tf_op jit(solution)/shard_map/ppermute | solution.py:439
  47.6 17.7 %collective-permute-start.21 = (bf16[1024,128]{1,0:T(8,128)(2,1)S(1)}, bf16[1024,128]{1,0:T(8,128)(2,1)S(1)}, u32[]{:S(2)}, u32[]{:S(2)}) collective-permute-start(bf16[1024,128]{1,0:T(8,128)(2,1)S(1)} %get-tuple-element.77), channel_id=1, source_target_pairs={{0,2},{1,3},{2,0},{3,1},{4,6},{5,7},{6,4},{7,5},{8,10},{9,11},{10,... | collective-permute-start | bytes 786440 | tf_op jit(solution)/shard_map/ppermute | solution.py:439
  47.6 23.9 %collective-permute-start.22 = (bf16[1024,128]{1,0:T(8,128)(2,1)S(1)}, bf16[1024,128]{1,0:T(8,128)(2,1)S(1)}, u32[]{:S(2)}, u32[]{:S(2)}) collective-permute-start(bf16[1024,128]{1,0:T(8,128)(2,1)S(1)} %get-tuple-element.78), channel_id=1, source_target_pairs={{0,4},{1,5},{2,6},{3,7},{4,0},{5,1},{6,2},{7,3},{8,12},{9,13},{10,... | collective-permute-start | bytes 786440 | tf_op jit(solution)/shard_map/ppermute | solution.py:439
  51.5 20.2 %collective-permute-start.23 = (bf16[1024,128]{1,0:T(8,128)(2,1)S(1)}, bf16[1024,128]{1,0:T(8,128)(2,1)S(1)}, u32[]{:S(2)}, u32[]{:S(2)}) collective-permute-start(bf16[1024,128]{1,0:T(8,128)(2,1)S(1)} %get-tuple-element.79), channel_id=1, source_target_pairs={{0,6},{1,7},{2,4},{3,5},{4,2},{5,3},{6,0},{7,1},{8,14},{9,15},{10,... | collective-permute-start | bytes 786440 | tf_op jit(solution)/shard_map/ppermute | solution.py:439
  58.8 5.7 %collective-permute-start.7 = (bf16[512,128]{1,0:T(8,128)(2,1)S(1)}, bf16[512,128]{1,0:T(8,128)(2,1)S(1)}, u32[]{:S(2)}, u32[]{:S(2)}) collective-permute-start(bf16[512,128]{1,0:T(8,128)(2,1)S(1)} %get-tuple-element.58), channel_id=1, source_target_pairs={{0,24},{1,25},{2,26},{3,27},{4,28},{5,29},{6,30},{7,31},{8,16},{9,... | collective-permute-start | bytes 393224 | tf_op jit(solution)/shard_map/ppermute | solution.py:439
  58.8 41.5 %copy-start.1 = (bf16[3,3,3,128,128]{4,3,2,1,0:T(8,128)(2,1)S(1)}, bf16[3,3,3,128,128]{4,3,2,1,0:T(8,128)(2,1)}, u32[]{:S(2)}) copy-start(bf16[3,3,3,128,128]{4,3,2,1,0:T(8,128)(2,1)} %first_ref.1) | copy-start | bytes 2654212
  58.8 41.5 %copy-start.2 = (bf16[3,3,3,128,128]{4,3,2,1,0:T(8,128)(2,1)S(1)}, bf16[3,3,3,128,128]{4,3,2,1,0:T(8,128)(2,1)}, u32[]{:S(2)}) copy-start(bf16[3,3,3,128,128]{4,3,2,1,0:T(8,128)(2,1)} %second_ref.1) | copy-start | bytes 2654212
  60.2 11.5 %collective-permute-start.12 = (bf16[512,128]{1,0:T(8,128)(2,1)S(1)}, bf16[512,128]{1,0:T(8,128)(2,1)S(1)}, u32[]{:S(2)}, u32[]{:S(2)}) collective-permute-start(bf16[512,128]{1,0:T(8,128)(2,1)S(1)} %get-tuple-element.65), channel_id=1, source_target_pairs={{0,8},{1,9},{2,10},{3,11},{4,12},{5,13},{6,14},{7,15},{8,0},{9,1},... | collective-permute-start | bytes 393224 | tf_op jit(solution)/shard_map/ppermute | solution.py:439
  64.5 12.0 %collective-permute-start.13 = (bf16[512,128]{1,0:T(8,128)(2,1)S(1)}, bf16[512,128]{1,0:T(8,128)(2,1)S(1)}, u32[]{:S(2)}, u32[]{:S(2)}) collective-permute-start(bf16[512,128]{1,0:T(8,128)(2,1)S(1)} %get-tuple-element.66), channel_id=1, source_target_pairs={{0,16},{1,17},{2,18},{3,19},{4,20},{5,21},{6,22},{7,23},{8,24},{9,... | collective-permute-start | bytes 393224 | tf_op jit(solution)/shard_map/ppermute | solution.py:439
  65.3 11.3 %collective-permute-start.14 = (bf16[512,128]{1,0:T(8,128)(2,1)S(1)}, bf16[512,128]{1,0:T(8,128)(2,1)S(1)}, u32[]{:S(2)}, u32[]{:S(2)}) collective-permute-start(bf16[512,128]{1,0:T(8,128)(2,1)S(1)} %get-tuple-element.67), channel_id=1, source_target_pairs={{0,24},{1,25},{2,26},{3,27},{4,28},{5,29},{6,30},{7,31},{8,16},{9,... | collective-permute-start | bytes 393224 | tf_op jit(solution)/shard_map/ppermute | solution.py:439
  71.5 5.3 %collective-permute-start.18 = (bf16[512,128]{1,0:T(8,128)(2,1)S(1)}, bf16[512,128]{1,0:T(8,128)(2,1)S(1)}, u32[]{:S(2)}, u32[]{:S(2)}) collective-permute-start(bf16[512,128]{1,0:T(8,128)(2,1)S(1)} %get-tuple-element.73), channel_id=1, source_target_pairs={{0,8},{1,9},{2,10},{3,11},{4,12},{5,13},{6,14},{7,15},{8,0},{9,1},... | collective-permute-start | bytes 393224 | tf_op jit(solution)/shard_map/ppermute | solution.py:439
  71.7 10.2 %collective-permute-start.19 = (bf16[512,128]{1,0:T(8,128)(2,1)S(1)}, bf16[512,128]{1,0:T(8,128)(2,1)S(1)}, u32[]{:S(2)}, u32[]{:S(2)}) collective-permute-start(bf16[512,128]{1,0:T(8,128)(2,1)S(1)} %get-tuple-element.74), channel_id=1, source_target_pairs={{0,16},{1,17},{2,18},{3,19},{4,20},{5,21},{6,22},{7,23},{8,24},{9,... | collective-permute-start | bytes 393224 | tf_op jit(solution)/shard_map/ppermute | solution.py:439
  71.7 26.7 %collective-permute-start.20 = (bf16[512,128]{1,0:T(8,128)(2,1)S(1)}, bf16[512,128]{1,0:T(8,128)(2,1)S(1)}, u32[]{:S(2)}, u32[]{:S(2)}) collective-permute-start(bf16[512,128]{1,0:T(8,128)(2,1)S(1)} %get-tuple-element.75), channel_id=1, source_target_pairs={{0,24},{1,25},{2,26},{3,27},{4,28},{5,29},{6,30},{7,31},{8,16},{9,... | collective-permute-start | bytes 393224 | tf_op jit(solution)/shard_map/ppermute | solution.py:439
  76.5 24.8 %collective-permute-start.24 = (bf16[512,128]{1,0:T(8,128)(2,1)S(1)}, bf16[512,128]{1,0:T(8,128)(2,1)S(1)}, u32[]{:S(2)}, u32[]{:S(2)}) collective-permute-start(bf16[512,128]{1,0:T(8,128)(2,1)S(1)} %get-tuple-element.81), channel_id=1, source_target_pairs={{0,8},{1,9},{2,10},{3,11},{4,12},{5,13},{6,14},{7,15},{8,0},{9,1},... | collective-permute-start | bytes 393224 | tf_op jit(solution)/shard_map/ppermute | solution.py:439
  76.6 24.7 %collective-permute-start.25 = (bf16[512,128]{1,0:T(8,128)(2,1)S(1)}, bf16[512,128]{1,0:T(8,128)(2,1)S(1)}, u32[]{:S(2)}, u32[]{:S(2)}) collective-permute-start(bf16[512,128]{1,0:T(8,128)(2,1)S(1)} %get-tuple-element.82), channel_id=1, source_target_pairs={{0,16},{1,17},{2,18},{3,19},{4,20},{5,21},{6,22},{7,23},{8,24},{9,... | collective-permute-start | bytes 393224 | tf_op jit(solution)/shard_map/ppermute | solution.py:439
  76.8 24.4 %collective-permute-start.26 = (bf16[512,128]{1,0:T(8,128)(2,1)S(1)}, bf16[512,128]{1,0:T(8,128)(2,1)S(1)}, u32[]{:S(2)}, u32[]{:S(2)}) collective-permute-start(bf16[512,128]{1,0:T(8,128)(2,1)S(1)} %get-tuple-element.83), channel_id=1, source_target_pairs={{0,24},{1,25},{2,26},{3,27},{4,28},{5,29},{6,30},{7,31},{8,16},{9,... | collective-permute-start | bytes 393224 | tf_op jit(solution)/shard_map/ppermute | solution.py:439
  81.9 19.4 %collective-permute-start.27 = (bf16[16,512]{1,0:T(8,128)(2,1)S(1)}, bf16[16,512]{1,0:T(8,128)(2,1)S(1)}, u32[]{:S(2)}, u32[]{:S(2)}) collective-permute-start(bf16[16,512]{1,0:T(8,128)(2,1)S(1)} %get-tuple-element.84), channel_id=1, source_target_pairs={{0,1},{1,2},{2,3},{4,5},{5,6},{6,7},{8,9},{9,10},{10,11},{12,13},{... | collective-permute-start | bytes 49160 | tf_op jit(solution)/shard_map/ppermute | solution.py:563
  98.4 5.1 %collective-permute-start.28 = (bf16[16,512]{1,0:T(8,128)(2,1)S(1)}, bf16[16,512]{1,0:T(8,128)(2,1)S(1)}, u32[]{:S(2)}, u32[]{:S(2)}) collective-permute-start(bf16[16,512]{1,0:T(8,128)(2,1)S(1)} %get-tuple-element.85), channel_id=1, source_target_pairs={{1,0},{2,1},{3,2},{5,4},{6,5},{7,6},{9,8},{10,9},{11,10},{13,12},{... | collective-permute-start | bytes 49160 | tf_op jit(solution)/shard_map/ppermute | solution.py:563
  103.4 5.1 %copy-start.3 = (f32[128]{0:T(128)S(1)}, f32[128]{0:T(128)}, u32[]{:S(2)}) copy-start(f32[128]{0:T(128)} %param.13) | copy-start | bytes 1540
  103.4 5.1 %copy-start.4 = (f32[128]{0:T(128)S(1)}, f32[128]{0:T(128)}, u32[]{:S(2)}) copy-start(f32[128]{0:T(128)} %param.15) | copy-start | bytes 1540
  103.8 8.3 %collective-permute-start.29 = (bf16[2,80,512]{2,1,0:T(8,128)(2,1)S(1)}, bf16[2,80,512]{2,1,0:T(8,128)(2,1)S(1)}, u32[]{:S(2)}, u32[]{:S(2)}) collective-permute-start(bf16[2,80,512]{2,1,0:T(8,128)(2,1)S(1)} %get-tuple-element.88), channel_id=1, source_target_pairs={{0,4},{4,8},{8,12},{12,16},{16,20},{20,24},{24,28},{1,5},{5,9},{9,... | collective-permute-start | bytes 491528 | tf_op jit(solution)/shard_map/ppermute | solution.py:563
  107.2 7.3 %collective-permute-start.30 = (bf16[2,80,512]{2,1,0:T(8,128)(2,1)S(1)}, bf16[2,80,512]{2,1,0:T(8,128)(2,1)S(1)}, u32[]{:S(2)}, u32[]{:S(2)}) collective-permute-start(bf16[2,80,512]{2,1,0:T(8,128)(2,1)S(1)} %get-tuple-element.89), channel_id=1, source_target_pairs={{4,0},{8,4},{12,8},{16,12},{20,16},{24,20},{28,24},{5,1},{9,5},{13... | collective-permute-start | bytes 491528 | tf_op jit(solution)/shard_map/ppermute | solution.py:563

commit v2 on v1

--- a/solution.py
+++ b/solution.py
@@ -59,7 +59,7 @@
 def index_kernel(shape, slots, blocks, *refs):
     n_z, n_y, n_x, n_c = shape
     codes = refs[:n_c]
-    index_ref, label_ref, counts, labels = refs[n_c:]
+    index_ref, label_ref, label2_ref, counts, labels, labels2 = refs[n_c:]
     tiles = n_z * n_y * n_x * n_c
     groups = n_y * n_x
     spare = groups * n_z * slots
@@ -72,6 +72,7 @@
 
     def blank(s, carry):
         labels[s] = -1
+        labels2[s] = -1
         return carry
 
     lax.fori_loop(0, spare, blank, 0, unroll=8)
@@ -89,81 +90,94 @@
             rest, x_to = split_low(rest, n_x)
             z_to, y_to = split_low(rest, n_y)
             group = apart(y_to, y, n_y) * n_x + apart(x_to, x, n_x)
-            slot = (group * n_z + apart(z_to, z, n_z)) * slots + rank
-            slot = jnp.where(c_to == c, slot, spare)
+            step = apart(z_to, z, n_z)
+            slot = jnp.where(c_to == c, (group * n_z + step) * slots + rank, spare)
+            slot2 = jnp.where(c_to == c, (step * groups + group) * slots + rank, spare)
             index_ref[source * pairs + p] = slot
+            index_ref[(n_c + source) * pairs + p] = slot2
             labels[slot] = block
+            labels2[slot2] = block
             return carry
 
         lax.fori_loop(0, pairs, place, 0, unroll=4)
     lane = lax.broadcasted_iota(jnp.int32, (LABEL_ROWS, label_ref.shape[1]), 1)
-    for g in range(groups):
-        row = jnp.full(lane.shape, -1, jnp.int32)
-        for k in range(n_z * slots):
-            row = jnp.where(lane == k, labels[g * n_z * slots + k], row)
-        label_ref[g * LABEL_ROWS : (g + 1) * LABEL_ROWS, :] = row.astype(jnp.float32).astype(jnp.bfloat16)
-
-
-def contribute_kernel(n_c, groups, per_group, images, top, spans, first, *refs):
+    for source, target, outer in ((labels, label_ref, groups), (labels2, label2_ref, n_z)):
+        inner = spare // outer
+        for g in range(outer):
+            row = jnp.full(lane.shape, -1, jnp.int32)
+            for k in range(inner):
+                row = jnp.where(lane == k, source[g * inner + k], row)
+            target[g * LABEL_ROWS : (g + 1) * LABEL_ROWS, :] = row.astype(jnp.float32).astype(jnp.bfloat16)
+
+
+def contribute_kernel(n_c, outer, per_group, images, top, spans, base, direct, labelled, *refs):
     index_ref = refs[0]
     heads = refs[1 : 1 + n_c]
     refs = refs[1 + n_c :]
-    begin, rows = min(span[0] for span in spans), sum(span[1] for span in spans)
+    rows = sum(span[1] for span in spans)
     pairs = images * top
     size = heads[0].shape[1]
-    if first:
+    if labelled:
         label_ref, refs = refs[0], refs[1:]
-    else:
+    if not direct:
         sources, refs = refs[:n_c], refs[n_c:]
-    outs = refs[: groups * len(spans)]
-    refs = refs[groups * len(spans) :]
+    outs = refs[: outer * len(spans)]
+    refs = refs[outer * len(spans) :]
     buffers, refs = refs[: len(spans)], refs[len(spans) :]
     store_sems = refs[0]
-    if not first:
+    if not direct:
         held, load_sems = refs[1:]
-        loads = [
-            pltpu.make_async_copy(
-                sources[s].at[:, pl.ds(begin, rows), :], held.at[pl.ds(s * pairs, pairs)], load_sems.at[s]
-            )
-            for s in range(n_c)
-        ]
+        loads = []
+        for s in range(n_c):
+            at = 0
+            for i, (start, chunk) in enumerate(spans):
+                loads.append(
+                    pltpu.make_async_copy(
+                        sources[s].at[:, pl.ds(start, chunk), :],
+                        held.at[pl.ds(s * pairs, pairs), pl.ds(at, chunk)],
+                        load_sems.at[s * len(spans) + i],
+                    )
+                )
+                at += chunk
         for load in loads:
             load.start()
     for s in range(n_c):
-        if not first:
-            loads[s].wait()
-        base = heads[s].shape[0] - images * size
+        if not direct:
+            for load in loads[s * len(spans) : (s + 1) * len(spans)]:
+                load.wait()
+        pixel_base = heads[s].shape[0] - images * size
 
         def image(b, carry):
             p0 = s * pairs + b * top
-            if first:
+            if direct:
                 weights = heads[s][pl.ds(pl.multiple_of(b * top * rows, top * rows), top * rows), :]
             else:
                 weights = held[pl.ds(p0, top)].reshape(top * rows, size)
-            pixels = heads[s][pl.ds(pl.multiple_of(base + b * size, size), size), :]
+            pixels = heads[s][pl.ds(pl.multiple_of(pixel_base + b * size, size), size), :]
             product = jnp.dot(weights, pixels, preferred_element_type=jnp.float32)
             product = product.astype(jnp.bfloat16)
             for t in range(top):
-                slot = index_ref[p0 + t]
-                for (start, chunk), buffer in zip(spans, buffers):
-                    at = t * rows + start - begin
+                slot = index_ref[base + p0 + t]
+                at = t * rows
+                for (_, chunk), buffer in zip(spans, buffers):
                     buffer[pl.ds(pl.multiple_of(slot * chunk, chunk), chunk), :] = product[at : at + chunk]
+                    at += chunk
             return carry
 
         lax.fori_loop(0, images, image, 0, unroll=4)
     copies = []
     for i, ((_, chunk), buffer) in enumerate(zip(spans, buffers)):
         length = per_group * chunk
-        for g in range(groups):
-            n = i * groups + g
-            data = outs[n].at[pl.ds(0, length)] if first else outs[n]
+        for g in range(outer):
+            n = i * outer + g
+            data = outs[n].at[pl.ds(0, length)] if labelled else outs[n]
             copies.append(pltpu.make_async_copy(buffer.at[pl.ds(g * length, length)], data, store_sems.at[n]))
-            if first:
+            if labelled:
                 copies.append(
                     pltpu.make_async_copy(
                         label_ref.at[pl.ds(g * LABEL_ROWS, LABEL_ROWS)],
                         outs[n].at[pl.ds(length, LABEL_ROWS)],
-                        store_sems.at[groups * len(spans) + g],
+                        store_sems.at[outer * len(spans) + n],
                     )
                 )
     for copy in copies:
@@ -242,14 +256,14 @@
             ref[:, z * channels : (z + 1) * channels] = part
 
 
-def finish_kernel(n_z, spans, blocks, size, *refs):
-    count = n_z * len(spans)
-    parts = refs[:count]
-    left_ref, right_ref, _, out_ref, first_ref, last_ref, total = refs[count:]
-    for k, (start, chunk) in enumerate(spans):
+def finish_kernel(spans, counts, blocks, size, *refs):
+    left_ref, right_ref, _, out_ref, first_ref, last_ref, total = refs[sum(counts) :]
+    parts = 0
+    for (start, chunk), count in zip(spans, counts):
         for block in range(blocks):
             at = block * size + start
-            total[at : at + chunk, :] = sum_parts(parts[k * n_z : (k + 1) * n_z], block, chunk)
+            total[at : at + chunk, :] = sum_parts(refs[parts : parts + count], block, chunk)
+        parts += count
     cells = total.shape[0] // DEPTH
     channels = total.shape[1]
     for z in range(DEPTH):
@@ -422,8 +436,6 @@
     shape = (n_z, n_y, n_x, n_c)
     groups = n_y * n_x
     slots = n_c * capacity
-    per_group = n_z * slots
-    stride = per_group + 1
     quarter = size // 4
     spans = [(part * quarter, quarter) for part in ORDER]
 
@@ -440,101 +452,116 @@
 
     code = (target_tile * blocks + target_block).reshape(-1)
     weights = pair_weight[0].reshape(images * top, size, size)
-    begin, rows = spans[0]
+    turned = len(spans) - 1
+    begin, rows = spans[turned]
     head = jnp.concatenate(
         [weights[:, begin : begin + rows].reshape(-1, size), features[0].reshape(-1, channels)], axis=0
     )
     shared = [(code, head, weights)]
     for dc in range(1, n_c):
         shared.append(tuple(moved_by(v, dc=dc) for v in shared[0]))
-    index, labels = pl.pallas_call(
+    index, labels, labels_turned = pl.pallas_call(
         functools.partial(index_kernel, shape, slots, blocks),
         out_shape=(
-            jax.ShapeDtypeStruct((n_c * images * top,), jnp.int32),
+            jax.ShapeDtypeStruct((2 * n_c * images * top,), jnp.int32),
             jax.ShapeDtypeStruct((groups * LABEL_ROWS, channels), jnp.bfloat16),
+            jax.ShapeDtypeStruct((n_z * LABEL_ROWS, channels), jnp.bfloat16),
         ),
         in_specs=[smem()] * n_c,
-        out_specs=(smem(), vmem()),
-        scratch_shapes=[pltpu.SMEM((devices,), jnp.int32), pltpu.SMEM((groups * per_group + 1,), jnp.int32)],
+        out_specs=(smem(), vmem(), vmem()),
+        scratch_shapes=[pltpu.SMEM((devices,), jnp.int32)]
+        + [pltpu.SMEM((groups * n_z * slots + 1,), jnp.int32)] * 2,
         compiler_params=params(),
         name="index",
     )(*[v[0] for v in shared])
 
-    def contribute(ks):
+    def contribute(ks, marks):
         own = [spans[k] for k in ks]
-        first = ks[0] == 0
+        direct = ks == [turned]
+        outer = n_z if direct else groups
+        per = groups * n_z * slots // outer
         outs, scratch = [], []
         for _, chunk in own:
-            outs += arrays(groups, per_group * chunk + (LABEL_ROWS if first else 0), channels)
-            scratch.append(VMEM(((groups * per_group + 1) * chunk, channels), jnp.bfloat16))
-        rows = sum(chunk for _, chunk in own)
-        scratch.append(pltpu.SemaphoreType.DMA((len(outs) + groups,)))
+            outs += arrays(outer, per * chunk + (0 if marks is None else LABEL_ROWS), channels)
+            scratch.append(VMEM(((groups * n_z * slots + 1) * chunk, channels), jnp.bfloat16))
+        scratch.append(pltpu.SemaphoreType.DMA((2 * len(outs),)))
         in_specs = [smem()] + [vmem()] * n_c
         args = [index] + [v[1] for v in shared]
-        if first:
+        if marks is not None:
             in_specs.append(vmem())
-            args.append(labels)
-        else:
+            args.append(marks)
+        if not direct:
             in_specs += [anywhere()] * n_c
             args += [v[2] for v in shared]
             scratch += [
-                VMEM((n_c * images * top, rows, size), jnp.bfloat16),
-                pltpu.SemaphoreType.DMA((n_c,)),
+                VMEM((n_c * images * top, sum(chunk for _, chunk in own), size), jnp.bfloat16),
+                pltpu.SemaphoreType.DMA((n_c * len(own),)),
             ]
+        base = n_c * images * top if direct else 0
         made = pl.pallas_call(
-            functools.partial(contribute_kernel, n_c, groups, per_group, images, top, own, first),
+            functools.partial(
+                contribute_kernel, n_c, outer, per, images, top, own, base, direct, marks is not None
+            ),
             out_shape=tuple(outs),
             in_specs=in_specs,
             out_specs=(anywhere(),) * len(outs),
             scratch_shapes=scratch,
             compiler_params=params(),
         )(*args)
-        for i, k in enumerate(ks):
-            messages[k] = made[i * groups : (i + 1) * groups]
-
-    def exchange(k):
+        return [made[i * outer : (i + 1) * outer] for i in range(len(ks))]
+
+    def over_plane(values):
         return [
             moved_by(value, dy=g // n_x, dx=g % n_x) if g else value
-            for g, value in enumerate(messages[k])
+            for g, value in enumerate(values)
         ]
 
+    def over_depth(values):
+        return [moved_by(value, dz=dz) if dz else value for dz, value in enumerate(values)]
+
     def merge(k, received, plan):
-        first = k == 0
+        first = plan is None
+        outer = len(received)
+        inner = groups * n_z // outer
         chunk = spans[k][1]
-        outs = arrays(n_z, blocks * chunk, channels)
-        out_specs = [vmem()] * n_z
-        scratch = [VMEM((n_z * blocks * chunk, channels), jnp.float32)]
-        in_specs = [vmem()] * groups
+        outs = arrays(inner, blocks * chunk, channels)
+        out_specs = [vmem()] * inner
+        scratch = [VMEM((inner * blocks * chunk, channels), jnp.float32)]
+        in_specs = [vmem()] * outer
         args = tuple(received)
         if first:
-            outs.append(jax.ShapeDtypeStruct((stride * groups,), jnp.int32))
+            outs.append(jax.ShapeDtypeStruct(((inner * slots + 1) * outer,), jnp.int32))
             out_specs.append(smem())
             scratch += [
-                VMEM((groups, channels), jnp.int32),
-                pltpu.SMEM((groups, channels), jnp.int32),
+                VMEM((outer, channels), jnp.int32),
+                pltpu.SMEM((outer, channels), jnp.int32),
                 pltpu.SemaphoreType.DMA,
             ]
         else:
             in_specs.append(smem())
             args += (plan,)
-        return pl.pallas_call(
-            functools.partial(merge_kernel, n_z, groups, slots, chunk, blocks, first),
+        merged = pl.pallas_call(
+            functools.partial(merge_kernel, inner, outer, slots, chunk, blocks, first),
             out_shape=tuple(outs),
             in_specs=in_specs,
             out_specs=tuple(out_specs),
             scratch_shapes=scratch,
             compiler_params=params(),
         )(*args)
-
-    messages = {}
-    contribute([0])
-    contribute(list(range(1, len(spans))))
+        return merged[:inner], merged[-1]
+
+    (made,) = contribute([turned], labels_turned)
+    received = over_depth(made)
+    messages = contribute([0], labels)
+    messages += contribute(list(range(1, turned)), None)
     plan, final = None, []
-    for k in range(len(spans)):
-        merged = merge(k, exchange(k), plan)
-        if k == 0:
-            plan = merged[-1]
-        final += [moved_by(part, dz=dz) if dz else part for dz, part in enumerate(merged[:n_z])]
+    for k in range(turned):
+        merged, new_plan = merge(k, over_plane(messages[k]), plan)
+        plan = new_plan if plan is None else plan
+        final += over_depth(merged)
+    last_merged = merged[0]
+    merged, _ = merge(turned, received, None)
+    final += over_plane(merged)
     bands = jax.ShapeDtypeStruct((3, 2, 9 * channels, 2 * channels), jnp.bfloat16)
     band1, band2 = pl.pallas_call(
         band_kernel,
@@ -543,7 +570,7 @@
         out_specs=(vmem(), vmem()),
         compiler_params=params(),
         name="bands",
-    )(conv1_weight, conv2_weight, merged[0])
+    )(conv1_weight, conv2_weight, last_merged)
     cells = TX * TY
     lanes = DEPTH * channels
     halves = blocks // TX
@@ -556,7 +583,7 @@
         scratch_shapes=[VMEM((2, 2 * TX * DEPTH, channels), jnp.float32)],
         compiler_params=params(),
         name="tail",
-    )(*final[: 2 * n_z], final[(len(spans) - 1) * n_z])
+    )(*final[: 2 * n_z], last_merged)
 
     def moved(value, axis, count, step):
         pairs = [(i, i + step) for i in range(count) if 0 <= i + step < count]
@@ -567,7 +594,7 @@
     wide = 80
     packed = jax.ShapeDtypeStruct((2, wide, lanes), jnp.bfloat16)
     main, first_rows, last_rows = pl.pallas_call(
-        functools.partial(finish_kernel, n_z, spans, blocks, size),
+        functools.partial(finish_kernel, spans, [n_z] * turned + [groups], blocks, size),
         out_shape=(jax.ShapeDtypeStruct((cells, lanes), jnp.bfloat16), packed, packed),
         in_specs=[vmem()] * (len(final) + 2) + [anywhere()],
         out_specs=(vmem(),) * 3,

time: 119 us -> 117 us (0.983)
  waiting for transfers between devices: 44.9 us -> 26.7 us
  starting transfers between devices: 47 us -> 56.8 us
  Pallas kernels: 23.6 us -> 29.4 us
    ppermute x27, waiting for transfers between devices: 40.4 us -> 19.3 us  [moved_by(): return lax.ppermute(value, ('frames', 'rows'), pairs)]
    ppermute x27, starting transfers between devices: 23.9 us -> 40.9 us  [moved_by(): return lax.ppermute(value, ('frames', 'rows'), pairs)]
    ppermute x4, starting transfers between devices: 23.1 us -> 15.9 us  [moved(): return lax.ppermute(value, axis, pairs)]
    pallas_call x7 -> x8, Pallas kernels: 12.9 us -> 18.1 us  [the longest x3 9.92 us: contribute(): pl.pallas_call(functools.partial(contribute_kernel, n_c, outer, per, imag...]
    ppermute x4, waiting for transfers between devices: 4.47 us -> 7.37 us  [moved(): return lax.ppermute(value, axis, pairs)]
  transfers between devices with their start and end apart: 31 -> 31, of which waited for: 13 -> 9; matrix products, arithmetic and copies ran while one was open for 2% -> 2% of each run, Pallas kernels for 17% -> 22%
where the time goes in v2:
time: 117 us; the launch traced here: 116 us
  starting transfers between devices  56.8 us (49%)
  Pallas kernels  29.4 us (25%)
  waiting for transfers between devices  26.7 us (23%)
  local copies, waits for them, and re-layouts  1.29 us (1%)
  other arithmetic  1.26 us (1%)
    ppermute x27, starting transfers between devices, moved_by(): return lax.ppermute(value, ('frames', 'rows'), pairs)  40.9 us
    ppermute x27, waiting for transfers between devices, moved_by(): return lax.ppermute(value, ('frames', 'rows'), pairs)  19.3 us
    ppermute x4, starting transfers between devices, moved(): return lax.ppermute(value, axis, pairs)  15.9 us
    pallas_call x3, Pallas kernels, contribute(): pl.pallas_call(functools.partial(contribute_kernel, n_c, outer, per, imag...  9.92 us
    pallas_call x4, Pallas kernels, merge(): pl.pallas_call(functools.partial(merge_kernel, inner, outer, slots, chunk...  7.84 us
    ppermute x4, waiting for transfers between devices, moved(): return lax.ppermute(value, axis, pairs)  7.37 us
    pallas_call x1, Pallas kernels, shards(): pl.pallas_call(border_kernel, out_shape=jax.ShapeDtypeStruct((cells * DEP...  3.68 us
    pallas_call x1, Pallas kernels, shards(): pl.pallas_call(interior_kernel, out_shape=(jax.ShapeDtypeStruct(((TX - 4)...  3.61 us
  transfers between devices with their start and end apart: 31, of which 9 were waited for; matrix products, arithmetic and copies ran while one was open for 2% of the time, Pallas kernels for 22%

profile of v2, /device:TPU:1, one launch (start us, length us, event | category | flops | bytes accessed | tf_op | source)
XLA Modules:
  0.0 115.7 jit_solution(4458094916856352364)
XLA Ops:
  0.0 0.0 collective-permute-start.2
  0.0 1.1 slice.4
  1.1 0.0 copy-start
  1.1 1.3 %pad_maximum_fusion.refs_1_ = bf16[4096,128]{1,0:T(8,128)(2,1)S(1)} fusion(bf16[2048,128]{1,0:T(8,128)(2,1)} %bitcast.18, bf16[2048,128]{1,0:T(8,128)(2,1)S(1)} %bitcast.17), kind=kLoop, calls=%fused_computation | loop fusion | flops 2097152 | bytes 2097152 | tf_op jit(solution)/shard_map/concatenate | solution.py:457
  2.4 0.5 collective-permute-start.1
  3.0 0.1 copy.10
  3.0 0.1 reshape.12.refs_0_
  3.1 0.1 collective-permute-start
  3.2 2.8 %collective-permute-done.refs_1_ = s32[64]{0:T(128)S(1)} collective-permute-done((s32[64]{0:T(128)S(1)}, s32[64]{0:T(128)S(1)}, u32[]{:S(2)}, u32[]{:S(2)}) %collective-permute-start) | collective-permute-done | bytes 288 | tf_op jit(solution)/shard_map/ppermute | solution.py:451
  6.0 3.0 %index.1 = (s32[256]{0:T(256)S(1)}, bf16[64,128]{1,0:T(8,128)(2,1)S(1)}, bf16[64,128]{1,0:T(8,128)(2,1)S(1)}) custom-call(s32[64]{0:T(128)S(1)} %reshape.12.refs_0_, s32[64]{0:T(128)S(1)} %collective-permute-done.refs_1_), custom_call_target="tpu_custom_call" | custom-call | tf_op jit(solution)/shard_map/index/pallas_call | solution.py:463
  9.0 0.0 collective-permute-done.1.refs_2_
  9.0 2.8 %shard_map.87 = (bf16[1040,128]{1,0:T(8,128)(2,1)S(1)}, bf16[1040,128]{1,0:T(8,128)(2,1)S(1)}, bf16[1040,128]{1,0:T(8,128)(2,1)S(1)}, bf16[1040,128]{1,0:T(8,128)(2,1)S(1)}) custom-call(s32[256]{0:T(256)S(1)} %get-tuple-element.50.refs_0_, bf16[4096,128]{1,0:T(8,128)(2,1)S(1)} %pad_maximum_fusion.refs_1_, bf16[4096,128]{1,0:T(8,128)(2,1)} %collective-permute-done.1.refs_2_, ...), custom_call_target="tpu_custom_call" | custom-call | tf_op jit(solution)/shard_map/pallas_call | solution.py:501
  11.9 2.5 %collective-permute-start.21 = (bf16[1040,128]{1,0:T(8,128)(2,1)S(1)}, bf16[1040,128]{1,0:T(8,128)(2,1)S(1)}, u32[]{:S(2)}, u32[]{:S(2)}) collective-permute-start(bf16[1040,128]{1,0:T(8,128)(2,1)S(1)} %get-tuple-element.79), channel_id=1, source_target_pairs={{0,8},{1,9},{2,10},{3,11},{4,12},{5,13},{6,14},{7,15},{8,0},{9,1},... | collective-permute-start | bytes 798728 | tf_op jit(solution)/shard_map/ppermute | solution.py:451
  14.4 2.3 %collective-permute-start.22 = (bf16[1040,128]{1,0:T(8,128)(2,1)S(1)}, bf16[1040,128]{1,0:T(8,128)(2,1)S(1)}, u32[]{:S(2)}, u32[]{:S(2)}) collective-permute-start(bf16[1040,128]{1,0:T(8,128)(2,1)S(1)} %get-tuple-element.80), channel_id=1, source_target_pairs={{0,16},{1,17},{2,18},{3,19},{4,20},{5,21},{6,22},{7,23},{8,24},{9,... | collective-permute-start | bytes 798728 | tf_op jit(solution)/shard_map/ppermute | solution.py:451
  16.7 0.0 collective-permute-start.23
  16.7 0.0 collective-permute-done.2.refs_5_.refs_4_
  16.7 3.3 %shard_map.82 = (bf16[1040,128]{1,0:T(8,128)(2,1)S(1)}, bf16[1040,128]{1,0:T(8,128)(2,1)S(1)}, bf16[1040,128]{1,0:T(8,128)(2,1)S(1)}, bf16[1040,128]{1,0:T(8,128)(2,1)S(1)}) custom-call(s32[256]{0:T(256)S(1)} %get-tuple-element.50.refs_0_, bf16[4096,128]{1,0:T(8,128)(2,1)S(1)} %pad_maximum_fusion.refs_1_, bf16[4096,128]{1,0:T(8,128)(2,1)} %collective-permute-done.1.refs_2_, ...), custom_call_target="tpu_custom_call" | custom-call | tf_op jit(solution)/shard_map/pallas_call | solution.py:501
  20.0 1.3 %collective-permute-start.3 = (bf16[1040,128]{1,0:T(8,128)(2,1)S(1)}, bf16[1040,128]{1,0:T(8,128)(2,1)S(1)}, u32[]{:S(2)}, u32[]{:S(2)}) collective-permute-start(bf16[1040,128]{1,0:T(8,128)(2,1)S(1)} %get-tuple-element.53), channel_id=1, source_target_pairs={{0,2},{1,3},{2,0},{3,1},{4,6},{5,7},{6,4},{7,5},{8,10},{9,11},{10,... | collective-permute-start | bytes 798728 | tf_op jit(solution)/shard_map/ppermute | solution.py:451
  21.2 3.8 %shard_map.84 = (bf16[1024,128]{1,0:T(8,128)(2,1)S(1)}, bf16[1024,128]{1,0:T(8,128)(2,1)S(1)}, bf16[1024,128]{1,0:T(8,128)(2,1)S(1)}, bf16[1024,128]{1,0:T(8,128...) custom-call(s32[256]{0:T(256)S(1)} %get-tuple-element.50.refs_0_, ...), custom_call_target="tpu_custom_call" | custom-call | tf_op jit(solution)/shard_map/pallas_call | solution.py:501
  25.1 0.3 collective-permute-start.9
  25.4 0.5 collective-permute-done.21.refs_1_
  25.9 1.1 collective-permute-start.4
  27.0 0.0 collective-permute-done.22.refs_2_
  27.0 1.2 %collective-permute-start.5 = (bf16[1040,128]{1,0:T(8,128)(2,1)S(1)}, bf16[1040,128]{1,0:T(8,128)(2,1)S(1)}, u32[]{:S(2)}, u32[]{:S(2)}) collective-permute-start(bf16[1040,128]{1,0:T(8,128)(2,1)S(1)} %get-tuple-element.55), channel_id=1, source_target_pairs={{0,6},{1,7},{2,4},{3,5},{4,2},{5,3},{6,0},{7,1},{8,14},{9,15},{10,... | collective-permute-start | bytes 798728 | tf_op jit(solution)/shard_map/ppermute | solution.py:451
  28.2 6.0 %collective-permute-done.23.refs_3_ = bf16[1040,128]{1,0:T(8,128)(2,1)S(1)} collective-permute-done((bf16[1040,128]{1,0:T(8,128)(2,1)S(1)}, bf16[1040,128]{1,0:T(8,128)(2,1)S(1)}, u32[]{:S(2)}, u32[]{:S(2)}) %collective-permute-start.23) | collective-permute-done | bytes 266272 | tf_op jit(solution)/shard_map/ppermute | solution.py:451
  34.1 2.4 %shard_map.88 = (bf16[512,128]{1,0:T(8,128)(2,1)S(1)}, bf16[512,128]{1,0:T(8,128)(2,1)S(1)}, bf16[512,128]{1,0:T(8,128)(2,1)S(1)}, bf16[512,128]{1,0:T(8,128)(2,1)S(1)}, s32[132]{0:T(256)}) custom-call(bf16[1040,128]{1,0:T(8,128)(2,1)S(1)} %get-tuple-element.78.refs_0_, bf16[1040,128]{1,0:T(8,128)(2,1)S(1)} %collective-permute-done.21.refs_1_, ...), custom_call_target="tpu_custom_call" | custom-call | tf_op jit(solution)/shard_map/pallas_call | solution.py:543
  36.6 1.3 %collective-permute-start.24 = (bf16[512,128]{1,0:T(8,128)(2,1)S(1)}, bf16[512,128]{1,0:T(8,128)(2,1)S(1)}, u32[]{:S(2)}, u32[]{:S(2)}) collective-permute-start(bf16[512,128]{1,0:T(8,128)(2,1)S(1)} %get-tuple-element.83), channel_id=1, source_target_pairs={{0,2},{1,3},{2,0},{3,1},{4,6},{5,7},{6,4},{7,5},{8,10},{9,11},{10,... | collective-permute-start | bytes 393224 | tf_op jit(solution)/shard_map/ppermute | solution.py:451
  37.8 2.9 %collective-permute-done.24.refs_13_ = bf16[512,128]{1,0:T(8,128)(2,1)S(1)} collective-permute-done((bf16[512,128]{1,0:T(8,128)(2,1)S(1)}, bf16[512,128]{1,0:T(8,128)(2,1)S(1)}, u32[]{:S(2)}, u32[]{:S(2)}) %collective-permute-start.24) | collective-permute-done | bytes 131104 | tf_op jit(solution)/shard_map/ppermute | solution.py:451
  40.8 2.3 %collective-permute-start.10 = (bf16[1024,128]{1,0:T(8,128)(2,1)S(1)}, bf16[1024,128]{1,0:T(8,128)(2,1)S(1)}, u32[]{:S(2)}, u32[]{:S(2)}) collective-permute-start(bf16[1024,128]{1,0:T(8,128)(2,1)S(1)} %get-tuple-element.62), channel_id=1, source_target_pairs={{0,4},{1,5},{2,6},{3,7},{4,0},{5,1},{6,2},{7,3},{8,12},{9,13},{10,... | collective-permute-start | bytes 786440 | tf_op jit(solution)/shard_map/ppermute | solution.py:451
  43.0 0.9 collective-permute-start.11
  43.9 0.3 collective-permute-start.15
  44.3 1.4 %collective-permute-start.16 = (bf16[1024,128]{1,0:T(8,128)(2,1)S(1)}, bf16[1024,128]{1,0:T(8,128)(2,1)S(1)}, u32[]{:S(2)}, u32[]{:S(2)}) collective-permute-start(bf16[1024,128]{1,0:T(8,128)(2,1)S(1)} %get-tuple-element.71), channel_id=1, source_target_pairs={{0,4},{1,5},{2,6},{3,7},{4,0},{5,1},{6,2},{7,3},{8,12},{9,13},{10,... | collective-permute-start | bytes 786440 | tf_op jit(solution)/shard_map/ppermute | solution.py:451
  45.7 0.0 collective-permute-done.5.refs_3_
  45.7 1.0 collective-permute-start.17
  46.7 2.6 %shard_map.83 = (bf16[512,128]{1,0:T(8,128)(2,1)S(1)}, bf16[512,128]{1,0:T(8,128)(2,1)S(1)}, bf16[512,128]{1,0:T(8,128)(2,1)S(1)}, bf16[512,128]{1,0:T(8,128)(2,1)S(1)}, s32[132]{0:T(256)S(1)}) custom-call(bf16[1040,128]{1,0:T(8,128)(2,1)S(1)} %get-tuple-element.52.refs_0_, bf16[1040,128]{1,0:T(8,128)(2,1)S(1)} %collective-permute-done.3.refs_1_, ...), custom_call_target="tpu_custom_call" | custom-call | tf_op jit(solution)/shard_map/pallas_call | solution.py:543
  49.3 0.9 collective-permute-done.10.refs_2_
  50.2 8.4 %collective-permute-start.6 = (bf16[512,128]{1,0:T(8,128)(2,1)S(1)}, bf16[512,128]{1,0:T(8,128)(2,1)S(1)}, u32[]{:S(2)}, u32[]{:S(2)}) collective-permute-start(bf16[512,128]{1,0:T(8,128)(2,1)S(1)} %get-tuple-element.57), channel_id=1, source_target_pairs={{0,8},{1,9},{2,10},{3,11},{4,12},{5,13},{6,14},{7,15},{8,0},{9,1},... | collective-permute-start | bytes 393224 | tf_op jit(solution)/shard_map/ppermute | solution.py:451
  58.6 0.0 collective-permute-done.11.refs_3_
  58.6 1.6 %collective-permute-start.7 = (bf16[512,128]{1,0:T(8,128)(2,1)S(1)}, bf16[512,128]{1,0:T(8,128)(2,1)S(1)}, u32[]{:S(2)}, u32[]{:S(2)}) collective-permute-start(bf16[512,128]{1,0:T(8,128)(2,1)S(1)} %get-tuple-element.58), channel_id=1, source_target_pairs={{0,16},{1,17},{2,18},{3,19},{4,20},{5,21},{6,22},{7,23},{8,24},{9,... | collective-permute-start | bytes 393224 | tf_op jit(solution)/shard_map/ppermute | solution.py:451
  60.2 0.0 collective-permute-done.15.refs_1_
  60.2 0.4 collective-permute-start.8
  60.7 1.4 %shard_map.85 = (bf16[512,128]{1,0:T(8,128)(2,1)S(1)}, bf16[512,128]{1,0:T(8,128)(2,1)S(1)}, bf16[512,128]{1,0:T(8,128)(2,1)S(1)}, bf16[512,128]{1,0:T(8,128)(2,1)S(1)}) custom-call(bf16[1024,128]{1,0:T(8,128)(2,1)S(1)} %get-tuple-element.60.refs_0_, bf16[1024,128]{1,0:T(8,128)(2,1)S(1)} %collective-permute-done.9.refs_1_, ...), custom_call_target="tpu_custom_call" | custom-call | tf_op jit(solution)/shard_map/pallas_call | solution.py:543
  62.1 2.1 %collective-permute-done.16.refs_2_ = bf16[1024,128]{1,0:T(8,128)(2,1)S(1)} collective-permute-done((bf16[1024,128]{1,0:T(8,128)(2,1)S(1)}, bf16[1024,128]{1,0:T(8,128)(2,1)S(1)}, u32[]{:S(2)}, u32[]{:S(2)}) %collective-permute-start.16) | collective-permute-done | bytes 262176 | tf_op jit(solution)/shard_map/ppermute | solution.py:451
  64.2 5.2 %collective-permute-start.12 = (bf16[512,128]{1,0:T(8,128)(2,1)S(1)}, bf16[512,128]{1,0:T(8,128)(2,1)S(1)}, u32[]{:S(2)}, u32[]{:S(2)}) collective-permute-start(bf16[512,128]{1,0:T(8,128)(2,1)S(1)} %get-tuple-element.66), channel_id=1, source_target_pairs={{0,8},{1,9},{2,10},{3,11},{4,12},{5,13},{6,14},{7,15},{8,0},{9,1},... | collective-permute-start | bytes 393224 | tf_op jit(solution)/shard_map/ppermute | solution.py:451
  69.4 0.0 collective-permute-done.17.refs_3_
  69.4 1.4 %collective-permute-start.13 = (bf16[512,128]{1,0:T(8,128)(2,1)S(1)}, bf16[512,128]{1,0:T(8,128)(2,1)S(1)}, u32[]{:S(2)}, u32[]{:S(2)}) collective-permute-start(bf16[512,128]{1,0:T(8,128)(2,1)S(1)} %get-tuple-element.67), channel_id=1, source_target_pairs={{0,16},{1,17},{2,18},{3,19},{4,20},{5,21},{6,22},{7,23},{8,24},{9,... | collective-permute-start | bytes 393224 | tf_op jit(solution)/shard_map/ppermute | solution.py:451
  70.8 0.0 collective-permute-done.6.refs_1_
  70.8 0.9 collective-permute-start.14
  71.7 2.2 %collective-permute-start.25 = (bf16[512,128]{1,0:T(8,128)(2,1)S(1)}, bf16[512,128]{1,0:T(8,128)(2,1)S(1)}, u32[]{:S(2)}, u32[]{:S(2)}) collective-permute-start(bf16[512,128]{1,0:T(8,128)(2,1)S(1)} %get-tuple-element.84), channel_id=1, source_target_pairs={{0,4},{1,5},{2,6},{3,7},{4,0},{5,1},{6,2},{7,3},{8,12},{9,13},{10,... | collective-permute-start | bytes 393224 | tf_op jit(solution)/shard_map/ppermute | solution.py:451
  73.9 1.0 collective-permute-start.26
  74.9 1.4 %shard_map.86 = (bf16[512,128]{1,0:T(8,128)(2,1)S(1)}, bf16[512,128]{1,0:T(8,128)(2,1)S(1)}, bf16[512,128]{1,0:T(8,128)(2,1)S(1)}, bf16[512,128]{1,0:T(8,128)(2,1)S(1)}) custom-call(bf16[1024,128]{1,0:T(8,128)(2,1)S(1)} %get-tuple-element.69.refs_0_, bf16[1024,128]{1,0:T(8,128)(2,1)S(1)} %collective-permute-done.15.refs_1_, ...), custom_call_target="tpu_custom_call" | custom-call | tf_op jit(solution)/shard_map/pallas_call | solution.py:543
  76.3 0.5 collective-permute-start.18
  76.8 4.1 %collective-permute-done.13.refs_6_ = bf16[512,128]{1,0:T(8,128)(2,1)S(1)} collective-permute-done((bf16[512,128]{1,0:T(8,128)(2,1)S(1)}, bf16[512,128]{1,0:T(8,128)(2,1)S(1)}, u32[]{:S(2)}, u32[]{:S(2)}) %collective-permute-start.13) | collective-permute-done | bytes 131104 | tf_op jit(solution)/shard_map/ppermute | solution.py:451
  80.9 2.8 %collective-permute-start.20 = (bf16[512,128]{1,0:T(8,128)(2,1)S(1)}, bf16[512,128]{1,0:T(8,128)(2,1)S(1)}, u32[]{:S(2)}, u32[]{:S(2)}) collective-permute-start(bf16[512,128]{1,0:T(8,128)(2,1)S(1)} %get-tuple-element.76), channel_id=1, source_target_pairs={{0,24},{1,25},{2,26},{3,27},{4,28},{5,29},{6,30},{7,31},{8,16},{9,... | collective-permute-start | bytes 393224 | tf_op jit(solution)/shard_map/ppermute | solution.py:451
  83.7 11.4 %collective-permute-start.27 = (bf16[16,512]{1,0:T(8,128)(2,1)S(1)}, bf16[16,512]{1,0:T(8,128)(2,1)S(1)}, u32[]{:S(2)}, u32[]{:S(2)}) collective-permute-start(bf16[16,512]{1,0:T(8,128)(2,1)S(1)} %get-tuple-element.86), channel_id=1, source_target_pairs={{0,1},{1,2},{2,3},{4,5},{5,6},{6,7},{8,9},{9,10},{10,11},{12,13},{... | collective-permute-start | bytes 49160 | tf_op jit(solution)/shard_map/ppermute | solution.py:590
  95.2 1.9 %collective-permute-start.28 = (bf16[16,512]{1,0:T(8,128)(2,1)S(1)}, bf16[16,512]{1,0:T(8,128)(2,1)S(1)}, u32[]{:S(2)}, u32[]{:S(2)}) collective-permute-start(bf16[16,512]{1,0:T(8,128)(2,1)S(1)} %get-tuple-element.87), channel_id=1, source_target_pairs={{1,0},{2,1},{3,2},{5,4},{6,5},{7,6},{9,8},{10,9},{11,10},{13,12},{... | collective-permute-start | bytes 49160 | tf_op jit(solution)/shard_map/ppermute | solution.py:590
  97.1 0.9 bands.1
  98.1 2.1 %collective-permute-done.28.refs_17_.right_ref = bf16[16,512]{1,0:T(8,128)(2,1)S(1)} collective-permute-done((bf16[16,512]{1,0:T(8,128)(2,1)S(1)}, bf16[16,512]{1,0:T(8,128)(2,1)S(1)}, u32[]{:S(2)}, u32[]{:S(2)}) %collective-permute-start.28) | collective-permute-done | bytes 16416 | tf_op jit(solution)/shard_map/ppermute | solution.py:590
  100.2 0.4 finish.1
  100.6 1.3 %collective-permute-start.29 = (bf16[2,80,512]{2,1,0:T(8,128)(2,1)S(1)}, bf16[2,80,512]{2,1,0:T(8,128)(2,1)S(1)}, u32[]{:S(2)}, u32[]{:S(2)}) collective-permute-start(bf16[2,80,512]{2,1,0:T(8,128)(2,1)S(1)} %get-tuple-element.90), channel_id=1, source_target_pairs={{0,4},{4,8},{8,12},{12,16},{16,20},{20,24},{24,28},{1,5},{5,9},{9,... | collective-permute-start | bytes 491528 | tf_op jit(solution)/shard_map/ppermute | solution.py:590
  101.9 1.3 %collective-permute-start.30 = (bf16[2,80,512]{2,1,0:T(8,128)(2,1)S(1)}, bf16[2,80,512]{2,1,0:T(8,128)(2,1)S(1)}, u32[]{:S(2)}, u32[]{:S(2)}) collective-permute-start(bf16[2,80,512]{2,1,0:T(8,128)(2,1)S(1)} %get-tuple-element.91), channel_id=1, source_target_pairs={{4,0},{8,4},{12,8},{16,12},{20,16},{24,20},{28,24},{5,1},{9,5},{13... | collective-permute-start | bytes 491528 | tf_op jit(solution)/shard_map/ppermute | solution.py:590
  103.2 3.6 %interior.1 = (bf16[1024,128]{1,0:T(8,128)(2,1)S(1)}, bf16[4,80,512]{2,1,0:T(8,128)(2,1)S(1)}) custom-call(bf16[8,64,512]{2,1,0:T(8,128)(2,1)S(1)} %bitcast.11, bf16[16,512]{1,0:T(8,128)(2,1)S(1)} %collective-permute-done.27.refs_16_.left_ref, bf16[16,512]{1,0:T(8,128)(2,1)S(1)} %collective-permute-done.28.refs_17_.right_ref, ...), custom_call_target="tpu_custom_call" | custom-call | tf_op jit(solution)/shard_map/interior/pallas_call | solution.py:618
  106.8 5.2 %collective-permute-done.30.high_ref = bf16[2,80,512]{2,1,0:T(8,128)(2,1)S(1)} collective-permute-done((bf16[2,80,512]{2,1,0:T(8,128)(2,1)S(1)}, bf16[2,80,512]{2,1,0:T(8,128)(2,1)S(1)}, u32[]{:S(2)}, u32[]{:S(2)}) %collective-permute-start.30) | collective-permute-done | bytes 163872 | tf_op jit(solution)/shard_map/ppermute | solution.py:590
  112.0 3.7 %border.1 = bf16[2048,128]{1,0:T(8,128)(2,1)} custom-call(bf16[8,64,512]{2,1,0:T(8,128)(2,1)S(1)} %bitcast.12, bf16[2,80,512]{2,1,0:T(8,128)(2,1)S(1)} %collective-permute-done.29.low_ref, bf16[2,80,512]{2,1,0:T(8,128)(2,1)S(1)} %collective-permute-done.30.high_ref, bf16[16,512]{1,0:T(8,128)(2,1)S(1)} %collective-permute-done.27.refs_16_.left_ref, ...), custom_call_target="tpu_custom_call" | custom-call | tf_op jit(solution)/shard_map/border/pallas_call | solution.py:630
  (30 shorter events, 0.1 us)
Async XLA Ops:
  0.0 2.9 %copy-start.5 = (s32[1,16,4]{1,2,0:T(4,128)S(1)}, s32[1,16,4]{1,2,0:T(4,128)}, u32[]{:S(2)}) copy-start(s32[1,16,4]{1,2,0:T(4,128)} %param.11) | copy-start | bytes 772
  0.0 2.9 %copy-start.6 = (s32[1,16,4]{1,2,0:T(4,128)S(1)}, s32[1,16,4]{1,2,0:T(4,128)}, u32[]{:S(2)}) copy-start(s32[1,16,4]{1,2,0:T(4,128)} %param.10) | copy-start | bytes 772
  0.0 16.7 %collective-permute-start.2 = (bf16[64,128,128]{2,1,0:T(8,128)(2,1)}, bf16[64,128,128]{2,1,0:T(8,128)(2,1)}, u32[]{:S(2)}, u32[]{:S(2)}) collective-permute-start(bf16[64,128,128]{2,1,0:T(8,128)(2,1)} %bitcast.7), channel_id=1, source_target_pairs={{0,1},{1,0},{2,3},{3,2},{4,5},{5,4},{6,7},{7,6},{8,9},{9,8},{10,11... | collective-permute-start | bytes 6291464 | tf_op jit(solution)/shard_map/ppermute | solution.py:451
  1.1 15.6 %copy-start = (bf16[1,16,4,128,128]{4,3,2,1,0:T(8,128)(2,1)S(1)}, bf16[1,16,4,128,128]{4,3,2,1,0:T(8,128)(2,1)}, u32[]{:S(2)}) copy-start(bf16[1,16,4,128,128]{4,3,2,1,0:T(8,128)(2,1)} %param.9) | copy-start | bytes 6291460
  2.4 6.6 %collective-permute-start.1 = (bf16[4096,128]{1,0:T(8,128)(2,1)S(1)}, bf16[4096,128]{1,0:T(8,128)(2,1)}, u32[]{:S(2)}, u32[]{:S(2)}) collective-permute-start(bf16[4096,128]{1,0:T(8,128)(2,1)S(1)} %pad_maximum_fusion.refs_1_), channel_id=1, source_target_pairs={{0,1},{1,0},{2,3},{3,2},{4,5},{5,4},{6,7},{7,6},{8,9},{9,8},{10,11... | collective-permute-start | bytes 3145736 | tf_op jit(solution)/shard_map/ppermute | solution.py:451
  3.1 2.9 %collective-permute-start = (s32[64]{0:T(128)S(1)}, s32[64]{0:T(128)S(1)}, u32[]{:S(2)}, u32[]{:S(2)}) collective-permute-start(s32[64]{0:T(128)S(1)} %reshape.12.refs_0_), channel_id=1, source_target_pairs={{0,1},{1,0},{2,3},{3,2},{4,5},{5,4},{6,7},{7,6},{8,9},{9,8},{10,11... | collective-permute-start | bytes 776 | tf_op jit(solution)/shard_map/ppermute | solution.py:451
  11.9 14.0 %collective-permute-start.21 = (bf16[1040,128]{1,0:T(8,128)(2,1)S(1)}, bf16[1040,128]{1,0:T(8,128)(2,1)S(1)}, u32[]{:S(2)}, u32[]{:S(2)}) collective-permute-start(bf16[1040,128]{1,0:T(8,128)(2,1)S(1)} %get-tuple-element.79), channel_id=1, source_target_pairs={{0,8},{1,9},{2,10},{3,11},{4,12},{5,13},{6,14},{7,15},{8,0},{9,1},... | collective-permute-start | bytes 798728 | tf_op jit(solution)/shard_map/ppermute | solution.py:451
  14.4 12.6 %collective-permute-start.22 = (bf16[1040,128]{1,0:T(8,128)(2,1)S(1)}, bf16[1040,128]{1,0:T(8,128)(2,1)S(1)}, u32[]{:S(2)}, u32[]{:S(2)}) collective-permute-start(bf16[1040,128]{1,0:T(8,128)(2,1)S(1)} %get-tuple-element.80), channel_id=1, source_target_pairs={{0,16},{1,17},{2,18},{3,19},{4,20},{5,21},{6,22},{7,23},{8,24},{9,... | collective-permute-start | bytes 798728 | tf_op jit(solution)/shard_map/ppermute | solution.py:451
  16.7 17.5 %collective-permute-start.23 = (bf16[1040,128]{1,0:T(8,128)(2,1)S(1)}, bf16[1040,128]{1,0:T(8,128)(2,1)S(1)}, u32[]{:S(2)}, u32[]{:S(2)}) collective-permute-start(bf16[1040,128]{1,0:T(8,128)(2,1)S(1)} %get-tuple-element.81), channel_id=1, source_target_pairs={{0,24},{1,25},{2,26},{3,27},{4,28},{5,29},{6,30},{7,31},{8,16},{9,... | collective-permute-start | bytes 798728 | tf_op jit(solution)/shard_map/ppermute | solution.py:451
  20.0 24.0 %collective-permute-start.3 = (bf16[1040,128]{1,0:T(8,128)(2,1)S(1)}, bf16[1040,128]{1,0:T(8,128)(2,1)S(1)}, u32[]{:S(2)}, u32[]{:S(2)}) collective-permute-start(bf16[1040,128]{1,0:T(8,128)(2,1)S(1)} %get-tuple-element.53), channel_id=1, source_target_pairs={{0,2},{1,3},{2,0},{3,1},{4,6},{5,7},{6,4},{7,5},{8,10},{9,11},{10,... | collective-permute-start | bytes 798728 | tf_op jit(solution)/shard_map/ppermute | solution.py:451
  25.1 17.9 %collective-permute-start.9 = (bf16[1024,128]{1,0:T(8,128)(2,1)S(1)}, bf16[1024,128]{1,0:T(8,128)(2,1)S(1)}, u32[]{:S(2)}, u32[]{:S(2)}) collective-permute-start(bf16[1024,128]{1,0:T(8,128)(2,1)S(1)} %get-tuple-element.61), channel_id=1, source_target_pairs={{0,2},{1,3},{2,0},{3,1},{4,6},{5,7},{6,4},{7,5},{8,10},{9,11},{10,... | collective-permute-start | bytes 786440 | tf_op jit(solution)/shard_map/ppermute | solution.py:451
  25.9 18.4 %collective-permute-start.4 = (bf16[1040,128]{1,0:T(8,128)(2,1)S(1)}, bf16[1040,128]{1,0:T(8,128)(2,1)S(1)}, u32[]{:S(2)}, u32[]{:S(2)}) collective-permute-start(bf16[1040,128]{1,0:T(8,128)(2,1)S(1)} %get-tuple-element.54), channel_id=1, source_target_pairs={{0,4},{1,5},{2,6},{3,7},{4,0},{5,1},{6,2},{7,3},{8,12},{9,13},{10,... | collective-permute-start | bytes 798728 | tf_op jit(solution)/shard_map/ppermute | solution.py:451
  27.0 18.7 %collective-permute-start.5 = (bf16[1040,128]{1,0:T(8,128)(2,1)S(1)}, bf16[1040,128]{1,0:T(8,128)(2,1)S(1)}, u32[]{:S(2)}, u32[]{:S(2)}) collective-permute-start(bf16[1040,128]{1,0:T(8,128)(2,1)S(1)} %get-tuple-element.55), channel_id=1, source_target_pairs={{0,6},{1,7},{2,4},{3,5},{4,2},{5,3},{6,0},{7,1},{8,14},{9,15},{10,... | collective-permute-start | bytes 798728 | tf_op jit(solution)/shard_map/ppermute | solution.py:451
  36.6 4.2 %collective-permute-start.24 = (bf16[512,128]{1,0:T(8,128)(2,1)S(1)}, bf16[512,128]{1,0:T(8,128)(2,1)S(1)}, u32[]{:S(2)}, u32[]{:S(2)}) collective-permute-start(bf16[512,128]{1,0:T(8,128)(2,1)S(1)} %get-tuple-element.83), channel_id=1, source_target_pairs={{0,2},{1,3},{2,0},{3,1},{4,6},{5,7},{6,4},{7,5},{8,10},{9,11},{10,... | collective-permute-start | bytes 393224 | tf_op jit(solution)/shard_map/ppermute | solution.py:451
  40.8 9.4 %collective-permute-start.10 = (bf16[1024,128]{1,0:T(8,128)(2,1)S(1)}, bf16[1024,128]{1,0:T(8,128)(2,1)S(1)}, u32[]{:S(2)}, u32[]{:S(2)}) collective-permute-start(bf16[1024,128]{1,0:T(8,128)(2,1)S(1)} %get-tuple-element.62), channel_id=1, source_target_pairs={{0,4},{1,5},{2,6},{3,7},{4,0},{5,1},{6,2},{7,3},{8,12},{9,13},{10,... | collective-permute-start | bytes 786440 | tf_op jit(solution)/shard_map/ppermute | solution.py:451
  43.0 15.6 %collective-permute-start.11 = (bf16[1024,128]{1,0:T(8,128)(2,1)S(1)}, bf16[1024,128]{1,0:T(8,128)(2,1)S(1)}, u32[]{:S(2)}, u32[]{:S(2)}) collective-permute-start(bf16[1024,128]{1,0:T(8,128)(2,1)S(1)} %get-tuple-element.63), channel_id=1, source_target_pairs={{0,6},{1,7},{2,4},{3,5},{4,2},{5,3},{6,0},{7,1},{8,14},{9,15},{10,... | collective-permute-start | bytes 786440 | tf_op jit(solution)/shard_map/ppermute | solution.py:451
  43.9 16.3 %collective-permute-start.15 = (bf16[1024,128]{1,0:T(8,128)(2,1)S(1)}, bf16[1024,128]{1,0:T(8,128)(2,1)S(1)}, u32[]{:S(2)}, u32[]{:S(2)}) collective-permute-start(bf16[1024,128]{1,0:T(8,128)(2,1)S(1)} %get-tuple-element.70), channel_id=1, source_target_pairs={{0,2},{1,3},{2,0},{3,1},{4,6},{5,7},{6,4},{7,5},{8,10},{9,11},{10,... | collective-permute-start | bytes 786440 | tf_op jit(solution)/shard_map/ppermute | solution.py:451
  44.3 19.9 %collective-permute-start.16 = (bf16[1024,128]{1,0:T(8,128)(2,1)S(1)}, bf16[1024,128]{1,0:T(8,128)(2,1)S(1)}, u32[]{:S(2)}, u32[]{:S(2)}) collective-permute-start(bf16[1024,128]{1,0:T(8,128)(2,1)S(1)} %get-tuple-element.71), channel_id=1, source_target_pairs={{0,4},{1,5},{2,6},{3,7},{4,0},{5,1},{6,2},{7,3},{8,12},{9,13},{10,... | collective-permute-start | bytes 786440 | tf_op jit(solution)/shard_map/ppermute | solution.py:451
  45.7 23.8 %collective-permute-start.17 = (bf16[1024,128]{1,0:T(8,128)(2,1)S(1)}, bf16[1024,128]{1,0:T(8,128)(2,1)S(1)}, u32[]{:S(2)}, u32[]{:S(2)}) collective-permute-start(bf16[1024,128]{1,0:T(8,128)(2,1)S(1)} %get-tuple-element.72), channel_id=1, source_target_pairs={{0,6},{1,7},{2,4},{3,5},{4,2},{5,3},{6,0},{7,1},{8,14},{9,15},{10,... | collective-permute-start | bytes 786440 | tf_op jit(solution)/shard_map/ppermute | solution.py:451
  46.6 50.4 %copy-start.1 = (bf16[3,3,3,128,128]{4,3,2,1,0:T(8,128)(2,1)S(1)}, bf16[3,3,3,128,128]{4,3,2,1,0:T(8,128)(2,1)}, u32[]{:S(2)}) copy-start(bf16[3,3,3,128,128]{4,3,2,1,0:T(8,128)(2,1)} %first_ref.1) | copy-start | bytes 2654212
  46.6 50.4 %copy-start.2 = (bf16[3,3,3,128,128]{4,3,2,1,0:T(8,128)(2,1)S(1)}, bf16[3,3,3,128,128]{4,3,2,1,0:T(8,128)(2,1)}, u32[]{:S(2)}) copy-start(bf16[3,3,3,128,128]{4,3,2,1,0:T(8,128)(2,1)} %second_ref.1) | copy-start | bytes 2654212
  50.2 20.6 %collective-permute-start.6 = (bf16[512,128]{1,0:T(8,128)(2,1)S(1)}, bf16[512,128]{1,0:T(8,128)(2,1)S(1)}, u32[]{:S(2)}, u32[]{:S(2)}) collective-permute-start(bf16[512,128]{1,0:T(8,128)(2,1)S(1)} %get-tuple-element.57), channel_id=1, source_target_pairs={{0,8},{1,9},{2,10},{3,11},{4,12},{5,13},{6,14},{7,15},{8,0},{9,1},... | collective-permute-start | bytes 393224 | tf_op jit(solution)/shard_map/ppermute | solution.py:451
  58.6 13.1 %collective-permute-start.7 = (bf16[512,128]{1,0:T(8,128)(2,1)S(1)}, bf16[512,128]{1,0:T(8,128)(2,1)S(1)}, u32[]{:S(2)}, u32[]{:S(2)}) collective-permute-start(bf16[512,128]{1,0:T(8,128)(2,1)S(1)} %get-tuple-element.58), channel_id=1, source_target_pairs={{0,16},{1,17},{2,18},{3,19},{4,20},{5,21},{6,22},{7,23},{8,24},{9,... | collective-permute-start | bytes 393224 | tf_op jit(solution)/shard_map/ppermute | solution.py:451
  60.2 13.7 %collective-permute-start.8 = (bf16[512,128]{1,0:T(8,128)(2,1)S(1)}, bf16[512,128]{1,0:T(8,128)(2,1)S(1)}, u32[]{:S(2)}, u32[]{:S(2)}) collective-permute-start(bf16[512,128]{1,0:T(8,128)(2,1)S(1)} %get-tuple-element.59), channel_id=1, source_target_pairs={{0,24},{1,25},{2,26},{3,27},{4,28},{5,29},{6,30},{7,31},{8,16},{9,... | collective-permute-start | bytes 393224 | tf_op jit(solution)/shard_map/ppermute | solution.py:451
  64.2 12.1 %collective-permute-start.12 = (bf16[512,128]{1,0:T(8,128)(2,1)S(1)}, bf16[512,128]{1,0:T(8,128)(2,1)S(1)}, u32[]{:S(2)}, u32[]{:S(2)}) collective-permute-start(bf16[512,128]{1,0:T(8,128)(2,1)S(1)} %get-tuple-element.66), channel_id=1, source_target_pairs={{0,8},{1,9},{2,10},{3,11},{4,12},{5,13},{6,14},{7,15},{8,0},{9,1},... | collective-permute-start | bytes 393224 | tf_op jit(solution)/shard_map/ppermute | solution.py:451
  69.4 11.4 %collective-permute-start.13 = (bf16[512,128]{1,0:T(8,128)(2,1)S(1)}, bf16[512,128]{1,0:T(8,128)(2,1)S(1)}, u32[]{:S(2)}, u32[]{:S(2)}) collective-permute-start(bf16[512,128]{1,0:T(8,128)(2,1)S(1)} %get-tuple-element.67), channel_id=1, source_target_pairs={{0,16},{1,17},{2,18},{3,19},{4,20},{5,21},{6,22},{7,23},{8,24},{9,... | collective-permute-start | bytes 393224 | tf_op jit(solution)/shard_map/ppermute | solution.py:451
  70.8 10.1 %collective-permute-start.14 = (bf16[512,128]{1,0:T(8,128)(2,1)S(1)}, bf16[512,128]{1,0:T(8,128)(2,1)S(1)}, u32[]{:S(2)}, u32[]{:S(2)}) collective-permute-start(bf16[512,128]{1,0:T(8,128)(2,1)S(1)} %get-tuple-element.68), channel_id=1, source_target_pairs={{0,24},{1,25},{2,26},{3,27},{4,28},{5,29},{6,30},{7,31},{8,16},{9,... | collective-permute-start | bytes 393224 | tf_op jit(solution)/shard_map/ppermute | solution.py:451
  71.7 12.0 %collective-permute-start.25 = (bf16[512,128]{1,0:T(8,128)(2,1)S(1)}, bf16[512,128]{1,0:T(8,128)(2,1)S(1)}, u32[]{:S(2)}, u32[]{:S(2)}) collective-permute-start(bf16[512,128]{1,0:T(8,128)(2,1)S(1)} %get-tuple-element.84), channel_id=1, source_target_pairs={{0,4},{1,5},{2,6},{3,7},{4,0},{5,1},{6,2},{7,3},{8,12},{9,13},{10,... | collective-permute-start | bytes 393224 | tf_op jit(solution)/shard_map/ppermute | solution.py:451
  73.9 21.3 %collective-permute-start.26 = (bf16[512,128]{1,0:T(8,128)(2,1)S(1)}, bf16[512,128]{1,0:T(8,128)(2,1)S(1)}, u32[]{:S(2)}, u32[]{:S(2)}) collective-permute-start(bf16[512,128]{1,0:T(8,128)(2,1)S(1)} %get-tuple-element.85), channel_id=1, source_target_pairs={{0,6},{1,7},{2,4},{3,5},{4,2},{5,3},{6,0},{7,1},{8,14},{9,15},{10,... | collective-permute-start | bytes 393224 | tf_op jit(solution)/shard_map/ppermute | solution.py:451
  76.3 21.7 %collective-permute-start.18 = (bf16[512,128]{1,0:T(8,128)(2,1)S(1)}, bf16[512,128]{1,0:T(8,128)(2,1)S(1)}, u32[]{:S(2)}, u32[]{:S(2)}) collective-permute-start(bf16[512,128]{1,0:T(8,128)(2,1)S(1)} %get-tuple-element.74), channel_id=1, source_target_pairs={{0,8},{1,9},{2,10},{3,11},{4,12},{5,13},{6,14},{7,15},{8,0},{9,1},... | collective-permute-start | bytes 393224 | tf_op jit(solution)/shard_map/ppermute | solution.py:451
  80.9 17.2 %collective-permute-start.19 = (bf16[512,128]{1,0:T(8,128)(2,1)S(1)}, bf16[512,128]{1,0:T(8,128)(2,1)S(1)}, u32[]{:S(2)}, u32[]{:S(2)}) collective-permute-start(bf16[512,128]{1,0:T(8,128)(2,1)S(1)} %get-tuple-element.75), channel_id=1, source_target_pairs={{0,16},{1,17},{2,18},{3,19},{4,20},{5,21},{6,22},{7,23},{8,24},{9,... | collective-permute-start | bytes 393224 | tf_op jit(solution)/shard_map/ppermute | solution.py:451
  80.9 17.2 %collective-permute-start.20 = (bf16[512,128]{1,0:T(8,128)(2,1)S(1)}, bf16[512,128]{1,0:T(8,128)(2,1)S(1)}, u32[]{:S(2)}, u32[]{:S(2)}) collective-permute-start(bf16[512,128]{1,0:T(8,128)(2,1)S(1)} %get-tuple-element.76), channel_id=1, source_target_pairs={{0,24},{1,25},{2,26},{3,27},{4,28},{5,29},{6,30},{7,31},{8,16},{9,... | collective-permute-start | bytes 393224 | tf_op jit(solution)/shard_map/ppermute | solution.py:451
  83.7 14.4 %collective-permute-start.27 = (bf16[16,512]{1,0:T(8,128)(2,1)S(1)}, bf16[16,512]{1,0:T(8,128)(2,1)S(1)}, u32[]{:S(2)}, u32[]{:S(2)}) collective-permute-start(bf16[16,512]{1,0:T(8,128)(2,1)S(1)} %get-tuple-element.86), channel_id=1, source_target_pairs={{0,1},{1,2},{2,3},{4,5},{5,6},{6,7},{8,9},{9,10},{10,11},{12,13},{... | collective-permute-start | bytes 49160 | tf_op jit(solution)/shard_map/ppermute | solution.py:590
  95.2 5.1 %collective-permute-start.28 = (bf16[16,512]{1,0:T(8,128)(2,1)S(1)}, bf16[16,512]{1,0:T(8,128)(2,1)S(1)}, u32[]{:S(2)}, u32[]{:S(2)}) collective-permute-start(bf16[16,512]{1,0:T(8,128)(2,1)S(1)} %get-tuple-element.87), channel_id=1, source_target_pairs={{1,0},{2,1},{3,2},{5,4},{6,5},{7,6},{9,8},{10,9},{11,10},{13,12},{... | collective-permute-start | bytes 49160 | tf_op jit(solution)/shard_map/ppermute | solution.py:590
  100.2 3.0 %copy-start.3 = (f32[128]{0:T(128)S(1)}, f32[128]{0:T(128)}, u32[]{:S(2)}) copy-start(f32[128]{0:T(128)} %param.13) | copy-start | bytes 1540
  100.2 3.0 %copy-start.4 = (f32[128]{0:T(128)S(1)}, f32[128]{0:T(128)}, u32[]{:S(2)}) copy-start(f32[128]{0:T(128)} %param.15) | copy-start | bytes 1540
  100.6 6.2 %collective-permute-start.29 = (bf16[2,80,512]{2,1,0:T(8,128)(2,1)S(1)}, bf16[2,80,512]{2,1,0:T(8,128)(2,1)S(1)}, u32[]{:S(2)}, u32[]{:S(2)}) collective-permute-start(bf16[2,80,512]{2,1,0:T(8,128)(2,1)S(1)} %get-tuple-element.90), channel_id=1, source_target_pairs={{0,4},{4,8},{8,12},{12,16},{16,20},{20,24},{24,28},{1,5},{5,9},{9,... | collective-permute-start | bytes 491528 | tf_op jit(solution)/shard_map/ppermute | solution.py:590
  101.9 10.2 %collective-permute-start.30 = (bf16[2,80,512]{2,1,0:T(8,128)(2,1)S(1)}, bf16[2,80,512]{2,1,0:T(8,128)(2,1)S(1)}, u32[]{:S(2)}, u32[]{:S(2)}) collective-permute-start(bf16[2,80,512]{2,1,0:T(8,128)(2,1)S(1)} %get-tuple-element.91), channel_id=1, source_target_pairs={{4,0},{8,4},{12,8},{16,12},{20,16},{24,20},{28,24},{5,1},{9,5},{13... | collective-permute-start | bytes 491528 | tf_op jit(solution)/shard_map/ppermute | solution.py:590

commit v3 on v2

--- a/solution.py
+++ b/solution.py
@@ -59,7 +59,7 @@
 def index_kernel(shape, slots, blocks, *refs):
     n_z, n_y, n_x, n_c = shape
     codes = refs[:n_c]
-    index_ref, label_ref, label2_ref, counts, labels, labels2 = refs[n_c:]
+    index_ref, label_ref, label2_ref, counts, labels = refs[n_c:]
     tiles = n_z * n_y * n_x * n_c
     groups = n_y * n_x
     spare = groups * n_z * slots
@@ -68,14 +68,13 @@
         counts[t] = 0
         return carry
 
-    lax.fori_loop(0, tiles, clear, 0, unroll=8)
+    lax.fori_loop(0, tiles, clear, 0, unroll=16)
 
     def blank(s, carry):
         labels[s] = -1
-        labels2[s] = -1
         return carry
 
-    lax.fori_loop(0, spare, blank, 0, unroll=8)
+    lax.fori_loop(0, spare, blank, 0, unroll=32)
     z, y = split_low(lax.axis_index("frames"), n_y)
     x, c = split_low(lax.axis_index("rows"), n_c)
     pairs = codes[0].shape[0]
@@ -96,31 +95,34 @@
             index_ref[source * pairs + p] = slot
             index_ref[(n_c + source) * pairs + p] = slot2
             labels[slot] = block
-            labels2[slot2] = block
             return carry
 
-        lax.fori_loop(0, pairs, place, 0, unroll=4)
+        lax.fori_loop(0, pairs, place, 0, unroll=16)
     lane = lax.broadcasted_iota(jnp.int32, (LABEL_ROWS, label_ref.shape[1]), 1)
-    for source, target, outer in ((labels, label_ref, groups), (labels2, label2_ref, n_z)):
-        inner = spare // outer
-        for g in range(outer):
-            row = jnp.full(lane.shape, -1, jnp.int32)
-            for k in range(inner):
-                row = jnp.where(lane == k, source[g * inner + k], row)
-            target[g * LABEL_ROWS : (g + 1) * LABEL_ROWS, :] = row.astype(jnp.float32).astype(jnp.bfloat16)
+    for g in range(groups):
+        row = jnp.full(lane.shape, -1, jnp.int32)
+        for k in range(n_z * slots):
+            row = jnp.where(lane == k, labels[g * n_z * slots + k], row)
+        label_ref[g * LABEL_ROWS : (g + 1) * LABEL_ROWS, :] = row.astype(jnp.float32).astype(jnp.bfloat16)
+    for step in range(n_z):
+        row = jnp.full(lane.shape, -1, jnp.int32)
+        for g in range(groups):
+            for rank in range(slots):
+                label = labels[(g * n_z + step) * slots + rank]
+                row = jnp.where(lane == g * slots + rank, label, row)
+        label2_ref[step * LABEL_ROWS : (step + 1) * LABEL_ROWS, :] = row.astype(jnp.float32).astype(jnp.bfloat16)
 
 
 def contribute_kernel(n_c, outer, per_group, images, top, spans, base, direct, labelled, *refs):
     index_ref = refs[0]
-    heads = refs[1 : 1 + n_c]
-    refs = refs[1 + n_c :]
+    features = refs[1 : 1 + n_c]
+    sources = refs[1 + n_c : 1 + 2 * n_c]
+    refs = refs[1 + 2 * n_c :]
     rows = sum(span[1] for span in spans)
     pairs = images * top
-    size = heads[0].shape[1]
+    size = features[0].shape[1]
     if labelled:
         label_ref, refs = refs[0], refs[1:]
-    if not direct:
-        sources, refs = refs[:n_c], refs[n_c:]
     outs = refs[: outer * len(spans)]
     refs = refs[outer * len(spans) :]
     buffers, refs = refs[: len(spans)], refs[len(spans) :]
@@ -145,16 +147,14 @@
         if not direct:
             for load in loads[s * len(spans) : (s + 1) * len(spans)]:
                 load.wait()
-        pixel_base = heads[s].shape[0] - images * size
 
         def image(b, carry):
             p0 = s * pairs + b * top
             if direct:
-                weights = heads[s][pl.ds(pl.multiple_of(b * top * rows, top * rows), top * rows), :]
+                weights = sources[s][pl.ds(pl.multiple_of(b * top * rows, top * rows), top * rows), :]
             else:
                 weights = held[pl.ds(p0, top)].reshape(top * rows, size)
-            pixels = heads[s][pl.ds(pl.multiple_of(pixel_base + b * size, size), size), :]
-            product = jnp.dot(weights, pixels, preferred_element_type=jnp.float32)
+            product = jnp.dot(weights, features[s][b], preferred_element_type=jnp.float32)
             product = product.astype(jnp.bfloat16)
             for t in range(top):
                 slot = index_ref[base + p0 + t]
@@ -213,7 +213,7 @@
                 plan_ref[g * stride + 1 + count] = s * blocks + jnp.maximum(label, 0)
                 return count + (label >= 0).astype(jnp.int32)
 
-            plan_ref[g * stride] = lax.fori_loop(0, per_group, note, 0, unroll=8)
+            plan_ref[g * stride] = lax.fori_loop(0, per_group, note, 0, unroll=32)
     for g in range(groups):
 
         def add(n, carry):
@@ -454,10 +454,7 @@
     weights = pair_weight[0].reshape(images * top, size, size)
     turned = len(spans) - 1
     begin, rows = spans[turned]
-    head = jnp.concatenate(
-        [weights[:, begin : begin + rows].reshape(-1, size), features[0].reshape(-1, channels)], axis=0
-    )
-    shared = [(code, head, weights)]
+    shared = [(code, weights[:, begin : begin + rows].reshape(-1, size), features[0], weights)]
     for dc in range(1, n_c):
         shared.append(tuple(moved_by(v, dc=dc) for v in shared[0]))
     index, labels, labels_turned = pl.pallas_call(
@@ -469,8 +466,10 @@
         ),
         in_specs=[smem()] * n_c,
         out_specs=(smem(), vmem(), vmem()),
-        scratch_shapes=[pltpu.SMEM((devices,), jnp.int32)]
-        + [pltpu.SMEM((groups * n_z * slots + 1,), jnp.int32)] * 2,
+        scratch_shapes=[
+            pltpu.SMEM((devices,), jnp.int32),
+            pltpu.SMEM((groups * n_z * slots + 1,), jnp.int32),
+        ],
         compiler_params=params(),
         name="index",
     )(*[v[0] for v in shared])
@@ -485,14 +484,12 @@
             outs += arrays(outer, per * chunk + (0 if marks is None else LABEL_ROWS), channels)
             scratch.append(VMEM(((groups * n_z * slots + 1) * chunk, channels), jnp.bfloat16))
         scratch.append(pltpu.SemaphoreType.DMA((2 * len(outs),)))
-        in_specs = [smem()] + [vmem()] * n_c
-        args = [index] + [v[1] for v in shared]
+        in_specs = [smem()] + [vmem()] * n_c + [vmem() if direct else anywhere()] * n_c
+        args = [index] + [v[2] for v in shared] + [v[1 if direct else 3] for v in shared]
         if marks is not None:
             in_specs.append(vmem())
             args.append(marks)
         if not direct:
-            in_specs += [anywhere()] * n_c
-            args += [v[2] for v in shared]
             scratch += [
                 VMEM((n_c * images * top, sum(chunk for _, chunk in own), size), jnp.bfloat16),
                 pltpu.SemaphoreType.DMA((n_c * len(own),)),
@@ -591,8 +588,7 @@
 
     left = moved(right_cols, "rows", n_rows, 1)
     right = moved(left_cols, "rows", n_rows, -1)
-    wide = 80
-    packed = jax.ShapeDtypeStruct((2, wide, lanes), jnp.bfloat16)
+    packed = jax.ShapeDtypeStruct((2, TY + 8, lanes), jnp.bfloat16)
     main, first_rows, last_rows = pl.pallas_call(
         functools.partial(finish_kernel, spans, [n_z] * turned + [groups], blocks, size),
         out_shape=(jax.ShapeDtypeStruct((cells, lanes), jnp.bfloat16), packed, packed),
@@ -605,6 +601,7 @@
     low = moved(last_rows, "frames", n_frames, 1)
     high = moved(first_rows, "frames", n_frames, -1)
     main = main.reshape(TX, TY, lanes)
+    wide = 80
     bias = (conv1_bias[None], conv2_bias[None])
 
     def conv_scratch(height, hidden, out):

time: 117 us -> 117 us (level)
  Pallas kernels: 29.4 us -> 27.1 us
  starting transfers between devices: 56.8 us -> 58.2 us
  local copies, waits for them, and re-layouts: 1.29 us -> 2.47 us
    pallas_call x3, Pallas kernels: 9.92 us -> 8.5 us  [contribute(): pl.pallas_call(functools.partial(contribute_kernel, n_c, outer, per, imag...]
    concatenate x1 -> x0, other arithmetic: 1.26 us -> none  [shards(): jnp.concatenate([weights[:, begin:begin + rows].reshape(-1, size), featur...]
    ppermute x27 -> x28, starting transfers between devices: 40.9 us -> 41.5 us  [moved_by(): return lax.ppermute(value, ('frames', 'rows'), pairs)]
    ppermute x27 -> x28, waiting for transfers between devices: 19.3 us -> 19.9 us  [moved_by(): return lax.ppermute(value, ('frames', 'rows'), pairs)]
  transfers between devices with their start and end apart: 31 -> 32, of which waited for: 9 -> 9; matrix products, arithmetic and copies ran while one was open for 2% -> 2% of each run, Pallas kernels for 22% -> 20%
where the time goes in v3:
time: 117 us; the launch traced here: 116 us
  starting transfers between devices  58.2 us (50%)
  Pallas kernels  27.1 us (23%)
  waiting for transfers between devices  26.8 us (23%)
  local copies, waits for them, and re-layouts  2.47 us (2%)
    ppermute x28, starting transfers between devices, moved_by(): return lax.ppermute(value, ('frames', 'rows'), pairs)  41.5 us
    ppermute x28, waiting for transfers between devices, moved_by(): return lax.ppermute(value, ('frames', 'rows'), pairs)  19.9 us
    ppermute x4, starting transfers between devices, moved(): return lax.ppermute(value, axis, pairs)  16.7 us
    pallas_call x3, Pallas kernels, contribute(): pl.pallas_call(functools.partial(contribute_kernel, n_c, outer, per, imag...  8.5 us
    pallas_call x4, Pallas kernels, merge(): pl.pallas_call(functools.partial(merge_kernel, inner, outer, slots, chunk...  7.33 us
    ppermute x4, waiting for transfers between devices, moved(): return lax.ppermute(value, axis, pairs)  6.95 us
    pallas_call x1, Pallas kernels, shards(): pl.pallas_call(border_kernel, out_shape=jax.ShapeDtypeStruct((cells * DEP...  3.68 us
    pallas_call x1, Pallas kernels, shards(): pl.pallas_call(interior_kernel, out_shape=(jax.ShapeDtypeStruct(((TX - 4)...  3.61 us
  transfers between devices with their start and end apart: 32, of which 9 were waited for; matrix products, arithmetic and copies ran while one was open for 2% of the time, Pallas kernels for 20%

profile of v3, /device:TPU:1, one launch (start us, length us, event | category | flops | bytes accessed | tf_op | source)
XLA Modules:
  0.0 115.6 jit_solution(4214964732005845364)
XLA Ops:
  0.0 0.0 collective-permute-start.2
  0.0 1.2 %slice.4 = bf16[64,32,128]{2,1,0:T(8,128)(2,1)S(1)} slice(bf16[64,128,128]{2,1,0:T(8,128)(2,1)} %bitcast.8), slice={[0:64], [64:96], [0:128]} | slice | bytes 1048576 | tf_op jit(solution)/shard_map/slice | solution.py:457
  1.3 0.5 collective-permute-start.21
  1.8 0.1 collective-permute-start.1
  1.9 0.7 multiply_add_fusion
  2.6 0.1 copy.10
  2.7 0.1 reshape.12.refs_0_
  2.8 0.5 collective-permute-start
  3.3 2.6 %collective-permute-done.refs_1_ = s32[64]{0:T(128)S(1)} collective-permute-done((s32[64]{0:T(128)S(1)}, s32[64]{0:T(128)S(1)}, u32[]{:S(2)}, u32[]{:S(2)}) %collective-permute-start) | collective-permute-done | bytes 288 | tf_op jit(solution)/shard_map/ppermute | solution.py:451
  5.9 2.6 %index.1 = (s32[256]{0:T(256)S(1)}, bf16[64,128]{1,0:T(8,128)(2,1)S(1)}, bf16[64,128]{1,0:T(8,128)(2,1)S(1)}) custom-call(s32[64]{0:T(128)S(1)} %reshape.12.refs_0_, s32[64]{0:T(128)S(1)} %collective-permute-done.refs_1_), custom_call_target="tpu_custom_call" | custom-call | tf_op jit(solution)/shard_map/index/pallas_call | solution.py:460
  8.5 0.0 collective-permute-done.21.refs_4_
  8.5 0.0 copy-start.1
  8.6 1.0 copy-done.1
  9.6 2.8 %shard_map.87 = (bf16[1040,128]{1,0:T(8,128)(2,1)S(1)}, bf16[1040,128]{1,0:T(8,128)(2,1)S(1)}, bf16[1040,128]{1,0:T(8,128)(2,1)S(1)}, bf16[1040,128]{1,0:T(8,128)(2,1)S(1)}) custom-call(s32[256]{0:T(256)S(1)} %get-tuple-element.50.refs_0_, bf16[16,128,128]{2,1,0:T(8,128)(2,1)S(1)} %bitcast.12, bf16[16,128,128]{2,1,0:T(8,128)(2,1)S(1)} %collective-permute-done.1.refs_2_, ...), custom_call_target="tpu_custom_call" | custom-call | tf_op jit(solution)/shard_map/pallas_call | solution.py:498
  12.4 2.5 %collective-permute-start.22 = (bf16[1040,128]{1,0:T(8,128)(2,1)S(1)}, bf16[1040,128]{1,0:T(8,128)(2,1)S(1)}, u32[]{:S(2)}, u32[]{:S(2)}) collective-permute-start(bf16[1040,128]{1,0:T(8,128)(2,1)S(1)} %get-tuple-element.79), channel_id=1, source_target_pairs={{0,8},{1,9},{2,10},{3,11},{4,12},{5,13},{6,14},{7,15},{8,0},{9,1},... | collective-permute-start | bytes 798728 | tf_op jit(solution)/shard_map/ppermute | solution.py:451
  14.8 2.3 %collective-permute-start.23 = (bf16[1040,128]{1,0:T(8,128)(2,1)S(1)}, bf16[1040,128]{1,0:T(8,128)(2,1)S(1)}, u32[]{:S(2)}, u32[]{:S(2)}) collective-permute-start(bf16[1040,128]{1,0:T(8,128)(2,1)S(1)} %get-tuple-element.80), channel_id=1, source_target_pairs={{0,16},{1,17},{2,18},{3,19},{4,20},{5,21},{6,22},{7,23},{8,24},{9,... | collective-permute-start | bytes 798728 | tf_op jit(solution)/shard_map/ppermute | solution.py:451
  17.1 0.0 collective-permute-start.24
  17.2 2.6 %shard_map.82 = (bf16[1040,128]{1,0:T(8,128)(2,1)S(1)}, bf16[1040,128]{1,0:T(8,128)(2,1)S(1)}, bf16[1040,128]{1,0:T(8,128)(2,1)S(1)}, bf16[1040,128]{1,0:T(8,128)(2,1)S(1)}) custom-call(s32[256]{0:T(256)S(1)} %get-tuple-element.50.refs_0_, bf16[16,128,128]{2,1,0:T(8,128)(2,1)S(1)} %bitcast.13, bf16[16,128,128]{2,1,0:T(8,128)(2,1)S(1)} %collective-permute-done.1.refs_2_, ...), custom_call_target="tpu_custom_call" | custom-call | tf_op jit(solution)/shard_map/pallas_call | solution.py:498
  19.8 1.3 %collective-permute-start.3 = (bf16[1040,128]{1,0:T(8,128)(2,1)S(1)}, bf16[1040,128]{1,0:T(8,128)(2,1)S(1)}, u32[]{:S(2)}, u32[]{:S(2)}) collective-permute-start(bf16[1040,128]{1,0:T(8,128)(2,1)S(1)} %get-tuple-element.53), channel_id=1, source_target_pairs={{0,2},{1,3},{2,0},{3,1},{4,6},{5,7},{6,4},{7,5},{8,10},{9,11},{10,... | collective-permute-start | bytes 798728 | tf_op jit(solution)/shard_map/ppermute | solution.py:451
  21.1 3.1 %shard_map.84 = (bf16[1024,128]{1,0:T(8,128)(2,1)S(1)}, bf16[1024,128]{1,0:T(8,128)(2,1)S(1)}, bf16[1024,128]{1,0:T(8,128)(2,1)S(1)}, bf16[1024,128]{1,0:T(8,128...) custom-call(s32[256]{0:T(256)S(1)} %get-tuple-element.50.refs_0_, ...), custom_call_target="tpu_custom_call" | custom-call | tf_op jit(solution)/shard_map/pallas_call | solution.py:498
  24.2 0.0 copy-start.3
  24.2 0.0 copy-start.4
  24.2 0.3 collective-permute-start.9
  24.5 1.8 %collective-permute-done.22.refs_1_ = bf16[1040,128]{1,0:T(8,128)(2,1)S(1)} collective-permute-done((bf16[1040,128]{1,0:T(8,128)(2,1)S(1)}, bf16[1040,128]{1,0:T(8,128)(2,1)S(1)}, u32[]{:S(2)}, u32[]{:S(2)}) %collective-permute-start.22) | collective-permute-done | bytes 266272 | tf_op jit(solution)/shard_map/ppermute | solution.py:451
  26.4 1.1 collective-permute-start.4
  27.5 1.1 collective-permute-start.5
  28.6 6.0 %collective-permute-done.24.refs_3_ = bf16[1040,128]{1,0:T(8,128)(2,1)S(1)} collective-permute-done((bf16[1040,128]{1,0:T(8,128)(2,1)S(1)}, bf16[1040,128]{1,0:T(8,128)(2,1)S(1)}, u32[]{:S(2)}, u32[]{:S(2)}) %collective-permute-start.24) | collective-permute-done | bytes 266272 | tf_op jit(solution)/shard_map/ppermute | solution.py:451
  34.6 2.2 %shard_map.88 = (bf16[512,128]{1,0:T(8,128)(2,1)S(1)}, bf16[512,128]{1,0:T(8,128)(2,1)S(1)}, bf16[512,128]{1,0:T(8,128)(2,1)S(1)}, bf16[512,128]{1,0:T(8,128)(2,1)S(1)}, s32[132]{0:T(256)}) custom-call(bf16[1040,128]{1,0:T(8,128)(2,1)S(1)} %get-tuple-element.78.refs_0_, bf16[1040,128]{1,0:T(8,128)(2,1)S(1)} %collective-permute-done.22.refs_1_, ...), custom_call_target="tpu_custom_call" | custom-call | tf_op jit(solution)/shard_map/pallas_call | solution.py:540
  36.8 1.3 %collective-permute-start.25 = (bf16[512,128]{1,0:T(8,128)(2,1)S(1)}, bf16[512,128]{1,0:T(8,128)(2,1)S(1)}, u32[]{:S(2)}, u32[]{:S(2)}) collective-permute-start(bf16[512,128]{1,0:T(8,128)(2,1)S(1)} %get-tuple-element.83), channel_id=1, source_target_pairs={{0,2},{1,3},{2,0},{3,1},{4,6},{5,7},{6,4},{7,5},{8,10},{9,11},{10,... | collective-permute-start | bytes 393224 | tf_op jit(solution)/shard_map/ppermute | solution.py:451
  38.1 2.6 %collective-permute-done.25.refs_13_ = bf16[512,128]{1,0:T(8,128)(2,1)S(1)} collective-permute-done((bf16[512,128]{1,0:T(8,128)(2,1)S(1)}, bf16[512,128]{1,0:T(8,128)(2,1)S(1)}, u32[]{:S(2)}, u32[]{:S(2)}) %collective-permute-start.25) | collective-permute-done | bytes 131104 | tf_op jit(solution)/shard_map/ppermute | solution.py:451
  40.7 2.3 %collective-permute-start.10 = (bf16[1024,128]{1,0:T(8,128)(2,1)S(1)}, bf16[1024,128]{1,0:T(8,128)(2,1)S(1)}, u32[]{:S(2)}, u32[]{:S(2)}) collective-permute-start(bf16[1024,128]{1,0:T(8,128)(2,1)S(1)} %get-tuple-element.62), channel_id=1, source_target_pairs={{0,4},{1,5},{2,6},{3,7},{4,0},{5,1},{6,2},{7,3},{8,12},{9,13},{10,... | collective-permute-start | bytes 786440 | tf_op jit(solution)/shard_map/ppermute | solution.py:451
  43.0 0.9 collective-permute-start.11
  43.9 0.0 collective-permute-done.3.refs_1_
  43.9 0.3 collective-permute-start.15
  44.3 1.4 %collective-permute-start.16 = (bf16[1024,128]{1,0:T(8,128)(2,1)S(1)}, bf16[1024,128]{1,0:T(8,128)(2,1)S(1)}, u32[]{:S(2)}, u32[]{:S(2)}) collective-permute-start(bf16[1024,128]{1,0:T(8,128)(2,1)S(1)} %get-tuple-element.71), channel_id=1, source_target_pairs={{0,4},{1,5},{2,6},{3,7},{4,0},{5,1},{6,2},{7,3},{8,12},{9,13},{10,... | collective-permute-start | bytes 786440 | tf_op jit(solution)/shard_map/ppermute | solution.py:451
  45.7 1.0 collective-permute-start.17
  46.6 2.4 %shard_map.83 = (bf16[512,128]{1,0:T(8,128)(2,1)S(1)}, bf16[512,128]{1,0:T(8,128)(2,1)S(1)}, bf16[512,128]{1,0:T(8,128)(2,1)S(1)}, bf16[512,128]{1,0:T(8,128)(2,1)S(1)}, s32[132]{0:T(256)S(1)}) custom-call(bf16[1040,128]{1,0:T(8,128)(2,1)S(1)} %get-tuple-element.52.refs_0_, bf16[1040,128]{1,0:T(8,128)(2,1)S(1)} %collective-permute-done.3.refs_1_, ...), custom_call_target="tpu_custom_call" | custom-call | tf_op jit(solution)/shard_map/pallas_call | solution.py:540
  49.0 1.1 collective-permute-done.10.refs_2_
  50.1 8.6 %collective-permute-start.6 = (bf16[512,128]{1,0:T(8,128)(2,1)S(1)}, bf16[512,128]{1,0:T(8,128)(2,1)S(1)}, u32[]{:S(2)}, u32[]{:S(2)}) collective-permute-start(bf16[512,128]{1,0:T(8,128)(2,1)S(1)} %get-tuple-element.57), channel_id=1, source_target_pairs={{0,8},{1,9},{2,10},{3,11},{4,12},{5,13},{6,14},{7,15},{8,0},{9,1},... | collective-permute-start | bytes 393224 | tf_op jit(solution)/shard_map/ppermute | solution.py:451
  58.7 1.9 %collective-permute-start.7 = (bf16[512,128]{1,0:T(8,128)(2,1)S(1)}, bf16[512,128]{1,0:T(8,128)(2,1)S(1)}, u32[]{:S(2)}, u32[]{:S(2)}) collective-permute-start(bf16[512,128]{1,0:T(8,128)(2,1)S(1)} %get-tuple-element.58), channel_id=1, source_target_pairs={{0,16},{1,17},{2,18},{3,19},{4,20},{5,21},{6,22},{7,23},{8,24},{9,... | collective-permute-start | bytes 393224 | tf_op jit(solution)/shard_map/ppermute | solution.py:451
  60.6 0.2 collective-permute-start.8
  60.8 1.4 %shard_map.85 = (bf16[512,128]{1,0:T(8,128)(2,1)S(1)}, bf16[512,128]{1,0:T(8,128)(2,1)S(1)}, bf16[512,128]{1,0:T(8,128)(2,1)S(1)}, bf16[512,128]{1,0:T(8,128)(2,1)S(1)}) custom-call(bf16[1024,128]{1,0:T(8,128)(2,1)S(1)} %get-tuple-element.60.refs_0_, bf16[1024,128]{1,0:T(8,128)(2,1)S(1)} %collective-permute-done.9.refs_1_, ...), custom_call_target="tpu_custom_call" | custom-call | tf_op jit(solution)/shard_map/pallas_call | solution.py:540
  62.2 1.6 %collective-permute-done.16.refs_2_ = bf16[1024,128]{1,0:T(8,128)(2,1)S(1)} collective-permute-done((bf16[1024,128]{1,0:T(8,128)(2,1)S(1)}, bf16[1024,128]{1,0:T(8,128)(2,1)S(1)}, u32[]{:S(2)}, u32[]{:S(2)}) %collective-permute-start.16) | collective-permute-done | bytes 262176 | tf_op jit(solution)/shard_map/ppermute | solution.py:451
  63.8 5.8 %collective-permute-start.12 = (bf16[512,128]{1,0:T(8,128)(2,1)S(1)}, bf16[512,128]{1,0:T(8,128)(2,1)S(1)}, u32[]{:S(2)}, u32[]{:S(2)}) collective-permute-start(bf16[512,128]{1,0:T(8,128)(2,1)S(1)} %get-tuple-element.66), channel_id=1, source_target_pairs={{0,8},{1,9},{2,10},{3,11},{4,12},{5,13},{6,14},{7,15},{8,0},{9,1},... | collective-permute-start | bytes 393224 | tf_op jit(solution)/shard_map/ppermute | solution.py:451
  69.6 1.4 %collective-permute-start.13 = (bf16[512,128]{1,0:T(8,128)(2,1)S(1)}, bf16[512,128]{1,0:T(8,128)(2,1)S(1)}, u32[]{:S(2)}, u32[]{:S(2)}) collective-permute-start(bf16[512,128]{1,0:T(8,128)(2,1)S(1)} %get-tuple-element.67), channel_id=1, source_target_pairs={{0,16},{1,17},{2,18},{3,19},{4,20},{5,21},{6,22},{7,23},{8,24},{9,... | collective-permute-start | bytes 393224 | tf_op jit(solution)/shard_map/ppermute | solution.py:451
  71.0 0.9 collective-permute-start.14
  71.9 2.2 %collective-permute-start.26 = (bf16[512,128]{1,0:T(8,128)(2,1)S(1)}, bf16[512,128]{1,0:T(8,128)(2,1)S(1)}, u32[]{:S(2)}, u32[]{:S(2)}) collective-permute-start(bf16[512,128]{1,0:T(8,128)(2,1)S(1)} %get-tuple-element.84), channel_id=1, source_target_pairs={{0,4},{1,5},{2,6},{3,7},{4,0},{5,1},{6,2},{7,3},{8,12},{9,13},{10,... | collective-permute-start | bytes 393224 | tf_op jit(solution)/shard_map/ppermute | solution.py:451
  74.1 1.0 collective-permute-start.27
  75.1 1.4 %shard_map.86 = (bf16[512,128]{1,0:T(8,128)(2,1)S(1)}, bf16[512,128]{1,0:T(8,128)(2,1)S(1)}, bf16[512,128]{1,0:T(8,128)(2,1)S(1)}, bf16[512,128]{1,0:T(8,128)(2,1)S(1)}) custom-call(bf16[1024,128]{1,0:T(8,128)(2,1)S(1)} %get-tuple-element.69.refs_0_, bf16[1024,128]{1,0:T(8,128)(2,1)S(1)} %collective-permute-done.15.refs_1_, ...), custom_call_target="tpu_custom_call" | custom-call | tf_op jit(solution)/shard_map/pallas_call | solution.py:540
  76.5 0.5 collective-permute-start.18
  77.0 4.1 %collective-permute-done.13.refs_6_ = bf16[512,128]{1,0:T(8,128)(2,1)S(1)} collective-permute-done((bf16[512,128]{1,0:T(8,128)(2,1)S(1)}, bf16[512,128]{1,0:T(8,128)(2,1)S(1)}, u32[]{:S(2)}, u32[]{:S(2)}) %collective-permute-start.13) | collective-permute-done | bytes 131104 | tf_op jit(solution)/shard_map/ppermute | solution.py:451
  81.1 2.0 %collective-permute-start.20 = (bf16[512,128]{1,0:T(8,128)(2,1)S(1)}, bf16[512,128]{1,0:T(8,128)(2,1)S(1)}, u32[]{:S(2)}, u32[]{:S(2)}) collective-permute-start(bf16[512,128]{1,0:T(8,128)(2,1)S(1)} %get-tuple-element.76), channel_id=1, source_target_pairs={{0,24},{1,25},{2,26},{3,27},{4,28},{5,29},{6,30},{7,31},{8,16},{9,... | collective-permute-start | bytes 393224 | tf_op jit(solution)/shard_map/ppermute | solution.py:451
  83.2 12.2 %collective-permute-start.28 = (bf16[16,512]{1,0:T(8,128)(2,1)S(1)}, bf16[16,512]{1,0:T(8,128)(2,1)S(1)}, u32[]{:S(2)}, u32[]{:S(2)}) collective-permute-start(bf16[16,512]{1,0:T(8,128)(2,1)S(1)} %get-tuple-element.86), channel_id=1, source_target_pairs={{0,1},{1,2},{2,3},{4,5},{5,6},{6,7},{8,9},{9,10},{10,11},{12,13},{... | collective-permute-start | bytes 49160 | tf_op jit(solution)/shard_map/ppermute | solution.py:587
  95.4 0.0 copy-start.5
  95.4 0.0 copy-start.6
  95.4 1.9 %collective-permute-start.29 = (bf16[16,512]{1,0:T(8,128)(2,1)S(1)}, bf16[16,512]{1,0:T(8,128)(2,1)S(1)}, u32[]{:S(2)}, u32[]{:S(2)}) collective-permute-start(bf16[16,512]{1,0:T(8,128)(2,1)S(1)} %get-tuple-element.87), channel_id=1, source_target_pairs={{1,0},{2,1},{3,2},{5,4},{6,5},{7,6},{9,8},{10,9},{11,10},{13,12},{... | collective-permute-start | bytes 49160 | tf_op jit(solution)/shard_map/ppermute | solution.py:587
  97.3 0.9 bands.1
  98.3 2.1 %collective-permute-done.29.refs_17_.right_ref = bf16[16,512]{1,0:T(8,128)(2,1)S(1)} collective-permute-done((bf16[16,512]{1,0:T(8,128)(2,1)S(1)}, bf16[16,512]{1,0:T(8,128)(2,1)S(1)}, u32[]{:S(2)}, u32[]{:S(2)}) %collective-permute-start.29) | collective-permute-done | bytes 16416 | tf_op jit(solution)/shard_map/ppermute | solution.py:587
  100.4 0.4 finish.1
  100.8 1.4 %collective-permute-start.30 = (bf16[2,72,512]{2,1,0:T(8,128)(2,1)S(1)}, bf16[2,72,512]{2,1,0:T(8,128)(2,1)S(1)}, u32[]{:S(2)}, u32[]{:S(2)}) collective-permute-start(bf16[2,72,512]{2,1,0:T(8,128)(2,1)S(1)} %get-tuple-element.90), channel_id=1, source_target_pairs={{0,4},{4,8},{8,12},{12,16},{16,20},{20,24},{24,28},{1,5},{5,9},{9,... | collective-permute-start | bytes 442376 | tf_op jit(solution)/shard_map/ppermute | solution.py:587
  102.2 1.3 %collective-permute-start.31 = (bf16[2,72,512]{2,1,0:T(8,128)(2,1)S(1)}, bf16[2,72,512]{2,1,0:T(8,128)(2,1)S(1)}, u32[]{:S(2)}, u32[]{:S(2)}) collective-permute-start(bf16[2,72,512]{2,1,0:T(8,128)(2,1)S(1)} %get-tuple-element.91), channel_id=1, source_target_pairs={{4,0},{8,4},{12,8},{16,12},{20,16},{24,20},{28,24},{5,1},{9,5},{13... | collective-permute-start | bytes 442376 | tf_op jit(solution)/shard_map/ppermute | solution.py:587
  103.5 3.6 %interior.1 = (bf16[1024,128]{1,0:T(8,128)(2,1)S(1)}, bf16[4,80,512]{2,1,0:T(8,128)(2,1)S(1)}) custom-call(bf16[8,64,512]{2,1,0:T(8,128)(2,1)S(1)} %bitcast.15, bf16[16,512]{1,0:T(8,128)(2,1)S(1)} %collective-permute-done.28.refs_16_.left_ref, bf16[16,512]{1,0:T(8,128)(2,1)S(1)} %collective-permute-done.29.refs_17_.right_ref, ...), custom_call_target="tpu_custom_call" | custom-call | tf_op jit(solution)/shard_map/interior/pallas_call | solution.py:615
  107.1 4.8 %collective-permute-done.31.high_ref = bf16[2,72,512]{2,1,0:T(8,128)(2,1)S(1)} collective-permute-done((bf16[2,72,512]{2,1,0:T(8,128)(2,1)S(1)}, bf16[2,72,512]{2,1,0:T(8,128)(2,1)S(1)}, u32[]{:S(2)}, u32[]{:S(2)}) %collective-permute-start.31) | collective-permute-done | bytes 147488 | tf_op jit(solution)/shard_map/ppermute | solution.py:587
  111.9 3.7 %border.1 = bf16[2048,128]{1,0:T(8,128)(2,1)} custom-call(bf16[8,64,512]{2,1,0:T(8,128)(2,1)S(1)} %bitcast.16, bf16[2,72,512]{2,1,0:T(8,128)(2,1)S(1)} %collective-permute-done.30.low_ref, bf16[2,72,512]{2,1,0:T(8,128)(2,1)S(1)} %collective-permute-done.31.high_ref, bf16[16,512]{1,0:T(8,128)(2,1)S(1)} %collective-permute-done.28.refs_16_.left_ref, ...), custom_call_target="tpu_custom_call" | custom-call | tf_op jit(solution)/shard_map/border/pallas_call | solution.py:627
  (31 shorter events, 0.1 us)
Async XLA Ops:
  0.0 17.2 %copy-start = (bf16[1,16,4,128,128]{4,3,2,1,0:T(8,128)(2,1)S(1)}, bf16[1,16,4,128,128]{4,3,2,1,0:T(8,128)(2,1)}, u32[]{:S(2)}) copy-start(bf16[1,16,4,128,128]{4,3,2,1,0:T(8,128)(2,1)} %param.9) | copy-start | bytes 6291460
  0.0 17.2 %collective-permute-start.2 = (bf16[64,128,128]{2,1,0:T(8,128)(2,1)}, bf16[64,128,128]{2,1,0:T(8,128)(2,1)}, u32[]{:S(2)}, u32[]{:S(2)}) collective-permute-start(bf16[64,128,128]{2,1,0:T(8,128)(2,1)} %bitcast.7), channel_id=1, source_target_pairs={{0,1},{1,0},{2,3},{3,2},{4,5},{5,4},{6,7},{7,6},{8,9},{9,8},{10,11... | collective-permute-start | bytes 6291464 | tf_op jit(solution)/shard_map/ppermute | solution.py:451
  1.3 7.3 %collective-permute-start.21 = (bf16[2048,128]{1,0:T(8,128)(2,1)S(1)}, bf16[2048,128]{1,0:T(8,128)(2,1)}, u32[]{:S(2)}, u32[]{:S(2)}) collective-permute-start(bf16[2048,128]{1,0:T(8,128)(2,1)S(1)} %bitcast.17), channel_id=1, source_target_pairs={{0,1},{1,0},{2,3},{3,2},{4,5},{5,4},{6,7},{7,6},{8,9},{9,8},{10,11... | collective-permute-start | bytes 1572872 | tf_op jit(solution)/shard_map/ppermute | solution.py:451
  1.8 6.7 %collective-permute-start.1 = (bf16[16,128,128]{2,1,0:T(8,128)(2,1)}, bf16[16,128,128]{2,1,0:T(8,128)(2,1)S(1)}, u32[]{:S(2)}, u32[]{:S(2)}) collective-permute-start(bf16[16,128,128]{2,1,0:T(8,128)(2,1)} %bitcast.11), channel_id=1, source_target_pairs={{0,1},{1,0},{2,3},{3,2},{4,5},{5,4},{6,7},{7,6},{8,9},{9,8},{10,11... | collective-permute-start | bytes 1572872 | tf_op jit(solution)/shard_map/ppermute | solution.py:451
  2.8 3.1 %collective-permute-start = (s32[64]{0:T(128)S(1)}, s32[64]{0:T(128)S(1)}, u32[]{:S(2)}, u32[]{:S(2)}) collective-permute-start(s32[64]{0:T(128)S(1)} %reshape.12.refs_0_), channel_id=1, source_target_pairs={{0,1},{1,0},{2,3},{3,2},{4,5},{5,4},{6,7},{7,6},{8,9},{9,8},{10,11... | collective-permute-start | bytes 776 | tf_op jit(solution)/shard_map/ppermute | solution.py:451
  8.5 1.0 copy-start.1
  9.6 11.5 %copy-start.2 = (bf16[1,16,128,128]{3,2,1,0:T(8,128)(2,1)S(1)}, bf16[1,16,128,128]{3,2,1,0:T(8,128)(2,1)}, u32[]{:S(2)}) copy-start(bf16[1,16,128,128]{3,2,1,0:T(8,128)(2,1)} %param.8) | copy-start | bytes 1572868
  12.4 14.0 %collective-permute-start.22 = (bf16[1040,128]{1,0:T(8,128)(2,1)S(1)}, bf16[1040,128]{1,0:T(8,128)(2,1)S(1)}, u32[]{:S(2)}, u32[]{:S(2)}) collective-permute-start(bf16[1040,128]{1,0:T(8,128)(2,1)S(1)} %get-tuple-element.79), channel_id=1, source_target_pairs={{0,8},{1,9},{2,10},{3,11},{4,12},{5,13},{6,14},{7,15},{8,0},{9,1},... | collective-permute-start | bytes 798728 | tf_op jit(solution)/shard_map/ppermute | solution.py:451
  14.8 12.6 %collective-permute-start.23 = (bf16[1040,128]{1,0:T(8,128)(2,1)S(1)}, bf16[1040,128]{1,0:T(8,128)(2,1)S(1)}, u32[]{:S(2)}, u32[]{:S(2)}) collective-permute-start(bf16[1040,128]{1,0:T(8,128)(2,1)S(1)} %get-tuple-element.80), channel_id=1, source_target_pairs={{0,16},{1,17},{2,18},{3,19},{4,20},{5,21},{6,22},{7,23},{8,24},{9,... | collective-permute-start | bytes 798728 | tf_op jit(solution)/shard_map/ppermute | solution.py:451
  17.1 17.5 %collective-permute-start.24 = (bf16[1040,128]{1,0:T(8,128)(2,1)S(1)}, bf16[1040,128]{1,0:T(8,128)(2,1)S(1)}, u32[]{:S(2)}, u32[]{:S(2)}) collective-permute-start(bf16[1040,128]{1,0:T(8,128)(2,1)S(1)} %get-tuple-element.81), channel_id=1, source_target_pairs={{0,24},{1,25},{2,26},{3,27},{4,28},{5,29},{6,30},{7,31},{8,16},{9,... | collective-permute-start | bytes 798728 | tf_op jit(solution)/shard_map/ppermute | solution.py:451
  19.8 24.1 %collective-permute-start.3 = (bf16[1040,128]{1,0:T(8,128)(2,1)S(1)}, bf16[1040,128]{1,0:T(8,128)(2,1)S(1)}, u32[]{:S(2)}, u32[]{:S(2)}) collective-permute-start(bf16[1040,128]{1,0:T(8,128)(2,1)S(1)} %get-tuple-element.53), channel_id=1, source_target_pairs={{0,2},{1,3},{2,0},{3,1},{4,6},{5,7},{6,4},{7,5},{8,10},{9,11},{10,... | collective-permute-start | bytes 798728 | tf_op jit(solution)/shard_map/ppermute | solution.py:451
  24.2 73.1 %copy-start.3 = (bf16[3,3,3,128,128]{4,3,2,1,0:T(8,128)(2,1)S(1)}, bf16[3,3,3,128,128]{4,3,2,1,0:T(8,128)(2,1)}, u32[]{:S(2)}) copy-start(bf16[3,3,3,128,128]{4,3,2,1,0:T(8,128)(2,1)} %first_ref.1) | copy-start | bytes 2654212
  24.2 73.1 %copy-start.4 = (bf16[3,3,3,128,128]{4,3,2,1,0:T(8,128)(2,1)S(1)}, bf16[3,3,3,128,128]{4,3,2,1,0:T(8,128)(2,1)}, u32[]{:S(2)}) copy-start(bf16[3,3,3,128,128]{4,3,2,1,0:T(8,128)(2,1)} %second_ref.1) | copy-start | bytes 2654212
  24.2 18.8 %collective-permute-start.9 = (bf16[1024,128]{1,0:T(8,128)(2,1)S(1)}, bf16[1024,128]{1,0:T(8,128)(2,1)S(1)}, u32[]{:S(2)}, u32[]{:S(2)}) collective-permute-start(bf16[1024,128]{1,0:T(8,128)(2,1)S(1)} %get-tuple-element.61), channel_id=1, source_target_pairs={{0,2},{1,3},{2,0},{3,1},{4,6},{5,7},{6,4},{7,5},{8,10},{9,11},{10,... | collective-permute-start | bytes 786440 | tf_op jit(solution)/shard_map/ppermute | solution.py:451
  26.4 17.9 %collective-permute-start.4 = (bf16[1040,128]{1,0:T(8,128)(2,1)S(1)}, bf16[1040,128]{1,0:T(8,128)(2,1)S(1)}, u32[]{:S(2)}, u32[]{:S(2)}) collective-permute-start(bf16[1040,128]{1,0:T(8,128)(2,1)S(1)} %get-tuple-element.54), channel_id=1, source_target_pairs={{0,4},{1,5},{2,6},{3,7},{4,0},{5,1},{6,2},{7,3},{8,12},{9,13},{10,... | collective-permute-start | bytes 798728 | tf_op jit(solution)/shard_map/ppermute | solution.py:451
  27.5 18.2 %collective-permute-start.5 = (bf16[1040,128]{1,0:T(8,128)(2,1)S(1)}, bf16[1040,128]{1,0:T(8,128)(2,1)S(1)}, u32[]{:S(2)}, u32[]{:S(2)}) collective-permute-start(bf16[1040,128]{1,0:T(8,128)(2,1)S(1)} %get-tuple-element.55), channel_id=1, source_target_pairs={{0,6},{1,7},{2,4},{3,5},{4,2},{5,3},{6,0},{7,1},{8,14},{9,15},{10,... | collective-permute-start | bytes 798728 | tf_op jit(solution)/shard_map/ppermute | solution.py:451
  36.8 3.9 %collective-permute-start.25 = (bf16[512,128]{1,0:T(8,128)(2,1)S(1)}, bf16[512,128]{1,0:T(8,128)(2,1)S(1)}, u32[]{:S(2)}, u32[]{:S(2)}) collective-permute-start(bf16[512,128]{1,0:T(8,128)(2,1)S(1)} %get-tuple-element.83), channel_id=1, source_target_pairs={{0,2},{1,3},{2,0},{3,1},{4,6},{5,7},{6,4},{7,5},{8,10},{9,11},{10,... | collective-permute-start | bytes 393224 | tf_op jit(solution)/shard_map/ppermute | solution.py:451
  40.7 9.4 %collective-permute-start.10 = (bf16[1024,128]{1,0:T(8,128)(2,1)S(1)}, bf16[1024,128]{1,0:T(8,128)(2,1)S(1)}, u32[]{:S(2)}, u32[]{:S(2)}) collective-permute-start(bf16[1024,128]{1,0:T(8,128)(2,1)S(1)} %get-tuple-element.62), channel_id=1, source_target_pairs={{0,4},{1,5},{2,6},{3,7},{4,0},{5,1},{6,2},{7,3},{8,12},{9,13},{10,... | collective-permute-start | bytes 786440 | tf_op jit(solution)/shard_map/ppermute | solution.py:451
  43.0 15.7 %collective-permute-start.11 = (bf16[1024,128]{1,0:T(8,128)(2,1)S(1)}, bf16[1024,128]{1,0:T(8,128)(2,1)S(1)}, u32[]{:S(2)}, u32[]{:S(2)}) collective-permute-start(bf16[1024,128]{1,0:T(8,128)(2,1)S(1)} %get-tuple-element.63), channel_id=1, source_target_pairs={{0,6},{1,7},{2,4},{3,5},{4,2},{5,3},{6,0},{7,1},{8,14},{9,15},{10,... | collective-permute-start | bytes 786440 | tf_op jit(solution)/shard_map/ppermute | solution.py:451
  43.9 16.7 %collective-permute-start.15 = (bf16[1024,128]{1,0:T(8,128)(2,1)S(1)}, bf16[1024,128]{1,0:T(8,128)(2,1)S(1)}, u32[]{:S(2)}, u32[]{:S(2)}) collective-permute-start(bf16[1024,128]{1,0:T(8,128)(2,1)S(1)} %get-tuple-element.70), channel_id=1, source_target_pairs={{0,2},{1,3},{2,0},{3,1},{4,6},{5,7},{6,4},{7,5},{8,10},{9,11},{10,... | collective-permute-start | bytes 786440 | tf_op jit(solution)/shard_map/ppermute | solution.py:451
  44.3 19.6 %collective-permute-start.16 = (bf16[1024,128]{1,0:T(8,128)(2,1)S(1)}, bf16[1024,128]{1,0:T(8,128)(2,1)S(1)}, u32[]{:S(2)}, u32[]{:S(2)}) collective-permute-start(bf16[1024,128]{1,0:T(8,128)(2,1)S(1)} %get-tuple-element.71), channel_id=1, source_target_pairs={{0,4},{1,5},{2,6},{3,7},{4,0},{5,1},{6,2},{7,3},{8,12},{9,13},{10,... | collective-permute-start | bytes 786440 | tf_op jit(solution)/shard_map/ppermute | solution.py:451
  45.7 24.0 %collective-permute-start.17 = (bf16[1024,128]{1,0:T(8,128)(2,1)S(1)}, bf16[1024,128]{1,0:T(8,128)(2,1)S(1)}, u32[]{:S(2)}, u32[]{:S(2)}) collective-permute-start(bf16[1024,128]{1,0:T(8,128)(2,1)S(1)} %get-tuple-element.72), channel_id=1, source_target_pairs={{0,6},{1,7},{2,4},{3,5},{4,2},{5,3},{6,0},{7,1},{8,14},{9,15},{10,... | collective-permute-start | bytes 786440 | tf_op jit(solution)/shard_map/ppermute | solution.py:451
  50.1 20.9 %collective-permute-start.6 = (bf16[512,128]{1,0:T(8,128)(2,1)S(1)}, bf16[512,128]{1,0:T(8,128)(2,1)S(1)}, u32[]{:S(2)}, u32[]{:S(2)}) collective-permute-start(bf16[512,128]{1,0:T(8,128)(2,1)S(1)} %get-tuple-element.57), channel_id=1, source_target_pairs={{0,8},{1,9},{2,10},{3,11},{4,12},{5,13},{6,14},{7,15},{8,0},{9,1},... | collective-permute-start | bytes 393224 | tf_op jit(solution)/shard_map/ppermute | solution.py:451
  58.7 13.2 %collective-permute-start.7 = (bf16[512,128]{1,0:T(8,128)(2,1)S(1)}, bf16[512,128]{1,0:T(8,128)(2,1)S(1)}, u32[]{:S(2)}, u32[]{:S(2)}) collective-permute-start(bf16[512,128]{1,0:T(8,128)(2,1)S(1)} %get-tuple-element.58), channel_id=1, source_target_pairs={{0,16},{1,17},{2,18},{3,19},{4,20},{5,21},{6,22},{7,23},{8,24},{9,... | collective-permute-start | bytes 393224 | tf_op jit(solution)/shard_map/ppermute | solution.py:451
  60.6 13.5 %collective-permute-start.8 = (bf16[512,128]{1,0:T(8,128)(2,1)S(1)}, bf16[512,128]{1,0:T(8,128)(2,1)S(1)}, u32[]{:S(2)}, u32[]{:S(2)}) collective-permute-start(bf16[512,128]{1,0:T(8,128)(2,1)S(1)} %get-tuple-element.59), channel_id=1, source_target_pairs={{0,24},{1,25},{2,26},{3,27},{4,28},{5,29},{6,30},{7,31},{8,16},{9,... | collective-permute-start | bytes 393224 | tf_op jit(solution)/shard_map/ppermute | solution.py:451
  63.8 12.7 %collective-permute-start.12 = (bf16[512,128]{1,0:T(8,128)(2,1)S(1)}, bf16[512,128]{1,0:T(8,128)(2,1)S(1)}, u32[]{:S(2)}, u32[]{:S(2)}) collective-permute-start(bf16[512,128]{1,0:T(8,128)(2,1)S(1)} %get-tuple-element.66), channel_id=1, source_target_pairs={{0,8},{1,9},{2,10},{3,11},{4,12},{5,13},{6,14},{7,15},{8,0},{9,1},... | collective-permute-start | bytes 393224 | tf_op jit(solution)/shard_map/ppermute | solution.py:451
  69.6 11.5 %collective-permute-start.13 = (bf16[512,128]{1,0:T(8,128)(2,1)S(1)}, bf16[512,128]{1,0:T(8,128)(2,1)S(1)}, u32[]{:S(2)}, u32[]{:S(2)}) collective-permute-start(bf16[512,128]{1,0:T(8,128)(2,1)S(1)} %get-tuple-element.67), channel_id=1, source_target_pairs={{0,16},{1,17},{2,18},{3,19},{4,20},{5,21},{6,22},{7,23},{8,24},{9,... | collective-permute-start | bytes 393224 | tf_op jit(solution)/shard_map/ppermute | solution.py:451
  71.0 10.1 %collective-permute-start.14 = (bf16[512,128]{1,0:T(8,128)(2,1)S(1)}, bf16[512,128]{1,0:T(8,128)(2,1)S(1)}, u32[]{:S(2)}, u32[]{:S(2)}) collective-permute-start(bf16[512,128]{1,0:T(8,128)(2,1)S(1)} %get-tuple-element.68), channel_id=1, source_target_pairs={{0,24},{1,25},{2,26},{3,27},{4,28},{5,29},{6,30},{7,31},{8,16},{9,... | collective-permute-start | bytes 393224 | tf_op jit(solution)/shard_map/ppermute | solution.py:451
  71.9 11.3 %collective-permute-start.26 = (bf16[512,128]{1,0:T(8,128)(2,1)S(1)}, bf16[512,128]{1,0:T(8,128)(2,1)S(1)}, u32[]{:S(2)}, u32[]{:S(2)}) collective-permute-start(bf16[512,128]{1,0:T(8,128)(2,1)S(1)} %get-tuple-element.84), channel_id=1, source_target_pairs={{0,4},{1,5},{2,6},{3,7},{4,0},{5,1},{6,2},{7,3},{8,12},{9,13},{10,... | collective-permute-start | bytes 393224 | tf_op jit(solution)/shard_map/ppermute | solution.py:451
  74.1 21.2 %collective-permute-start.27 = (bf16[512,128]{1,0:T(8,128)(2,1)S(1)}, bf16[512,128]{1,0:T(8,128)(2,1)S(1)}, u32[]{:S(2)}, u32[]{:S(2)}) collective-permute-start(bf16[512,128]{1,0:T(8,128)(2,1)S(1)} %get-tuple-element.85), channel_id=1, source_target_pairs={{0,6},{1,7},{2,4},{3,5},{4,2},{5,3},{6,0},{7,1},{8,14},{9,15},{10,... | collective-permute-start | bytes 393224 | tf_op jit(solution)/shard_map/ppermute | solution.py:451
  76.5 21.7 %collective-permute-start.18 = (bf16[512,128]{1,0:T(8,128)(2,1)S(1)}, bf16[512,128]{1,0:T(8,128)(2,1)S(1)}, u32[]{:S(2)}, u32[]{:S(2)}) collective-permute-start(bf16[512,128]{1,0:T(8,128)(2,1)S(1)} %get-tuple-element.74), channel_id=1, source_target_pairs={{0,8},{1,9},{2,10},{3,11},{4,12},{5,13},{6,14},{7,15},{8,0},{9,1},... | collective-permute-start | bytes 393224 | tf_op jit(solution)/shard_map/ppermute | solution.py:451
  81.1 17.2 %collective-permute-start.19 = (bf16[512,128]{1,0:T(8,128)(2,1)S(1)}, bf16[512,128]{1,0:T(8,128)(2,1)S(1)}, u32[]{:S(2)}, u32[]{:S(2)}) collective-permute-start(bf16[512,128]{1,0:T(8,128)(2,1)S(1)} %get-tuple-element.75), channel_id=1, source_target_pairs={{0,16},{1,17},{2,18},{3,19},{4,20},{5,21},{6,22},{7,23},{8,24},{9,... | collective-permute-start | bytes 393224 | tf_op jit(solution)/shard_map/ppermute | solution.py:451
  81.1 17.2 %collective-permute-start.20 = (bf16[512,128]{1,0:T(8,128)(2,1)S(1)}, bf16[512,128]{1,0:T(8,128)(2,1)S(1)}, u32[]{:S(2)}, u32[]{:S(2)}) collective-permute-start(bf16[512,128]{1,0:T(8,128)(2,1)S(1)} %get-tuple-element.76), channel_id=1, source_target_pairs={{0,24},{1,25},{2,26},{3,27},{4,28},{5,29},{6,30},{7,31},{8,16},{9,... | collective-permute-start | bytes 393224 | tf_op jit(solution)/shard_map/ppermute | solution.py:451
  83.2 15.1 %collective-permute-start.28 = (bf16[16,512]{1,0:T(8,128)(2,1)S(1)}, bf16[16,512]{1,0:T(8,128)(2,1)S(1)}, u32[]{:S(2)}, u32[]{:S(2)}) collective-permute-start(bf16[16,512]{1,0:T(8,128)(2,1)S(1)} %get-tuple-element.86), channel_id=1, source_target_pairs={{0,1},{1,2},{2,3},{4,5},{5,6},{6,7},{8,9},{9,10},{10,11},{12,13},{... | collective-permute-start | bytes 49160 | tf_op jit(solution)/shard_map/ppermute | solution.py:587
  95.4 8.1 %copy-start.5 = (f32[128]{0:T(128)S(1)}, f32[128]{0:T(128)}, u32[]{:S(2)}) copy-start(f32[128]{0:T(128)} %param.13) | copy-start | bytes 1540
  95.4 8.1 %copy-start.6 = (f32[128]{0:T(128)S(1)}, f32[128]{0:T(128)}, u32[]{:S(2)}) copy-start(f32[128]{0:T(128)} %param.15) | copy-start | bytes 1540
  95.4 5.1 %collective-permute-start.29 = (bf16[16,512]{1,0:T(8,128)(2,1)S(1)}, bf16[16,512]{1,0:T(8,128)(2,1)S(1)}, u32[]{:S(2)}, u32[]{:S(2)}) collective-permute-start(bf16[16,512]{1,0:T(8,128)(2,1)S(1)} %get-tuple-element.87), channel_id=1, source_target_pairs={{1,0},{2,1},{3,2},{5,4},{6,5},{7,6},{9,8},{10,9},{11,10},{13,12},{... | collective-permute-start | bytes 49160 | tf_op jit(solution)/shard_map/ppermute | solution.py:587
  100.8 6.3 %collective-permute-start.30 = (bf16[2,72,512]{2,1,0:T(8,128)(2,1)S(1)}, bf16[2,72,512]{2,1,0:T(8,128)(2,1)S(1)}, u32[]{:S(2)}, u32[]{:S(2)}) collective-permute-start(bf16[2,72,512]{2,1,0:T(8,128)(2,1)S(1)} %get-tuple-element.90), channel_id=1, source_target_pairs={{0,4},{4,8},{8,12},{12,16},{16,20},{20,24},{24,28},{1,5},{5,9},{9,... | collective-permute-start | bytes 442376 | tf_op jit(solution)/shard_map/ppermute | solution.py:587
  102.2 9.7 %collective-permute-start.31 = (bf16[2,72,512]{2,1,0:T(8,128)(2,1)S(1)}, bf16[2,72,512]{2,1,0:T(8,128)(2,1)S(1)}, u32[]{:S(2)}, u32[]{:S(2)}) collective-permute-start(bf16[2,72,512]{2,1,0:T(8,128)(2,1)S(1)} %get-tuple-element.91), channel_id=1, source_target_pairs={{4,0},{8,4},{12,8},{16,12},{20,16},{24,20},{28,24},{5,1},{9,5},{13... | collective-permute-start | bytes 442376 | tf_op jit(solution)/shard_map/ppermute | solution.py:587
